TPU v7x, 32 devices: a whole 2x2x4 slice. The times are simulated.
32 devices in a mesh: blk: 2 (over core), inner: 4 (over z), outer: 4 (over y, x).
Axes of the slice: x: 2, y: 2, z: 4, core: 2. Of those that a mesh axis runs over, the one named last changes fastest.
Arguments:
- hidden: bfloat16 [64, 256, 1152], P(('inner', 'outer'), 'blk'), may hold values from -6 to 6
- labels: int32 [64], P(('inner', 'outer')), may hold values from 0 to 1000
- steps_t: int32 [64], P(('inner', 'outer')), may hold values from 0 to 999
- live_slots: int32 [64], P(('inner', 'outer')), may hold values from 0 to 1, as said below
- label_table: bfloat16 [1001, 1152], replicated, may hold values from -6 to 6
- targets: bfloat16 [64, 256, 768], P(('inner', 'outer'), 'blk'), may hold values from -6 to 6
- cotangent: bfloat16 [64, 256, 1152], P(('inner', 'outer'), 'blk'), may hold values from -6 to 6
- weights: float32 [32014336], P(('inner', 'outer'))
- weight_momentum: float32 [32014336], P(('inner', 'outer')), may hold values from -320 to 320
- weight_average: float32 [32014336], P(('inner', 'outer'))
- biases: float32 [20992], P(('inner', 'outer')), may hold values from -1.25 to 1.25
- bias_momentum: float32 [20992], P(('inner', 'outer')), may hold values from -320 to 320
- bias_average: float32 [20992], P(('inner', 'outer')), may hold values from -1.25 to 1.25
Outputs:
- block_out: bfloat16 [64, 256, 1152], P(('inner', 'outer'), 'blk')
- grad_hidden: float32 [64, 256, 1152], P(('inner', 'outer'), 'blk')
- grad_cond: float32 [64, 1152], P(('inner', 'outer'))
- new_weight_momentum: float32 [32014336], P(('inner', 'outer'))
- new_weights: float32 [32014336], P(('inner', 'outer'))
- new_weights_low: bfloat16 [32014336], P(('inner', 'outer'))
- new_weight_average: float32 [32014336], P(('inner', 'outer'))
- new_bias_momentum: float32 [20992], P(('inner', 'outer'))
- new_biases: float32 [20992], P(('inner', 'outer'))
- new_biases_low: bfloat16 [20992], P(('inner', 'outer'))
- new_bias_average: float32 [20992], P(('inner', 'outer'))
Inputs may be any that keep to these rules, and one draw needn't show every extreme that they name: `live_slots`: of the 4 slots that one index of inner and outer holds at least one is live, and in the last such index all are.
All inputs are finite; a program needn't handle non-finite values.
Results may differ from a plain program's by a relative error of at most 0.02.
The roundings to bfloat16 on the way count: a program that leaves them out, or rounds other values in their place, can miss the bound.
Values may be sent and summed in bfloat16 or wider, within the bound.
No kernel may reach another device: no remote copies, remote signals or barrier semaphores. Data moves between devices by JAX's collectives and lax.ppermute only.
A program may use at most 384 MiB of HBM per device.

v0:
```python
import math

import jax
import jax.numpy as jnp
from jax import lax
from jax.sharding import PartitionSpec as P

E = 72
D = 1152
FF = 4608
PH = 2048
ZD = 768


LAMBDA_REPA = 0.5
MOMENTUM = 0.5
AVERAGE = 0.5
LR_COEF = 0.04
BIAS_FACTOR = 4.0
EPS_NORM = 1e-06


def passed_along(block, axis, distance):
    devices = range(lax.axis_size(axis))
    route = [((i - distance) % len(devices), i) for i in devices]
    return lax.ppermute(block, axis, route)


def mat_shapes():
    return [(D, 3 * D), (D, D), (D, FF), (FF, D), (D, 6 * D), (D, PH), (PH, PH), (PH, ZD)]


def bias_shapes():
    return [(D,), (D,), (D,), (FF,), (D,), (6 * D,), (PH,), (PH,), (ZD,)]


def split_shard(flat_vec, shapes, blocks):
    segments = []
    offset = 0
    for shape_now in shapes:
        rows_here = shape_now[0] // blocks
        length = rows_here * math.prod(shape_now[1:])
        segments.append(
            flat_vec[offset : offset + length].reshape((rows_here,) + tuple(shape_now[1:]))
        )
        offset += length
    return segments


def unpack_rows(flat_vec, shapes, blocks):
    line_grid = flat_vec.reshape(blocks, -1)
    segments = []
    offset = 0
    for shape_now in shapes:
        length = shape_now[0] // blocks * math.prod(shape_now[1:])
        segments.append(line_grid[:, offset : offset + length].reshape(shape_now))
        offset += length
    return segments


def outer_grid(segments, n_outer):
    grid_w = jnp.concatenate([segment.reshape(n_outer, -1) for segment in segments[:8]], axis=1)
    return (grid_w, segments[8].reshape(n_outer, -1))


def time_embed(steps_t):
    half_dim = D // 2
    frequency = jnp.exp(-math.log(10000.0) * jnp.arange(half_dim, dtype=jnp.float32) / half_dim)
    angles = steps_t.astype(jnp.float32)[:, None] * frequency[None, :]
    return jnp.concatenate([jnp.cos(angles), jnp.sin(angles)], axis=1)


def modulate(values, scale_v, shift_v):
    center = values - jnp.mean(values, axis=-1, keepdims=True)
    normed = center * lax.rsqrt(jnp.mean(center * center, axis=-1, keepdims=True) + EPS_NORM)
    return normed * (1.0 + scale_v[:, None, :]) + shift_v[:, None, :]


def gelu_tanh(values):
    return jax.nn.gelu(values, approximate=True)


def rms_unit(values):
    return values * lax.rsqrt(jnp.mean(values * values, axis=-1, keepdims=True) + EPS_NORM)


def matmul(left_arr, right_arr):
    return jnp.einsum("...i,ij->...j", left_arr, right_arr, preferred_element_type=jnp.float32)


def matmul_t(left_arr, right_arr):
    return jnp.einsum("...j,ij->...i", left_arr, right_arr, preferred_element_type=jnp.float32)


def outer_sum(left_arr, right_arr):
    return jnp.einsum("sni,snj->ij", left_arr, right_arr, preferred_element_type=jnp.float32)


def column_sum(tensor):
    return jnp.sum(tensor.astype(jnp.float32), axis=(0, 1))


def head_view(tensor):
    return tensor.reshape(tensor.shape[0], tensor.shape[1], -1, E)


def score_block(queries, kv_pair):
    raw_scores = jnp.einsum(
        "snhe,smhe->shnm",
        head_view(queries),
        head_view(kv_pair[..., :D]),
        preferred_element_type=jnp.float32,
    )
    return raw_scores * E ** (-0.5)


def weigh_values(probs_blk, kv_pair):
    mixed_out = jnp.einsum(
        "shnm,smhe->snhe",
        probs_blk.astype(jnp.bfloat16),
        head_view(kv_pair[..., D:]),
        preferred_element_type=jnp.float32,
    )
    return mixed_out.reshape(mixed_out.shape[0], mixed_out.shape[1], D)


def grad_block(queries, kv_pair, log_sum, grad_att):
    probs_blk = jnp.exp(score_block(queries, kv_pair) - log_sum[..., None])
    grad_prob = jnp.einsum(
        "snhe,smhe->shnm",
        head_view(grad_att),
        head_view(kv_pair[..., D:]),
        preferred_element_type=jnp.float32,
    )
    return (probs_blk, grad_prob)


def key_product(grad_scores, kv_pair):
    result = jnp.einsum(
        "shnm,smhe->snhe",
        grad_scores,
        head_view(kv_pair[..., :D]),
        preferred_element_type=jnp.float32,
    )
    return result.reshape(result.shape[0], result.shape[1], D)


def kv_grads(grad_scores, probs_blk, queries, grad_att):
    grad_keys = jnp.einsum(
        "shnm,snhe->smhe", grad_scores, head_view(queries), preferred_element_type=jnp.float32
    ) * E ** (-0.5)
    grad_vals = jnp.einsum(
        "shnm,snhe->smhe",
        probs_blk.astype(jnp.bfloat16),
        head_view(grad_att),
        preferred_element_type=jnp.float32,
    )
    rows_n = grad_keys.shape[1]
    return jnp.concatenate(
        [
            grad_keys.reshape(grad_keys.shape[0], rows_n, D),
            grad_vals.reshape(grad_vals.shape[0], rows_n, D),
        ],
        axis=-1,
    )


def body(
    hidden,
    labels,
    steps_t,
    live_slots,
    label_table,
    targets,
    cotangent,
    weights,
    weight_momentum,
    weight_average,
    biases,
    bias_momentum,
    bias_average,
):
    n_inner = lax.axis_size("inner")
    n_outer = lax.axis_size("outer")
    blocks = n_inner * n_outer
    slots = hidden.shape[0]
    local_tok = hidden.shape[1]
    p_qkv, p_proj, p_up, p_down, p_ada, p_one, p_two, p_three = split_shard(
        weights.astype(jnp.bfloat16), mat_shapes(), blocks
    )
    bias_low = biases.astype(jnp.bfloat16)
    w_qkv, w_proj, w_up, w_down, w_ada, w_one, w_two, w_three, bias_all = (
        lax.all_gather(p_qkv, ("inner", "outer"), axis=0, tiled=True),
        lax.all_gather(p_proj, ("inner", "outer"), axis=0, tiled=True),
        lax.all_gather(p_up, ("inner", "outer"), axis=0, tiled=True),
        lax.all_gather(p_down, ("inner", "outer"), axis=0, tiled=True),
        lax.all_gather(p_ada, ("inner", "outer"), axis=0, tiled=True),
        lax.all_gather(p_one, ("inner", "outer"), axis=0, tiled=True),
        lax.all_gather(p_two, ("inner", "outer"), axis=0, tiled=True),
        lax.all_gather(p_three, ("inner", "outer"), axis=0, tiled=True),
        lax.all_gather(bias_low, ("inner", "outer"), axis=0, tiled=True),
    )
    b_q, b_v, b_proj, b_up, b_down, b_ada, c_one, c_two, c_three = unpack_rows(
        bias_all.astype(jnp.float32), bias_shapes(), blocks
    )
    condition = label_table[labels].astype(jnp.float32) + time_embed(steps_t)
    cond_act, silu_cond = jax.vjp(jax.nn.silu, condition)
    cond_low = cond_act.astype(jnp.bfloat16)
    modulation = matmul(cond_low, w_ada) + b_ada
    shift_a, scale_a, gate_a, shift_m, scale_m, gate_m = [
        modulation[:, part_idx * D : (part_idx + 1) * D] for part_idx in range(6)
    ]
    hidden_f = hidden.astype(jnp.float32)
    mixed_a, pull_a = jax.vjp(modulate, hidden_f, scale_a, shift_a)
    mixed_a_low = mixed_a.astype(jnp.bfloat16)
    qkv_bias = jnp.concatenate([b_q, jnp.zeros((D,), jnp.float32), b_v])
    qkv_low = (matmul(mixed_a_low, w_qkv) + qkv_bias).astype(jnp.bfloat16)
    queries = qkv_low[..., :D]
    near_kv = qkv_low[..., D:]
    far_kv = passed_along(near_kv, "blk", 1)
    near_s = score_block(queries, near_kv)
    far_s = score_block(queries, far_kv)
    row_top = jnp.maximum(jnp.max(near_s, axis=-1), jnp.max(far_s, axis=-1))
    row_total = jnp.sum(jnp.exp(near_s - row_top[..., None]), axis=-1) + jnp.sum(
        jnp.exp(far_s - row_top[..., None]), axis=-1
    )
    log_sum = row_top + jnp.log(row_total)
    attended = weigh_values(jnp.exp(near_s - log_sum[..., None]), near_kv) + weigh_values(
        jnp.exp(far_s - log_sum[..., None]), far_kv
    )
    att_low = attended.astype(jnp.bfloat16)
    branch_a = matmul(att_low, w_proj) + b_proj
    residual = hidden_f + gate_a[:, None, :] * branch_a
    mixed_m, pull_m = jax.vjp(modulate, residual, scale_m, shift_m)
    mixed_m_low = mixed_m.astype(jnp.bfloat16)
    pre_act = matmul(mixed_m_low, w_up) + b_up
    activated, gelu_pull = jax.vjp(gelu_tanh, pre_act)
    act_low = activated.astype(jnp.bfloat16)
    branch_m = matmul(act_low, w_down) + b_down
    output = residual + gate_m[:, None, :] * branch_m
    out_low = output.astype(jnp.bfloat16)
    hid_one = matmul(out_low, w_one) + c_one
    act_one, silu_one = jax.vjp(jax.nn.silu, hid_one)
    one_low = act_one.astype(jnp.bfloat16)
    hid_two = matmul(one_low, w_two) + c_two
    act_two, silu_two = jax.vjp(jax.nn.silu, hid_two)
    two_low = act_two.astype(jnp.bfloat16)
    projection = matmul(two_low, w_three) + c_three
    live_f = live_slots.astype(jnp.float32)[:, None, None]
    unit_proj, unit_pull = jax.vjp(rms_unit, projection)
    grad_proj = unit_pull(-LAMBDA_REPA * live_f * rms_unit(targets.astype(jnp.float32)))[0].astype(
        jnp.bfloat16
    )
    grad_pthree = outer_sum(two_low, grad_proj)
    grad_cthree = column_sum(grad_proj)
    grad_htwo = silu_two(matmul_t(grad_proj, w_three))[0].astype(jnp.bfloat16)
    grad_ptwo = outer_sum(one_low, grad_htwo)
    grad_ctwo = column_sum(grad_htwo)
    grad_hone = silu_one(matmul_t(grad_htwo, w_two))[0].astype(jnp.bfloat16)
    grad_pone = outer_sum(out_low, grad_hone)
    grad_cone = column_sum(grad_hone)
    grad_output = cotangent.astype(jnp.float32) * live_f + matmul_t(grad_hone, w_one)
    grad_gate_m = jnp.sum(grad_output * branch_m, axis=1)
    grad_bm = (gate_m[:, None, :] * grad_output).astype(jnp.bfloat16)
    grad_wdown = outer_sum(act_low, grad_bm)
    grad_bdown = column_sum(grad_bm)
    grad_pre = gelu_pull(matmul_t(grad_bm, w_down))[0].astype(jnp.bfloat16)
    grad_wup = outer_sum(mixed_m_low, grad_pre)
    grad_bup = column_sum(grad_pre)
    grad_res_m, grad_scale_m, grad_shift_m = pull_m(matmul_t(grad_pre, w_up))
    grad_residual = grad_output + grad_res_m
    grad_gate_a = jnp.sum(grad_residual * branch_a, axis=1)
    grad_ba = (gate_a[:, None, :] * grad_residual).astype(jnp.bfloat16)
    grad_wproj = outer_sum(att_low, grad_ba)
    grad_bproj = column_sum(grad_ba)
    grad_att = matmul_t(grad_ba, w_proj).astype(jnp.bfloat16)
    near_p, near_dp = grad_block(queries, near_kv, log_sum, grad_att)
    far_p, far_dp = grad_block(queries, far_kv, log_sum, grad_att)
    row_delta = jnp.sum(near_p * near_dp, axis=-1) + jnp.sum(far_p * far_dp, axis=-1)
    near_ds = (near_p * (near_dp - row_delta[..., None])).astype(jnp.bfloat16)
    far_ds = (far_p * (far_dp - row_delta[..., None])).astype(jnp.bfloat16)
    grad_query = (key_product(near_ds, near_kv) + key_product(far_ds, far_kv)) * E ** (-0.5)
    far_dkv = kv_grads(far_ds, far_p, queries, grad_att)
    home_dkv = passed_along(far_dkv.astype(jnp.bfloat16), "blk", -1).astype(far_dkv.dtype)
    near_dkv = kv_grads(near_ds, near_p, queries, grad_att)
    grad_qkv = jnp.concatenate([grad_query, near_dkv + home_dkv], axis=-1).astype(jnp.bfloat16)
    grad_wqkv = outer_sum(mixed_a_low, grad_qkv)
    qkv_sums = column_sum(grad_qkv)
    grad_hid_a, grad_scale_a, grad_shift_a = pull_a(matmul_t(grad_qkv, w_qkv))
    grad_input = grad_residual + grad_hid_a
    grad_mod_part = jnp.concatenate(
        [grad_shift_a, grad_scale_a, grad_gate_a, grad_shift_m, grad_scale_m, grad_gate_m], axis=1
    )
    grad_mod = lax.psum(grad_mod_part.astype(jnp.bfloat16), "blk")
    grad_wada = 0.5 * jnp.einsum(
        "si,sj->ij", cond_low, grad_mod, preferred_element_type=jnp.float32
    )
    grad_bada = 0.5 * jnp.sum(grad_mod.astype(jnp.float32), axis=0)
    grad_cond = silu_cond(matmul_t(grad_mod, w_ada))[0]
    bias_terms = (
        qkv_sums[:D],
        qkv_sums[2 * D :],
        grad_bproj,
        grad_bup,
        grad_bdown,
        grad_bada,
        grad_cone,
        grad_ctwo,
        grad_cthree,
    )
    bias_grid = jnp.concatenate(
        [segment.reshape(blocks, -1) for segment in bias_terms], axis=1
    ).reshape(-1)
    inner_parts = (
        lax.psum_scatter(
            grad_wqkv.astype(jnp.bfloat16), "inner", scatter_dimension=0, tiled=True
        ).astype(jnp.float32),
        lax.psum_scatter(
            grad_wproj.astype(jnp.bfloat16), "inner", scatter_dimension=0, tiled=True
        ).astype(jnp.float32),
        lax.psum_scatter(
            grad_wup.astype(jnp.bfloat16), "inner", scatter_dimension=0, tiled=True
        ).astype(jnp.float32),
        lax.psum_scatter(
            grad_wdown.astype(jnp.bfloat16), "inner", scatter_dimension=0, tiled=True
        ).astype(jnp.float32),
        lax.psum_scatter(
            grad_wada.astype(jnp.bfloat16), "inner", scatter_dimension=0, tiled=True
        ).astype(jnp.float32),
        lax.psum_scatter(
            grad_pone.astype(jnp.bfloat16), "inner", scatter_dimension=0, tiled=True
        ).astype(jnp.float32),
        lax.psum_scatter(
            grad_ptwo.astype(jnp.bfloat16), "inner", scatter_dimension=0, tiled=True
        ).astype(jnp.float32),
        lax.psum_scatter(
            grad_pthree.astype(jnp.bfloat16), "inner", scatter_dimension=0, tiled=True
        ).astype(jnp.float32),
        lax.psum_scatter(
            bias_grid.astype(jnp.bfloat16), "inner", scatter_dimension=0, tiled=True
        ).astype(jnp.float32),
    )
    grid_w, grid_b = outer_grid(inner_parts, n_outer)
    summed_w, summed_b = (
        lax.psum(grid_w.astype(jnp.bfloat16), ("blk", "outer")).astype(jnp.float32),
        lax.psum(grid_b.astype(jnp.bfloat16), ("blk", "outer")).astype(jnp.float32),
    )
    own_index = lax.axis_index("outer")
    grad_w_flat = lax.dynamic_index_in_dim(summed_w, own_index, 0, keepdims=False)
    grad_b_flat = lax.dynamic_index_in_dim(summed_b, own_index, 0, keepdims=False)
    images_all = slots * blocks
    tokens_img = local_tok * lax.axis_size("blk")
    rate_w = LR_COEF / math.sqrt(images_all * tokens_img)
    rate_b = BIAS_FACTOR * rate_w
    mom_w = MOMENTUM * weight_momentum + grad_w_flat
    new_w = weights - rate_w * (grad_w_flat + MOMENTUM * mom_w)
    avg_w = AVERAGE * weight_average + (1.0 - AVERAGE) * new_w
    mom_b = MOMENTUM * bias_momentum + grad_b_flat
    new_b = biases - rate_b * (grad_b_flat + MOMENTUM * mom_b)
    avg_b = AVERAGE * bias_average + (1.0 - AVERAGE) * new_b
    return (
        out_low,
        grad_input,
        grad_cond,
        mom_w,
        new_w,
        new_w.astype(jnp.bfloat16),
        avg_w,
        mom_b,
        new_b,
        new_b.astype(jnp.bfloat16),
        avg_b,
    )


def solution(mesh):
    in_specs = (
        P(("inner", "outer"), "blk", None),
        P(("inner", "outer")),
        P(("inner", "outer")),
        P(("inner", "outer")),
        P(),
        P(("inner", "outer"), "blk", None),
        P(("inner", "outer"), "blk", None),
        P(("inner", "outer")),
        P(("inner", "outer")),
        P(("inner", "outer")),
        P(("inner", "outer")),
        P(("inner", "outer")),
        P(("inner", "outer")),
    )
    out_specs = (
        P(("inner", "outer"), "blk", None),
        P(("inner", "outer"), "blk", None),
        P(("inner", "outer"), None),
        P(("inner", "outer")),
        P(("inner", "outer")),
        P(("inner", "outer")),
        P(("inner", "outer")),
        P(("inner", "outer")),
        P(("inner", "outer")),
        P(("inner", "outer")),
        P(("inner", "outer")),
    )
    return jax.shard_map(body, mesh=mesh, in_specs=in_specs, out_specs=out_specs, check_vma=False)
```

profile of v0, /device:TPU:0, one launch (start us, length us, event | category | flops | bytes accessed | tf_op | source)
XLA Modules:
  0.0 2376.5 jit_solution(2534763386764745877)
XLA Ops:
  35.4 80.9 %all-reduce = bf16[20992]{0:T(1024)(128)(2,1)} all-reduce(bf16[20992]{0:T(1024)(128)(2,1)S(1)} %dynamic-update-slice), channel_id=1, replica_groups=mesh['blk'=2,'inner'=4,'outer'=4] {'inner','outer'}, use_global_device_ids=true, to_apply=%add | all-reduce | flops 20992 | bytes 83968
  125.7 79.5 %all-gather.9.cloned.1.call-done = bf16[1152,6912]{1,0:T(8,128)(2,1)} async-done(((bf16[72,6912]{1,0:T(8,128)(2,1)}), bf16[1152,6912]{1,0:T(8,128)(2,1)}) %all-gather.9.cloned.1.call-update) | async-done | bytes 15925264 | tf_op jit(solution)/shard_map/all_gather | solution.py:197
  213.0 102.7 %all-gather.11.cloned.1.call-done = bf16[1152,3456]{1,0:T(8,128)(2,1)} async-done(((bf16[72,3456]{1,0:T(8,128)(2,1)}), bf16[1152,3456]{1,0:T(8,128)(2,1)}) %all-gather.11.cloned.1.call-update) | async-done | bytes 7962640 | tf_op jit(solution)/shard_map/all_gather | solution.py:193
  366.1 14.8 all-gather.13.cloned.1.call-done
  388.3 127.6 %all-gather.15.cloned.1.call-done = bf16[1152,4608]{1,0:T(8,128)(2,1)} async-done(((bf16[72,4608]{1,0:T(8,128)(2,1)}), bf16[1152,4608]{1,0:T(8,128)(2,1)}) %all-gather.15.cloned.1.call-update) | async-done | bytes 10616848 | tf_op jit(solution)/shard_map/all_gather | solution.py:195
  516.0 12.2 fusion.9
  528.1 122.7 %all-gather.17.cloned.1.call-done = bf16[4608,1152]{1,0:T(8,128)(2,1)} async-done(((bf16[288,1152]{1,0:T(8,128)(2,1)}), bf16[4608,1152]{1,0:T(8,128)(2,1)}) %all-gather.17.cloned.1.call-update) | async-done | bytes 10616848 | tf_op jit(solution)/shard_map/all_gather | solution.py:196
  650.9 14.5 add_convert_fusion.1
  665.3 66.8 %all-gather.19.cloned.1.call-done = bf16[1152,2048]{1,0:T(8,128)(2,1)} async-done(((bf16[72,2048]{1,0:T(8,128)(2,1)}), bf16[1152,2048]{1,0:T(8,128)(2,1)}) %all-gather.19.cloned.1.call-update) | async-done | bytes 4718608 | tf_op jit(solution)/shard_map/all_gather | solution.py:198
  738.9 107.6 %all-gather.21.cloned.1.call-done = bf16[2048,2048]{1,0:T(8,128)(2,1)} async-done(((bf16[128,2048]{1,0:T(8,128)(2,1)}), bf16[2048,2048]{1,0:T(8,128)(2,1)}) %all-gather.21.cloned.1.call-update) | async-done | bytes 8388624 | tf_op jit(solution)/shard_map/all_gather | solution.py:199
  857.7 57.9 %all-gather.23.cloned.1.call-done = bf16[2048,768]{1,0:T(8,128)(2,1)} async-done(((bf16[128,768]{1,0:T(8,128)(2,1)}), bf16[2048,768]{1,0:T(8,128)(2,1)}) %all-gather.23.cloned.1.call-update) | async-done | bytes 3145744 | tf_op jit(solution)/shard_map/all_gather | solution.py:200
  941.8 17.3 fusion.114
  959.1 12.2 multiply_reduce_fusion.7
  1085.0 13.1 fusion.1
  1132.1 48.8 %reduce-scatter.19.cloned.1.call-done = bf16[288,2048]{1,0:T(8,128)(2,1)} async-done(((bf16[1152,2048]{1,0:T(8,128)(2,1)}), bf16[288,2048]{1,0:T(8,128)(2,1)}) %reduce-scatter.19.cloned.1.call-update) | async-done | bytes 1179664 | tf_op jit(solution)/shard_map/reduce_scatter | solution.py:330
  1184.1 144.1 %reduce-scatter.21.cloned.1.call-done = bf16[512,2048]{1,0:T(8,128)(2,1)} async-done(((bf16[2048,2048]{1,0:T(8,128)(2,1)}), bf16[512,2048]{1,0:T(8,128)(2,1)}) %reduce-scatter.21.cloned.1.call-update) | async-done | bytes 2097168 | tf_op jit(solution)/shard_map/reduce_scatter | solution.py:333
  1331.3 138.6 %reduce-scatter.9.cloned.1.call-done = bf16[288,3456]{1,0:T(8,128)(2,1)} async-done(((bf16[1152,3456]{1,0:T(8,128)(2,1)}), bf16[288,3456]{1,0:T(8,128)(2,1)}) %reduce-scatter.9.cloned.1.call-update) | async-done | bytes 1990672 | tf_op jit(solution)/shard_map/reduce_scatter | solution.py:315
  1477.8 175.2 %reduce-scatter.13.cloned.1.call-done = bf16[288,4608]{1,0:T(8,128)(2,1)} async-done(((bf16[1152,4608]{1,0:T(8,128)(2,1)}), bf16[288,4608]{1,0:T(8,128)(2,1)}) %reduce-scatter.13.cloned.1.call-update) | async-done | bytes 2654224 | tf_op jit(solution)/shard_map/reduce_scatter | solution.py:321
  1662.8 173.6 %reduce-scatter.15.cloned.1.call-done = bf16[1152,1152]{1,0:T(8,128)(2,1)} async-done(((bf16[4608,1152]{1,0:T(8,128)(2,1)}), bf16[1152,1152]{1,0:T(8,128)(2,1)}) %reduce-scatter.15.cloned.1.call-update) | async-done | bytes 2654224 | tf_op jit(solution)/shard_map/reduce_scatter | solution.py:324
  1845.2 262.1 %reduce-scatter.17.cloned.1.call-done = bf16[288,6912]{1,0:T(8,128)(2,1)} async-done(((bf16[1152,6912]{1,0:T(8,128)(2,1)}), bf16[288,6912]{1,0:T(8,128)(2,1)}) %reduce-scatter.17.cloned.1.call-update) | async-done | bytes 3981328 | tf_op jit(solution)/shard_map/reduce_scatter | solution.py:327
  2129.0 18.8 all-reduce.1
  2147.9 29.0 %psum.23 = bf16[4,1312]{1,0:T(4,128)(2,1)S(1)} all-reduce(bf16[4,1312]{1,0:T(4,128)(2,1)S(1)} %convert_element_type.227), channel_id=1, replica_groups=mesh['blk'=2,'inner'=4,'outer'=4] {'blk','outer'}, use_global_device_ids=true, to_apply=%region_42.43 | all-reduce | flops 5248 | bytes 20992 | tf_op jit(solution)/shard_map/psum | solution.py:346
  2188.8 146.3 %all-reduce.4.cloned.1.call-done = bf16[4,2000896]{1,0:T(4,128)(2,1)} async-done(((bf16[4,2000896]{1,0:T(4,128)(2,1)}), bf16[4,2000896]{1,0:T(4,128)(2,1)}) %all-reduce.4.cloned.1.call-update) | async-done | bytes 16007184 | tf_op jit(solution)/shard_map/psum | solution.py:345
  2344.8 20.1 add_multiply_fusion
  (379 shorter events, 373.8 us)
Async XLA Ops:
  7.2 116.3 %copy-start = (bf16[1001,1152]{1,0:T(8,128)(2,1)S(1)}, bf16[1001,1152]{1,0:T(8,128)(2,1)}, u32[]{:S(2)}) copy-start(bf16[1001,1152]{1,0:T(8,128)(2,1)} %param.17) | copy-start | bytes 6918916
  7.2 198.0 %all-gather.9.cloned.1.call-start = ((), (), s32[]{:S(2)}) async-start(), calls=%async_computation.8 | async-start | bytes 16920576 | tf_op jit(solution)/shard_map/all_gather | solution.py:197
  16.9 298.7 %all-gather.11.cloned.1.call-start = ((), (), s32[]{:S(2)}) async-start(), calls=%async_computation.9 | async-start | bytes 8460288 | tf_op jit(solution)/shard_map/all_gather | solution.py:193
  18.4 362.5 %all-gather.13.cloned.1.call-start = ((), (), s32[]{:S(2)}) async-start(), calls=%async_computation.10 | async-start | bytes 2820096 | tf_op jit(solution)/shard_map/all_gather | solution.py:194
  19.3 496.6 %all-gather.15.cloned.1.call-start = ((), (), s32[]{:S(2)}) async-start(), calls=%async_computation.11 | async-start | bytes 11280384 | tf_op jit(solution)/shard_map/all_gather | solution.py:195
  24.2 626.7 %all-gather.17.cloned.1.call-start = ((), (), s32[]{:S(2)}) async-start(), calls=%async_computation.12 | async-start | bytes 11280384 | tf_op jit(solution)/shard_map/all_gather | solution.py:196
  25.9 706.3 %all-gather.19.cloned.1.call-start = ((), (), s32[]{:S(2)}) async-start(), calls=%async_computation.13 | async-start | bytes 5013504 | tf_op jit(solution)/shard_map/all_gather | solution.py:198
  29.6 816.8 %all-gather.21.cloned.1.call-start = ((), (), s32[]{:S(2)}) async-start(), calls=%async_computation.14 | async-start | bytes 8912896 | tf_op jit(solution)/shard_map/all_gather | solution.py:199
  33.7 881.9 %all-gather.23.cloned.1.call-start = ((), (), s32[]{:S(2)}) async-start(), calls=%async_computation.15 | async-start | bytes 3342336 | tf_op jit(solution)/shard_map/all_gather | solution.py:200
  125.0 190.7 %copy-start.48 = (f32[4,128]{1,0:T(4,128)}, f32[4,128]{1,0:T(4,128)S(1)}, u32[]{:S(2)}) copy-start(f32[4,128]{1,0:T(4,128)S(1)} %broadcast_multiply_fusion.1) | copy-start | bytes 6148
  125.5 190.2 %copy-start.55 = (f32[4,128]{1,0:T(4,128)}, f32[4,128]{1,0:T(4,128)S(1)}, u32[]{:S(2)}) copy-start(f32[4,128]{1,0:T(4,128)S(1)} %fusion.94) | copy-start | bytes 6148
  213.0 111.5 %copy-start.41 = (f32[4,1152]{1,0:T(4,128)}, f32[4,1152]{1,0:T(4,128)S(1)}, u32[]{:S(2)}) copy-start(f32[4,1152]{1,0:T(4,128)S(1)} %get-tuple-element.51) | copy-start | bytes 55300
  213.0 303.0 %copy-start.59 = (f32[4,1152]{1,0:T(4,128)}, f32[4,1152]{1,0:T(4,128)S(1)}, u32[]{:S(2)}) copy-start(f32[4,1152]{1,0:T(4,128)S(1)} %get-tuple-element.48) | copy-start | bytes 55300
  327.1 17.2 collective-permute-start
  328.0 799.2 %reduce-scatter.11.cloned.1.call-start = ((), (), s32[]{:S(2)}) async-start(), calls=%async_computation.17 | async-start | bytes 3317760 | tf_op jit(solution)/shard_map/reduce_scatter | solution.py:318
  978.7 150.7 %reduce-scatter.23.cloned.1.call-start = ((), (), s32[]{:S(2)}) async-start(), calls=%async_computation.23 | async-start | bytes 3932160 | tf_op jit(solution)/shard_map/reduce_scatter | solution.py:336
  985.7 195.2 %reduce-scatter.19.cloned.1.call-start = ((), (), s32[]{:S(2)}) async-start(), calls=%async_computation.21 | async-start | bytes 5898240 | tf_op jit(solution)/shard_map/reduce_scatter | solution.py:330
  993.4 334.8 %reduce-scatter.21.cloned.1.call-start = ((), (), s32[]{:S(2)}) async-start(), calls=%async_computation.22 | async-start | bytes 10485760 | tf_op jit(solution)/shard_map/reduce_scatter | solution.py:333
  1004.3 465.6 %reduce-scatter.9.cloned.1.call-start = ((), (), s32[]{:S(2)}) async-start(), calls=%async_computation.16 | async-start | bytes 9953280 | tf_op jit(solution)/shard_map/reduce_scatter | solution.py:315
  1038.4 22.4 collective-permute-start.1
  1073.2 579.8 %reduce-scatter.13.cloned.1.call-start = ((), (), s32[]{:S(2)}) async-start(), calls=%async_computation.18 | async-start | bytes 13271040 | tf_op jit(solution)/shard_map/reduce_scatter | solution.py:321
  1085.0 751.4 %reduce-scatter.15.cloned.1.call-start = ((), (), s32[]{:S(2)}) async-start(), calls=%async_computation.19 | async-start | bytes 13271040 | tf_op jit(solution)/shard_map/reduce_scatter | solution.py:324
  1098.2 1009.1 %reduce-scatter.17.cloned.1.call-start = ((), (), s32[]{:S(2)}) async-start(), calls=%async_computation.20 | async-start | bytes 19906560 | tf_op jit(solution)/shard_map/reduce_scatter | solution.py:327
  1127.1 1208.1 %all-reduce.4.cloned.1.call-start = ((), (), s32[]{:S(2)}) async-start(), calls=%async_computation.24 | async-start | bytes 32014336 | tf_op jit(solution)/shard_map/psum | solution.py:345
  (85 other events, 1323.8 us)
Sparse Core Ops, SparseCore 0:
  17.1 188.0 all-gather.8
  208.5 107.1 all-gather.10
  318.4 62.4 all-gather.12
  383.5 132.4 all-gather.14
  519.2 131.6 all-gather.16
  653.5 78.6 all-gather.18
  735.0 111.4 all-gather.20
  849.2 66.3 all-gather.22
  978.8 51.1 reduce-scatter.10
  1032.7 59.9 reduce-scatter.22
  1095.6 85.2 reduce-scatter.18
  1183.1 144.9 reduce-scatter.20
  1331.1 138.7 reduce-scatter.8
  1472.2 180.6 reduce-scatter.12
  1655.2 181.1 reduce-scatter.14
  1838.7 268.4 reduce-scatter.16
  2123.9 211.2 all-reduce.3
where the time goes:
time: 2390 us; the launch traced here: 2380 us
  waiting for transfers between devices  1770 us (74%)
  matrix products  247 us (10%)
  local copies, waits for them, and re-layouts  137 us (6%)
  blocking collectives  133 us (6%)
  other arithmetic  73.7 us (3%)
    reduce_scatter x1, waiting for transfers between devices, body(): lax.psum_scatter(grad_wada.astype(jnp.bfloat16), 'inner', scatter_dimensi...  262 us
    reduce_scatter x1, waiting for transfers between devices, body(): lax.psum_scatter(grad_wup.astype(jnp.bfloat16), 'inner', scatter_dimensio...  175 us
    reduce_scatter x1, waiting for transfers between devices, body(): lax.psum_scatter(grad_wdown.astype(jnp.bfloat16), 'inner', scatter_dimens...  174 us
    psum x1, waiting for transfers between devices, body(): lax.psum(grid_w.astype(jnp.bfloat16), ('blk', 'outer')).astype(jnp.float32)  146 us
    reduce_scatter x1, waiting for transfers between devices, body(): lax.psum_scatter(grad_ptwo.astype(jnp.bfloat16), 'inner', scatter_dimensi...  144 us
    reduce_scatter x1, waiting for transfers between devices, body(): lax.psum_scatter(grad_wqkv.astype(jnp.bfloat16), 'inner', scatter_dimensi...  139 us
    all_gather x1, waiting for transfers between devices, body(): lax.all_gather(p_up, ('inner', 'outer'), axis=0, tiled=True)  128 us
    all_gather x1, waiting for transfers between devices, body(): lax.all_gather(p_down, ('inner', 'outer'), axis=0, tiled=True)  123 us
  transfers between devices with their start and end apart: 19, of which 15 were waited for; matrix products, arithmetic and copies ran while one was open for 13% of the time, Pallas kernels for 0%

commit v1 on v0

v1 whole, which is shorter than its diff:
```python
import math

import jax
import jax.numpy as jnp
from jax import lax
from jax.experimental import pallas as pl
from jax.experimental.pallas import tpu as pltpu
from jax.sharding import PartitionSpec as P

E = 72
D = 1152
FF = 4608
PH = 2048
ZD = 768


LAMBDA_REPA = 0.5
MOMENTUM = 0.5
AVERAGE = 0.5
LR_COEF = 0.04
BIAS_FACTOR = 4.0
EPS_NORM = 1e-06
GROUP = ("inner", "outer")
EVERY = ("blk", "inner", "outer")
LOW = jnp.bfloat16


def passed_along(block, axis, distance):
    devices = range(lax.axis_size(axis))
    route = [((i - distance) % len(devices), i) for i in devices]
    return lax.ppermute(block, axis, route)


def mat_shapes():
    return [(D, 3 * D), (D, D), (D, FF), (FF, D), (D, 6 * D), (D, PH), (PH, PH), (PH, ZD)]


def bias_shapes():
    return [(D,), (D,), (D,), (FF,), (D,), (6 * D,), (PH,), (PH,), (ZD,)]


def split_shard(flat_vec, shapes, blocks):
    segments = []
    offset = 0
    for shape_now in shapes:
        rows_here = shape_now[0] // blocks
        length = rows_here * math.prod(shape_now[1:])
        segments.append(
            flat_vec[offset : offset + length].reshape((rows_here,) + tuple(shape_now[1:]))
        )
        offset += length
    return segments


def unpack_rows(line_grid, shapes):
    blocks = line_grid.shape[0]
    segments = []
    offset = 0
    for shape_now in shapes:
        length = shape_now[0] // blocks * math.prod(shape_now[1:])
        segments.append(line_grid[:, offset : offset + length].reshape(shape_now))
        offset += length
    return segments


def flat_id(core, z_at, outer_at):
    return (core * 4 + z_at) * 4 + outer_at


def route_z(pairs_core0):
    route = []
    for z_from, z_to in pairs_core0:
        for outer_at in range(4):
            route.append((flat_id(0, z_from, outer_at), flat_id(0, z_to, outer_at)))
            route.append((flat_id(1, 3 - z_from, outer_at), flat_id(1, 3 - z_to, outer_at)))
    return route


def flipped(route):
    return [(target, source) for source, target in route]


def route_xy(step_core0, step_core1):
    route = []
    for z_at in range(4):
        for outer_at in range(4):
            for core, step in ((0, step_core0), (1, step_core1)):
                route.append((flat_id(core, z_at, outer_at), flat_id(core, z_at, outer_at ^ step)))
    return route


STEP_X, STEP_Y = 1, 2
NEAR_FIRST = route_xy(STEP_X, STEP_Y)
NEAR_SECOND = route_xy(STEP_Y, STEP_X)
Z_PAIR = route_z([(0, 1), (1, 0)])
Z_STRAIGHT = route_z([(0, 2), (1, 3)])
Z_CROSS = route_z([(0, 3), (1, 2)])
SWAP = [(0, 1), (1, 0)]
UP = [(0, 1), (1, 2), (2, 3), (3, 0)]
DOWN = [(1, 0), (2, 1), (3, 2), (0, 3)]
ACROSS = [(0, 2), (2, 0), (1, 3), (3, 1)]
OUT_X = [(0, 1), (1, 0), (2, 3), (3, 2)]
OUT_Y = [(0, 2), (2, 0), (1, 3), (3, 1)]


def place_blocks(sources, table, count):
    counts = [source.shape[0] for source in sources]

    def kernel(table_ref, *refs):
        source_refs = refs[: len(counts)]
        out_ref, sems = refs[len(counts) :]
        copies = []
        for source_ref, length in zip(source_refs, counts):
            for at in range(length):
                number = len(copies)
                copies.append(
                    pltpu.make_async_copy(
                        source_ref.at[at], out_ref.at[table_ref[number]], sems.at[number]
                    )
                )
        for copy in copies:
            copy.start()
        for copy in copies:
            copy.wait()

    shape = (count,) + sources[0].shape[1:]
    return pl.pallas_call(
        kernel,
        out_shape=jax.ShapeDtypeStruct(shape, sources[0].dtype),
        grid_spec=pltpu.PrefetchScalarGridSpec(
            num_scalar_prefetch=1,
            grid=(1,),
            in_specs=[pl.BlockSpec(memory_space=pl.ANY)] * len(sources),
            out_specs=pl.BlockSpec(memory_space=pl.ANY),
            scratch_shapes=[pltpu.SemaphoreType.DMA((count,))],
        ),
        name="place_blocks",
    )(table, *sources)


def pick_blocks(source, table, counts):
    total = sum(counts)

    def kernel(table_ref, source_ref, *refs):
        out_refs = refs[: len(counts)]
        sems = refs[len(counts)]
        copies = []
        for out_ref, length in zip(out_refs, counts):
            for at in range(length):
                number = len(copies)
                copies.append(
                    pltpu.make_async_copy(
                        source_ref.at[table_ref[number]], out_ref.at[at], sems.at[number]
                    )
                )
        for copy in copies:
            copy.start()
        for copy in copies:
            copy.wait()

    return pl.pallas_call(
        kernel,
        out_shape=[
            jax.ShapeDtypeStruct((length,) + source.shape[1:], source.dtype) for length in counts
        ],
        grid_spec=pltpu.PrefetchScalarGridSpec(
            num_scalar_prefetch=1,
            grid=(1,),
            in_specs=[pl.BlockSpec(memory_space=pl.ANY)],
            out_specs=[pl.BlockSpec(memory_space=pl.ANY)] * len(counts),
            scratch_shapes=[pltpu.SemaphoreType.DMA((total,))],
        ),
        name="pick_blocks",
    )(table, source)


class Staged:
    def __init__(self):
        self.core = lax.axis_index("blk")
        self.z_at = lax.axis_index("inner")
        outer_at = lax.axis_index("outer")
        self.y_at = outer_at // 2
        self.x_at = outer_at % 2
        self.own_half = (self.z_at // 2) == self.core
        self.own_row = self.z_at * 4 + outer_at

    def z_pair(self, core):
        low_bit = self.z_at % 2
        return 2 * core + low_bit, 2 * core + 1 - low_bit

    def near_order(self, core, picks):
        found = []
        for far, near in picks:
            first = jnp.where(core == 0, self.x_at, self.y_at) ^ near
            second = jnp.where(core == 0, self.y_at, self.x_at) ^ far
            y_now = jnp.where(core == 0, second, first)
            x_now = jnp.where(core == 0, first, second)
            found.append(y_now * 2 + x_now)
        return found

    def gather_rows(self, own):
        pair = lax.ppermute(own, EVERY, Z_PAIR)
        straight = lax.ppermute(own, EVERY, Z_STRAIGHT)
        cross = lax.ppermute(own, EVERY, Z_CROSS)
        two = jnp.where(
            self.own_half, jnp.stack([own, pair]), jnp.stack([straight, cross])
        )
        four = jnp.concatenate([two, lax.ppermute(two, EVERY, NEAR_FIRST)])
        far_four = lax.ppermute(four, EVERY, NEAR_SECOND)
        mate_four = lax.ppermute(four, "blk", SWAP)
        mate_far = lax.ppermute(far_four, "blk", SWAP)
        table = []
        for core in (self.core, 1 - self.core):
            for outer_at in self.near_order(core, [(0, 0), (0, 1), (1, 0), (1, 1)]):
                for z_now in self.z_pair(core):
                    table.append(z_now * 4 + outer_at)
        full = place_blocks(
            [four, far_four, mate_four, mate_far], jnp.stack(table).astype(jnp.int32), 16
        )
        return full.reshape(-1, own.shape[-1])

    def share_left(self, left):
        half = left.shape[-1] // 2
        tokens = left.reshape(-1, left.shape[-1])
        keep = lax.dynamic_slice_in_dim(tokens, self.core * half, half, 1)
        give = lax.dynamic_slice_in_dim(tokens, (1 - self.core) * half, half, 1)
        return jnp.concatenate([keep, lax.ppermute(give, "blk", SWAP)])

    def weight_grad(self, left, right):
        tokens = right.reshape(-1, right.shape[-1])
        both = jnp.concatenate([tokens, lax.ppermute(tokens, "blk", SWAP)])
        grad = jnp.einsum("ni,nj->ij", left, both, preferred_element_type=jnp.float32)
        blocks = grad.astype(LOW).reshape(8, -1, grad.shape[-1])
        low_bit = self.z_at % 2
        table = []
        for outer_at in self.near_order(self.core, [(1, 1), (1, 0), (0, 1), (0, 0)]):
            for z_now in (low_bit, 1 - low_bit):
                table.append(z_now * 4 + outer_at)
        give, keep = pick_blocks(blocks, jnp.stack(table).astype(jnp.int32), (4, 4))
        came = lax.ppermute(give, EVERY, NEAR_SECOND)
        give = (keep[:2].astype(jnp.float32) + came[:2].astype(jnp.float32)).astype(LOW)
        keep = (keep[2:].astype(jnp.float32) + came[2:].astype(jnp.float32)).astype(LOW)
        came = lax.ppermute(give, EVERY, NEAR_FIRST)
        first = (keep[0].astype(jnp.float32) + came[0].astype(jnp.float32)).astype(LOW)
        second = (keep[1].astype(jnp.float32) + came[1].astype(jnp.float32)).astype(LOW)
        pair = lax.ppermute(second, EVERY, flipped(Z_PAIR))
        straight = lax.ppermute(first, EVERY, flipped(Z_STRAIGHT))
        cross = lax.ppermute(second, EVERY, flipped(Z_CROSS))
        summed = (
            (first.astype(jnp.float32) + pair.astype(jnp.float32))
            + (straight.astype(jnp.float32) + cross.astype(jnp.float32))
        ).astype(LOW)
        mate = lax.ppermute(summed, "blk", SWAP)
        return jnp.where(self.own_half, summed, mate).astype(jnp.float32)

    def gather_slots(self, own):
        four = jnp.stack(
            [own]
            + [lax.ppermute(own, "inner", route) for route in (UP, DOWN, ACROSS)]
        )
        eight = jnp.stack([four, lax.ppermute(four, "outer", OUT_X)])
        full = jnp.stack([eight, lax.ppermute(eight, "outer", OUT_Y)])
        return full.reshape((16,) + own.shape)

    def reduce_slots(self, parts):
        parts = parts.reshape((2, 2, 4) + parts.shape[1:])
        eight = parts[0] + lax.ppermute(parts[1], "outer", OUT_Y)
        four = eight[0] + lax.ppermute(eight[1], "outer", OUT_X)
        return (
            (four[0] + lax.ppermute(four[1], "inner", DOWN))
            + (lax.ppermute(four[2], "inner", UP) + lax.ppermute(four[3], "inner", ACROSS))
        )

    def slots_seen_from(self, gathered):
        found = []
        for slot in range(16):
            back = (slot // 4) * 4 + (0, 2, 1, 3)[slot % 4]
            found.append(gathered[slot, back])
        return jnp.stack(found)

    def rows_in_order(self, slots):
        table = []
        for z_now in range(4):
            away = (z_now - self.z_at) % 4
            z_slot = jnp.where(away == 0, 0, jnp.where(away == 3, 1, jnp.where(away == 1, 2, 3)))
            for outer_now in range(4):
                flip = jnp.bitwise_xor(outer_now, self.y_at * 2 + self.x_at)
                table.append(flip * 4 + z_slot)
        flat = jnp.take(slots.reshape(16, -1), jnp.stack(table), axis=0)
        return flat.reshape(slots.shape)


def outer_sum(left_arr, right_arr):
    return jnp.einsum("sni,snj->ij", left_arr, right_arr, preferred_element_type=jnp.float32)


class Direct:
    def __init__(self):
        self.core = lax.axis_index("blk")
        self.own_row = lax.axis_index("inner") * lax.axis_size("outer") + lax.axis_index("outer")

    def gather_rows(self, own):
        return lax.all_gather(own, GROUP, axis=0, tiled=True)

    def share_left(self, left):
        return left

    def weight_grad(self, left, right):
        grad = outer_sum(left, right).astype(LOW)
        part = lax.psum_scatter(grad, GROUP, scatter_dimension=0, tiled=True)
        return lax.psum(part, "blk").astype(jnp.float32)

    def gather_slots(self, own):
        return lax.all_gather(own, GROUP, axis=0)

    def reduce_slots(self, parts):
        return lax.psum_scatter(parts, GROUP, scatter_dimension=0, tiled=False)

    def slots_seen_from(self, gathered):
        return lax.dynamic_index_in_dim(gathered, self.own_row, 1, keepdims=False)

    def rows_in_order(self, slots):
        return slots


def time_embed(steps_t):
    half_dim = D // 2
    frequency = jnp.exp(-math.log(10000.0) * jnp.arange(half_dim, dtype=jnp.float32) / half_dim)
    angles = steps_t.astype(jnp.float32)[:, None] * frequency[None, :]
    return jnp.concatenate([jnp.cos(angles), jnp.sin(angles)], axis=1)


def modulate(values, scale_v, shift_v):
    center = values - jnp.mean(values, axis=-1, keepdims=True)
    normed = center * lax.rsqrt(jnp.mean(center * center, axis=-1, keepdims=True) + EPS_NORM)
    return normed * (1.0 + scale_v[:, None, :]) + shift_v[:, None, :]


def gelu_tanh(values):
    return jax.nn.gelu(values, approximate=True)


def rms_unit(values):
    return values * lax.rsqrt(jnp.mean(values * values, axis=-1, keepdims=True) + EPS_NORM)


def matmul(left_arr, right_arr):
    return jnp.einsum("...i,ij->...j", left_arr, right_arr, preferred_element_type=jnp.float32)


def matmul_t(left_arr, right_arr):
    return jnp.einsum("...j,ij->...i", left_arr, right_arr, preferred_element_type=jnp.float32)


def column_sum(tensor):
    return jnp.sum(tensor.astype(jnp.float32), axis=(0, 1))


def head_view(tensor):
    return tensor.reshape(tensor.shape[0], tensor.shape[1], -1, E)


def score_block(queries, kv_pair):
    raw_scores = jnp.einsum(
        "snhe,smhe->shnm",
        head_view(queries),
        head_view(kv_pair[..., :D]),
        preferred_element_type=jnp.float32,
    )
    return raw_scores * E ** (-0.5)


def weigh_values(probs_blk, kv_pair):
    mixed_out = jnp.einsum(
        "shnm,smhe->snhe",
        probs_blk.astype(jnp.bfloat16),
        head_view(kv_pair[..., D:]),
        preferred_element_type=jnp.float32,
    )
    return mixed_out.reshape(mixed_out.shape[0], mixed_out.shape[1], D)


def grad_block(queries, kv_pair, log_sum, grad_att):
    probs_blk = jnp.exp(score_block(queries, kv_pair) - log_sum[..., None])
    grad_prob = jnp.einsum(
        "snhe,smhe->shnm",
        head_view(grad_att),
        head_view(kv_pair[..., D:]),
        preferred_element_type=jnp.float32,
    )
    return (probs_blk, grad_prob)


def key_product(grad_scores, kv_pair):
    result = jnp.einsum(
        "shnm,smhe->snhe",
        grad_scores,
        head_view(kv_pair[..., :D]),
        preferred_element_type=jnp.float32,
    )
    return result.reshape(result.shape[0], result.shape[1], D)


def kv_grads(grad_scores, probs_blk, queries, grad_att):
    grad_keys = jnp.einsum(
        "shnm,snhe->smhe", grad_scores, head_view(queries), preferred_element_type=jnp.float32
    ) * E ** (-0.5)
    grad_vals = jnp.einsum(
        "shnm,snhe->smhe",
        probs_blk.astype(jnp.bfloat16),
        head_view(grad_att),
        preferred_element_type=jnp.float32,
    )
    rows_n = grad_keys.shape[1]
    return jnp.concatenate(
        [
            grad_keys.reshape(grad_keys.shape[0], rows_n, D),
            grad_vals.reshape(grad_vals.shape[0], rows_n, D),
        ],
        axis=-1,
    )


def body(
    hidden,
    labels,
    steps_t,
    live_slots,
    label_table,
    targets,
    cotangent,
    weights,
    weight_momentum,
    weight_average,
    biases,
    bias_momentum,
    bias_average,
):
    n_inner = lax.axis_size("inner")
    n_outer = lax.axis_size("outer")
    blocks = n_inner * n_outer
    slots = hidden.shape[0]
    local_tok = hidden.shape[1]
    moves = Staged() if (n_inner, n_outer) == (4, 4) else Direct()
    p_qkv, p_proj, p_up, p_down, p_ada, p_one, p_two, p_three = split_shard(
        weights.astype(LOW), mat_shapes(), blocks
    )
    bias_low = biases.astype(LOW)
    condition = label_table[labels].astype(jnp.float32) + time_embed(steps_t)
    cond_act, silu_cond = jax.vjp(jax.nn.silu, condition)
    cond_low = cond_act.astype(LOW)
    packed = jnp.concatenate([cond_low.reshape(-1), bias_low])
    packed_all = moves.gather_slots(packed)
    cond_all = packed_all[:, : slots * D].reshape(blocks * slots, D)
    bias_all = moves.rows_in_order(packed_all[:, slots * D :])
    b_q, b_v, b_proj, b_up, b_down, b_ada, c_one, c_two, c_three = unpack_rows(
        bias_all.astype(jnp.float32), bias_shapes()
    )
    rows_d = D // blocks
    cond_own = lax.dynamic_slice_in_dim(cond_all, moves.own_row * rows_d, rows_d, 1)
    half_ada = 3 * D
    ada_half = lax.dynamic_slice_in_dim(p_ada, moves.core * half_ada, half_ada, 1)
    mod_part = matmul(cond_own, ada_half).reshape(blocks, slots, half_ada)
    mod_half = moves.reduce_slots(mod_part)
    mod_mate = lax.ppermute(mod_half, "blk", SWAP)
    modulation = (
        jnp.concatenate(
            [
                jnp.where(moves.core == 0, mod_half, mod_mate),
                jnp.where(moves.core == 0, mod_mate, mod_half),
            ],
            axis=1,
        )
        + b_ada
    )
    w_qkv, w_proj, w_up, w_down, w_one, w_two, w_three = [
        moves.gather_rows(p) for p in (p_qkv, p_proj, p_up, p_down, p_one, p_two, p_three)
    ]
    shift_a, scale_a, gate_a, shift_m, scale_m, gate_m = [
        modulation[:, part_idx * D : (part_idx + 1) * D] for part_idx in range(6)
    ]
    hidden_f = hidden.astype(jnp.float32)
    mixed_a, pull_a = jax.vjp(modulate, hidden_f, scale_a, shift_a)
    mixed_a_low = mixed_a.astype(LOW)
    left_qkv = moves.share_left(mixed_a_low)
    qkv_bias = jnp.concatenate([b_q, jnp.zeros((D,), jnp.float32), b_v])
    qkv_low = (matmul(mixed_a_low, w_qkv) + qkv_bias).astype(LOW)
    queries = qkv_low[..., :D]
    near_kv = qkv_low[..., D:]
    far_kv = passed_along(near_kv, "blk", 1)
    near_s = score_block(queries, near_kv)
    far_s = score_block(queries, far_kv)
    row_top = jnp.maximum(jnp.max(near_s, axis=-1), jnp.max(far_s, axis=-1))
    row_total = jnp.sum(jnp.exp(near_s - row_top[..., None]), axis=-1) + jnp.sum(
        jnp.exp(far_s - row_top[..., None]), axis=-1
    )
    log_sum = row_top + jnp.log(row_total)
    attended = weigh_values(jnp.exp(near_s - log_sum[..., None]), near_kv) + weigh_values(
        jnp.exp(far_s - log_sum[..., None]), far_kv
    )
    att_low = attended.astype(LOW)
    left_proj = moves.share_left(att_low)
    branch_a = matmul(att_low, w_proj) + b_proj
    residual = hidden_f + gate_a[:, None, :] * branch_a
    mixed_m, pull_m = jax.vjp(modulate, residual, scale_m, shift_m)
    mixed_m_low = mixed_m.astype(LOW)
    left_up = moves.share_left(mixed_m_low)
    pre_act = matmul(mixed_m_low, w_up) + b_up
    activated, gelu_pull = jax.vjp(gelu_tanh, pre_act)
    act_low = activated.astype(LOW)
    left_down = moves.share_left(act_low)
    branch_m = matmul(act_low, w_down) + b_down
    output = residual + gate_m[:, None, :] * branch_m
    out_low = output.astype(LOW)
    left_one = moves.share_left(out_low)
    hid_one = matmul(out_low, w_one) + c_one
    act_one, silu_one = jax.vjp(jax.nn.silu, hid_one)
    one_low = act_one.astype(LOW)
    left_two = moves.share_left(one_low)
    hid_two = matmul(one_low, w_two) + c_two
    act_two, silu_two = jax.vjp(jax.nn.silu, hid_two)
    two_low = act_two.astype(LOW)
    left_three = moves.share_left(two_low)
    projection = matmul(two_low, w_three) + c_three
    live_f = live_slots.astype(jnp.float32)[:, None, None]
    unit_proj, unit_pull = jax.vjp(rms_unit, projection)
    grad_proj = unit_pull(-LAMBDA_REPA * live_f * rms_unit(targets.astype(jnp.float32)))[0].astype(
        LOW
    )
    grad_pthree = moves.weight_grad(left_three, grad_proj)
    grad_cthree = column_sum(grad_proj)
    grad_htwo = silu_two(matmul_t(grad_proj, w_three))[0].astype(LOW)
    grad_ptwo = moves.weight_grad(left_two, grad_htwo)
    grad_ctwo = column_sum(grad_htwo)
    grad_hone = silu_one(matmul_t(grad_htwo, w_two))[0].astype(LOW)
    grad_pone = moves.weight_grad(left_one, grad_hone)
    grad_cone = column_sum(grad_hone)
    grad_output = cotangent.astype(jnp.float32) * live_f + matmul_t(grad_hone, w_one)
    grad_gate_m = jnp.sum(grad_output * branch_m, axis=1)
    grad_bm = (gate_m[:, None, :] * grad_output).astype(LOW)
    grad_wdown = moves.weight_grad(left_down, grad_bm)
    grad_bdown = column_sum(grad_bm)
    grad_pre = gelu_pull(matmul_t(grad_bm, w_down))[0].astype(LOW)
    grad_wup = moves.weight_grad(left_up, grad_pre)
    grad_bup = column_sum(grad_pre)
    grad_res_m, grad_scale_m, grad_shift_m = pull_m(matmul_t(grad_pre, w_up))
    grad_residual = grad_output + grad_res_m
    grad_gate_a = jnp.sum(grad_residual * branch_a, axis=1)
    grad_ba = (gate_a[:, None, :] * grad_residual).astype(LOW)
    grad_wproj = moves.weight_grad(left_proj, grad_ba)
    grad_bproj = column_sum(grad_ba)
    grad_att = matmul_t(grad_ba, w_proj).astype(LOW)
    near_p, near_dp = grad_block(queries, near_kv, log_sum, grad_att)
    far_p, far_dp = grad_block(queries, far_kv, log_sum, grad_att)
    row_delta = jnp.sum(near_p * near_dp, axis=-1) + jnp.sum(far_p * far_dp, axis=-1)
    near_ds = (near_p * (near_dp - row_delta[..., None])).astype(LOW)
    far_ds = (far_p * (far_dp - row_delta[..., None])).astype(LOW)
    grad_query = (key_product(near_ds, near_kv) + key_product(far_ds, far_kv)) * E ** (-0.5)
    far_dkv = kv_grads(far_ds, far_p, queries, grad_att)
    home_dkv = passed_along(far_dkv.astype(LOW), "blk", -1).astype(far_dkv.dtype)
    near_dkv = kv_grads(near_ds, near_p, queries, grad_att)
    grad_qkv = jnp.concatenate([grad_query, near_dkv + home_dkv], axis=-1).astype(LOW)
    grad_wqkv = moves.weight_grad(left_qkv, grad_qkv)
    qkv_sums = column_sum(grad_qkv)
    grad_hid_a, grad_scale_a, grad_shift_a = pull_a(matmul_t(grad_qkv, w_qkv))
    grad_input = grad_residual + grad_hid_a
    grad_mod_part = jnp.concatenate(
        [grad_shift_a, grad_scale_a, grad_gate_a, grad_shift_m, grad_scale_m, grad_gate_m], axis=1
    )
    bias_terms = (
        qkv_sums[:D],
        qkv_sums[2 * D :],
        grad_bproj,
        grad_bup,
        grad_bdown,
        grad_cone,
        grad_ctwo,
        grad_cthree,
    )
    bias_grid = jnp.concatenate(
        [segment.reshape(blocks, -1) for segment in bias_terms], axis=1
    ).reshape(-1)
    grad_small = jnp.concatenate([grad_mod_part.reshape(-1), bias_grid])
    grad_small = (grad_small + lax.ppermute(grad_small, "blk", SWAP)).astype(LOW)
    small_all = moves.gather_slots(grad_small)
    mod_len = slots * 6 * D
    grad_mod = small_all[:, :mod_len].reshape(blocks * slots, 6 * D)
    grad_wada = jnp.einsum("si,sj->ij", cond_own, grad_mod, preferred_element_type=jnp.float32)
    grad_bada = lax.dynamic_index_in_dim(
        jnp.sum(grad_mod.astype(jnp.float32), axis=0).reshape(blocks, -1),
        moves.own_row,
        0,
        keepdims=False,
    )
    bias_own = jnp.sum(
        lax.dynamic_index_in_dim(
            small_all[:, mod_len:].reshape(blocks, blocks, -1), moves.own_row, 1, keepdims=False
        ).astype(jnp.float32),
        axis=0,
    )
    ada_at = (3 * D + FF + D) // blocks
    grad_b_flat = jnp.concatenate([bias_own[:ada_at], grad_bada, bias_own[ada_at:]])
    cond_cols = matmul_t(grad_mod, p_ada).reshape(blocks, slots, rows_d)
    cond_rows = moves.rows_in_order(moves.slots_seen_from(moves.gather_slots(cond_cols)))
    grad_cond = silu_cond(cond_rows.transpose(1, 0, 2).reshape(slots, D))[0]
    grad_w_flat = jnp.concatenate(
        [
            part.reshape(-1)
            for part in (
                grad_wqkv,
                grad_wproj,
                grad_wup,
                grad_wdown,
                grad_wada,
                grad_pone,
                grad_ptwo,
                grad_pthree,
            )
        ]
    )
    images_all = slots * blocks
    tokens_img = local_tok * lax.axis_size("blk")
    rate_w = LR_COEF / math.sqrt(images_all * tokens_img)
    rate_b = BIAS_FACTOR * rate_w
    mom_w = MOMENTUM * weight_momentum + grad_w_flat
    new_w = weights - rate_w * (grad_w_flat + MOMENTUM * mom_w)
    avg_w = AVERAGE * weight_average + (1.0 - AVERAGE) * new_w
    mom_b = MOMENTUM * bias_momentum + grad_b_flat
    new_b = biases - rate_b * (grad_b_flat + MOMENTUM * mom_b)
    avg_b = AVERAGE * bias_average + (1.0 - AVERAGE) * new_b
    return (
        out_low,
        grad_input,
        grad_cond,
        mom_w,
        new_w,
        new_w.astype(LOW),
        avg_w,
        mom_b,
        new_b,
        new_b.astype(LOW),
        avg_b,
    )


def solution(mesh):
    in_specs = (
        P(("inner", "outer"), "blk", None),
        P(("inner", "outer")),
        P(("inner", "outer")),
        P(("inner", "outer")),
        P(),
        P(("inner", "outer"), "blk", None),
        P(("inner", "outer"), "blk", None),
        P(("inner", "outer")),
        P(("inner", "outer")),
        P(("inner", "outer")),
        P(("inner", "outer")),
        P(("inner", "outer")),
        P(("inner", "outer")),
    )
    out_specs = (
        P(("inner", "outer"), "blk", None),
        P(("inner", "outer"), "blk", None),
        P(("inner", "outer"), None),
        P(("inner", "outer")),
        P(("inner", "outer")),
        P(("inner", "outer")),
        P(("inner", "outer")),
        P(("inner", "outer")),
        P(("inner", "outer")),
        P(("inner", "outer")),
        P(("inner", "outer")),
    )
    return jax.shard_map(body, mesh=mesh, in_specs=in_specs, out_specs=out_specs, check_vma=False)
```

time: 2390 us -> 3230 us (1.35)
  Pallas kernels: 0 us -> 2210 us
  waiting for transfers between devices: 1770 us -> 276 us
  starting transfers between devices: 0.92 us -> 238 us
  blocking collectives: 133 us -> 0 us
  other arithmetic: 73.7 us -> 129 us
  matrix products: 247 us -> 211 us
    pallas_call x0 -> x14, Pallas kernels: none -> 2210 us  [the longest x7 1470 us: place_blocks(): pl.pallas_call(kernel, out_shape=jax.ShapeDtypeStruct(shape, sources[0].d...]
    reduce_scatter x8 -> x0, waiting for transfers between devices: 942 us -> none  [the longest x1 262 us: body(): lax.psum_scatter(grad_wada.astype(jnp.bfloat16), 'inner', scatter_dimensi...]
    all_gather x8 -> x0, waiting for transfers between devices: 680 us -> none  [the longest x1 128 us: body(): lax.all_gather(p_up, ('inner', 'outer'), axis=0, tiled=True)]
    ppermute x0 -> x127, waiting for transfers between devices: none -> 276 us  [the longest x7 63.3 us: weight_grad(): straight = lax.ppermute(first, EVERY, flipped(Z_STRAIGHT))]
    ppermute x0 -> x127, starting transfers between devices: none -> 237 us  [the longest x7 37.7 us: gather_rows(): mate_four = lax.ppermute(four, 'blk', SWAP)]
    psum x1 -> x0, waiting for transfers between devices: 146 us -> none  [body(): lax.psum(grid_w.astype(jnp.bfloat16), ('blk', 'outer')).astype(jnp.float32)]
    unnamed x2 -> x0, blocking collectives: 99.6 us -> none
    psum x2 -> x0, blocking collectives: 32.9 us -> none  [the longest x1 29 us: body(): lax.psum(grid_b.astype(jnp.bfloat16), ('blk', 'outer')).astype(jnp.float32)]
  transfers between devices with their start and end apart: 19 -> 129, of which waited for: 15 -> 35; matrix products, arithmetic and copies ran while one was open for 13% -> 8% of each run, Pallas kernels for 0% -> 69%
where the time goes in v1:
time: 3230 us; the launch traced here: 3220 us
  Pallas kernels  2210 us (68%)
  waiting for transfers between devices  276 us (9%)
  starting transfers between devices  238 us (7%)
  matrix products  211 us (7%)
  local copies, waits for them, and re-layouts  146 us (5%)
  other arithmetic  129 us (4%)
    pallas_call x7, Pallas kernels, place_blocks(): pl.pallas_call(kernel, out_shape=jax.ShapeDtypeStruct(shape, sources[0].d...  1470 us
    pallas_call x7, Pallas kernels, pick_blocks(): pl.pallas_call(kernel, out_shape=[jax.ShapeDtypeStruct((length,) + source...  742 us
  transfers between devices with their start and end apart: 129, of which 35 were waited for; matrix products, arithmetic and copies ran while one was open for 8% of the time, Pallas kernels for 69%

profile of v1, /device:TPU:0, one launch (start us, length us, event | category | flops | bytes accessed | tf_op | source)
XLA Modules:
  0.0 3215.7 jit_solution(11385259061557857665)
XLA Ops:
  143.8 17.0 collective-permute-start.8
  175.1 13.9 collective-permute-done.33
  232.7 14.2 collective-permute-start.45
  261.0 27.1 collective-permute-done.36
  288.1 14.1 collective-permute-start.16
  319.0 243.1 %place_blocks.7 = bf16[16,72,3456]{2,1,0:T(8,128)(2,1)} custom-call(s32[16]{0:T(128)} %stack.633.table_ref, bf16[4,72,3456]{2,1,0:T(8,128)(2,1)} %pad_maximum_fusion.7.refs_0_, bf16[4,72,3456]{2,1,0:T(8,128)(2,1)} %collective-permute-done.15.refs_1_, bf16[4,72,3456]{2,1,0:T(8,128)(2,1)} %copy-done.60, bf16[4,72,3456]{2,1,0:T(8,128)(2,1)} %copy-done.62), custom_call_target="tpu_custom_call" | custom-call | tf_op jit(solution)/shard_map/place_blocks/pallas_call | solution.py:127
  582.7 82.3 %place_blocks.8 = bf16[16,72,1152]{2,1,0:T(8,128)(2,1)} custom-call(s32[16]{0:T(128)} %stack.633.table_ref, bf16[4,72,1152]{2,1,0:T(8,128)(2,1)} %copy-done.52, bf16[4,72,1152]{2,1,0:T(8,128)(2,1)} %copy-done.81, bf16[4,72,1152]{2,1,0:T(8,128)(2,1)} %copy-done.82, bf16[4,72,1152]{2,1,0:T(8,128)(2,1)} %copy-done.83), custom_call_target="tpu_custom_call" | custom-call | tf_op jit(solution)/shard_map/place_blocks/pallas_call | solution.py:127
  665.0 97.2 %place_blocks.13 = bf16[16,128,768]{2,1,0:T(8,128)(2,1)} custom-call(s32[16]{0:T(128)} %stack.633.table_ref, bf16[4,128,768]{2,1,0:T(8,128)(2,1)} %copy-done.43, bf16[4,128,768]{2,1,0:T(8,128)(2,1)} %copy-done.74, bf16[4,128,768]{2,1,0:T(8,128)(2,1)} %copy-done.75, bf16[4,128,768]{2,1,0:T(8,128)(2,1)} %copy-done.76), custom_call_target="tpu_custom_call" | custom-call | tf_op jit(solution)/shard_map/place_blocks/pallas_call | solution.py:127
  762.2 144.9 %place_blocks.11 = bf16[16,72,2048]{2,1,0:T(8,128)(2,1)} custom-call(s32[16]{0:T(128)} %stack.633.table_ref, bf16[4,72,2048]{2,1,0:T(8,128)(2,1)} %copy-done.36, bf16[4,72,2048]{2,1,0:T(8,128)(2,1)} %collective-permute-done.44.refs_1_, bf16[4,72,2048]{2,1,0:T(8,128)(2,1)} %collective-permute-done.45.refs_2_, bf16[4,72,2048]{2,1,0:T(8,128)(2,1)} %collective-permute-done.46.refs_3_), custom_call_target="tpu_custom_call" | custom-call | tf_op jit(solution)/shard_map/place_blocks/pallas_call | solution.py:127
  920.9 256.0 %place_blocks.12 = bf16[16,128,2048]{2,1,0:T(8,128)(2,1)} custom-call(s32[16]{0:T(128)} %stack.633.table_ref, bf16[4,128,2048]{2,1,0:T(8,128)(2,1)} %pad_maximum_fusion.6.refs_0_, bf16[4,128,2048]{2,1,0:T(8,128)(2,1)} %collective-permute-done.51.refs_1_, bf16[4,128,2048]{2,1,0:T(8,128)(2,1)} %collective-permute-done.52.refs_2_, ...), custom_call_target="tpu_custom_call" | custom-call | tf_op jit(solution)/shard_map/place_blocks/pallas_call | solution.py:127
  1177.0 323.5 %place_blocks.9 = bf16[16,72,4608]{2,1,0:T(8,128)(2,1)} custom-call(s32[16]{0:T(128)} %stack.633.table_ref, bf16[4,72,4608]{2,1,0:T(8,128)(2,1)} %pad_maximum_fusion.2.refs_0_, bf16[4,72,4608]{2,1,0:T(8,128)(2,1)} %collective-permute-done.30.refs_1_, bf16[4,72,4608]{2,1,0:T(8,128)(2,1)} %collective-permute-done.31.refs_2_, ...), custom_call_target="tpu_custom_call" | custom-call | tf_op jit(solution)/shard_map/place_blocks/pallas_call | solution.py:127
  1500.5 323.5 %place_blocks.10 = bf16[16,288,1152]{2,1,0:T(8,128)(2,1)} custom-call(s32[16]{0:T(128)} %stack.633.table_ref, bf16[4,288,1152]{2,1,0:T(8,128)(2,1)} %pad_maximum_fusion.3.refs_0_, bf16[4,288,1152]{2,1,0:T(8,128)(2,1)} %collective-permute-done.37.refs_1_, bf16[4,288,1152]{2,1,0:T(8,128)(2,1)} %collective-permute-done.38.refs_2_, ...), custom_call_target="tpu_custom_call" | custom-call | tf_op jit(solution)/shard_map/place_blocks/pallas_call | solution.py:127
  1913.8 17.2 convert_reduce_fusion
  2017.5 49.5 %pick_blocks.13 = (bf16[4,128,768]{2,1,0:T(8,128)(2,1)}, bf16[4,128,768]{2,1,0:T(8,128)(2,1)}) custom-call(s32[8]{0:T(128)} %stack.715.table_ref, bf16[8,128,768]{2,1,0:T(8,128)(2,1)} %bitcast.354), custom_call_target="tpu_custom_call" | custom-call | tf_op jit(solution)/shard_map/pick_blocks/pallas_call | solution.py:161
  2074.9 42.0 %pick_blocks.8 = (bf16[4,72,1152]{2,1,0:T(8,128)(2,1)}, bf16[4,72,1152]{2,1,0:T(8,128)(2,1)}) custom-call(s32[8]{0:T(128)} %stack.715.table_ref, bf16[8,72,1152]{2,1,0:T(8,128)(2,1)} %bitcast.356), custom_call_target="tpu_custom_call" | custom-call | tf_op jit(solution)/shard_map/pick_blocks/pallas_call | solution.py:161
  2156.5 73.3 %pick_blocks.11 = (bf16[4,72,2048]{2,1,0:T(8,128)(2,1)}, bf16[4,72,2048]{2,1,0:T(8,128)(2,1)}) custom-call(s32[8]{0:T(128)} %stack.715.table_ref, bf16[8,72,2048]{2,1,0:T(8,128)(2,1)} %bitcast.350), custom_call_target="tpu_custom_call" | custom-call | tf_op jit(solution)/shard_map/pick_blocks/pallas_call | solution.py:161
  2229.8 128.9 %pick_blocks.12 = (bf16[4,128,2048]{2,1,0:T(8,128)(2,1)}, bf16[4,128,2048]{2,1,0:T(8,128)(2,1)}) custom-call(s32[8]{0:T(128)} %stack.715.table_ref, bf16[8,128,2048]{2,1,0:T(8,128)(2,1)} %bitcast.345), custom_call_target="tpu_custom_call" | custom-call | tf_op jit(solution)/shard_map/pick_blocks/pallas_call | solution.py:161
  2414.4 162.8 %pick_blocks.10 = (bf16[4,288,1152]{2,1,0:T(8,128)(2,1)}, bf16[4,288,1152]{2,1,0:T(8,128)(2,1)}) custom-call(s32[8]{0:T(128)} %stack.715.table_ref, bf16[8,288,1152]{2,1,0:T(8,128)(2,1)} %bitcast.330), custom_call_target="tpu_custom_call" | custom-call | tf_op jit(solution)/shard_map/pick_blocks/pallas_call | solution.py:161
  2659.5 26.4 collective-permute-done.72
  2729.8 162.6 %pick_blocks.9 = (bf16[4,72,4608]{2,1,0:T(8,128)(2,1)}, bf16[4,72,4608]{2,1,0:T(8,128)(2,1)}) custom-call(s32[8]{0:T(128)} %stack.715.table_ref, bf16[8,72,4608]{2,1,0:T(8,128)(2,1)} %bitcast.331), custom_call_target="tpu_custom_call" | custom-call | tf_op jit(solution)/shard_map/pick_blocks/pallas_call | solution.py:161
  2926.3 14.5 fusion.20
  2940.8 122.4 %pick_blocks.7 = (bf16[4,72,3456]{2,1,0:T(8,128)(2,1)}, bf16[4,72,3456]{2,1,0:T(8,128)(2,1)}) custom-call(s32[8]{0:T(128)} %stack.715.table_ref, bf16[8,72,3456]{2,1,0:T(8,128)(2,1)} %bitcast.347), custom_call_target="tpu_custom_call" | custom-call | tf_op jit(solution)/shard_map/pick_blocks/pallas_call | solution.py:161
  3151.8 18.7 collective-permute-done.94
  3190.4 20.1 add_multiply_fusion
  (830 shorter events, 816.3 us)
Async XLA Ops:
  307.7 255.1 %collective-permute-start.30 = (bf16[4,72,4608]{2,1,0:T(8,128)(2,1)}, bf16[4,72,4608]{2,1,0:T(8,128)(2,1)}, u32[]{:S(2)}, u32[]{:S(2)}) collective-permute-start(bf16[4,72,4608]{2,1,0:T(8,128)(2,1)} %pad_maximum_fusion.2.refs_0_), channel_id=1, source_target_pairs={{0,2},{16,17},{1,3},{17,16},{2,0},{18,19},{3,1},{19,18},{4,6},{20,... | collective-permute-start | bytes 7962632 | tf_op jit(solution)/shard_map/ppermute | solution.py:209
  308.8 254.5 %collective-permute-start.37 = (bf16[4,288,1152]{2,1,0:T(8,128)(2,1)}, bf16[4,288,1152]{2,1,0:T(8,128)(2,1)}, u32[]{:S(2)}, u32[]{:S(2)}) collective-permute-start(bf16[4,288,1152]{2,1,0:T(8,128)(2,1)} %pad_maximum_fusion.3.refs_0_), channel_id=1, source_target_pairs={{0,2},{16,17},{1,3},{17,16},{2,0},{18,19},{3,1},{19,18},{4,6},{20,... | collective-permute-start | bytes 7962632 | tf_op jit(solution)/shard_map/ppermute | solution.py:209
  309.8 252.9 %collective-permute-start.52 = (bf16[4,128,2048]{2,1,0:T(8,128)(2,1)}, bf16[4,128,2048]{2,1,0:T(8,128)(2,1)}, u32[]{:S(2)}, u32[]{:S(2)}) collective-permute-start(bf16[4,128,2048]{2,1,0:T(8,128)(2,1)} %pad_maximum_fusion.6.refs_0_), channel_id=1, source_target_pairs={{0,16},{16,0},{1,17},{17,1},{2,18},{18,2},{3,19},{19,3},{4,20},{20... | collective-permute-start | bytes 6291464 | tf_op jit(solution)/shard_map/ppermute | solution.py:210
  316.8 245.4 %collective-permute-start.46 = (bf16[4,72,2048]{2,1,0:T(8,128)(2,1)}, bf16[4,72,2048]{2,1,0:T(8,128)(2,1)}, u32[]{:S(2)}, u32[]{:S(2)}) collective-permute-start(bf16[4,72,2048]{2,1,0:T(8,128)(2,1)} %collective-permute-done.44.refs_1_), channel_id=1, source_target_pairs={{0,16},{16,0},{1,17},{17,1},{2,18},{18,2},{3,19},{19,3},{4,20},{20... | collective-permute-start | bytes 3538952 | tf_op jit(solution)/shard_map/ppermute | solution.py:211
  316.9 257.9 %collective-permute-start.53 = (bf16[4,128,2048]{2,1,0:T(8,128)(2,1)}, bf16[4,128,2048]{2,1,0:T(8,128)(2,1)}, u32[]{:S(2)}, u32[]{:S(2)}) collective-permute-start(bf16[4,128,2048]{2,1,0:T(8,128)(2,1)} %collective-permute-done.51.refs_1_), channel_id=1, source_target_pairs={{0,16},{16,0},{1,17},{17,1},{2,18},{18,2},{3,19},{19,3},{4,20},{20... | collective-permute-start | bytes 6291464 | tf_op jit(solution)/shard_map/ppermute | solution.py:211
  562.2 614.8 %collective-permute-start.31 = (bf16[4,72,4608]{2,1,0:T(8,128)(2,1)}, bf16[4,72,4608]{2,1,0:T(8,128)(2,1)}, u32[]{:S(2)}, u32[]{:S(2)}) collective-permute-start(bf16[4,72,4608]{2,1,0:T(8,128)(2,1)} %pad_maximum_fusion.2.refs_0_), channel_id=1, source_target_pairs={{0,16},{16,0},{1,17},{17,1},{2,18},{18,2},{3,19},{19,3},{4,20},{20... | collective-permute-start | bytes 7962632 | tf_op jit(solution)/shard_map/ppermute | solution.py:210
  562.8 937.7 %collective-permute-start.38 = (bf16[4,288,1152]{2,1,0:T(8,128)(2,1)}, bf16[4,288,1152]{2,1,0:T(8,128)(2,1)}, u32[]{:S(2)}, u32[]{:S(2)}) collective-permute-start(bf16[4,288,1152]{2,1,0:T(8,128)(2,1)} %pad_maximum_fusion.3.refs_0_), channel_id=1, source_target_pairs={{0,16},{16,0},{1,17},{17,1},{2,18},{18,2},{3,19},{19,3},{4,20},{20... | collective-permute-start | bytes 7962632 | tf_op jit(solution)/shard_map/ppermute | solution.py:210
  562.9 614.1 %collective-permute-start.32 = (bf16[4,72,4608]{2,1,0:T(8,128)(2,1)}, bf16[4,72,4608]{2,1,0:T(8,128)(2,1)}, u32[]{:S(2)}, u32[]{:S(2)}) collective-permute-start(bf16[4,72,4608]{2,1,0:T(8,128)(2,1)} %collective-permute-done.30.refs_1_), channel_id=1, source_target_pairs={{0,16},{16,0},{1,17},{17,1},{2,18},{18,2},{3,19},{19,3},{4,20},{20... | collective-permute-start | bytes 7962632 | tf_op jit(solution)/shard_map/ppermute | solution.py:211
  563.3 937.2 %collective-permute-start.39 = (bf16[4,288,1152]{2,1,0:T(8,128)(2,1)}, bf16[4,288,1152]{2,1,0:T(8,128)(2,1)}, u32[]{:S(2)}, u32[]{:S(2)}) collective-permute-start(bf16[4,288,1152]{2,1,0:T(8,128)(2,1)} %collective-permute-done.37.refs_1_), channel_id=1, source_target_pairs={{0,16},{16,0},{1,17},{17,1},{2,18},{18,2},{3,19},{19,3},{4,20},{20... | collective-permute-start | bytes 7962632 | tf_op jit(solution)/shard_map/ppermute | solution.py:211
  574.8 1249.3 %collective-permute-start.18 = (bf16[4,128,2304]{2,1,0:T(8,128)(2,1)}, bf16[4,128,2304]{2,1,0:T(8,128)(2,1)}, u32[]{:S(2)}, u32[]{:S(2)}) collective-permute-start(bf16[4,128,2304]{2,1,0:T(8,128)(2,1)} %slice.543), channel_id=1, source_target_pairs={{16,0},{0,16},{17,1},{1,17},{18,2},{2,18},{19,3},{3,19},{20,4},{4,... | collective-permute-start | bytes 7077896 | tf_op jit(solution)/shard_map/ppermute | solution.py:31
  2136.4 243.7 %collective-permute-start.61 = (bf16[4,128,2304]{2,1,0:T(8,128)(2,1)}, bf16[4,128,2304]{2,1,0:T(8,128)(2,1)}, u32[]{:S(2)}, u32[]{:S(2)}) collective-permute-start(bf16[4,128,2304]{2,1,0:T(8,128)(2,1)} %pad_maximum_fusion.4), channel_id=1, source_target_pairs={{16,0},{0,16},{17,1},{1,17},{18,2},{2,18},{19,3},{3,19},{20,4},{4,... | collective-permute-start | bytes 7077896 | tf_op jit(solution)/shard_map/ppermute | solution.py:31
  2138.0 582.1 %collective-permute-start.90 = (bf16[512,4608]{1,0:T(8,128)(2,1)}, bf16[512,4608]{1,0:T(8,128)(2,1)}, u32[]{:S(2)}, u32[]{:S(2)}) collective-permute-start(bf16[512,4608]{1,0:T(8,128)(2,1)} %bitcast.392), channel_id=1, source_target_pairs={{0,16},{16,0},{1,17},{17,1},{2,18},{18,2},{3,19},{19,3},{4,20},{20... | collective-permute-start | bytes 14155784 | tf_op jit(solution)/shard_map/ppermute | solution.py:231
  2140.1 229.8 %collective-permute-start.124 = (bf16[2,128,768]{2,1,0:T(8,128)(2,1)S(1)}, bf16[2,128,768]{2,1,0:T(8,128)(2,1)S(1)}, u32[]{:S(2)}, u32[]{:S(2)}) collective-permute-start(bf16[2,128,768]{2,1,0:T(8,128)(2,1)S(1)} %get-tuple-element.101), channel_id=1, source_target_pairs={{0,1},{16,18},{1,0},{17,19},{2,3},{18,16},{3,2},{19,17},{4,5},{20,... | collective-permute-start | bytes 1179656 | tf_op jit(solution)/shard_map/ppermute | solution.py:243
  2149.5 209.2 %collective-permute-start.84 = (bf16[2,72,1152]{2,1,0:T(8,128)(2,1)S(1)}, bf16[2,72,1152]{2,1,0:T(8,128)(2,1)S(1)}, u32[]{:S(2)}, u32[]{:S(2)}) collective-permute-start(bf16[2,72,1152]{2,1,0:T(8,128)(2,1)S(1)} %get-tuple-element.103), channel_id=1, source_target_pairs={{0,1},{16,18},{1,0},{17,19},{2,3},{18,16},{3,2},{19,17},{4,5},{20,... | collective-permute-start | bytes 995336 | tf_op jit(solution)/shard_map/ppermute | solution.py:243
  2379.3 230.5 %collective-permute-start.107 = (bf16[4,72,2048]{2,1,0:T(8,128)(2,1)}, bf16[4,72,2048]{2,1,0:T(8,128)(2,1)}, u32[]{:S(2)}, u32[]{:S(2)}) collective-permute-start(bf16[4,72,2048]{2,1,0:T(8,128)(2,1)} %get-tuple-element.34), channel_id=1, source_target_pairs={{0,2},{16,17},{1,3},{17,16},{2,0},{18,19},{3,1},{19,18},{4,6},{20,... | collective-permute-start | bytes 3538952 | tf_op jit(solution)/shard_map/ppermute | solution.py:240
  2380.2 200.8 %collective-permute-start.127 = (bf16[128,768]{1,0:T(8,128)(2,1)S(1)}, bf16[128,768]{1,0:T(8,128)(2,1)S(1)}, u32[]{:S(2)}, u32[]{:S(2)}) collective-permute-start(bf16[128,768]{1,0:T(8,128)(2,1)S(1)} %get-tuple-element.117), channel_id=1, source_target_pairs={{12,0},{16,28},{13,1},{17,29},{14,2},{18,30},{15,3},{19,31},{8,4},... | collective-permute-start | bytes 589832 | tf_op jit(solution)/shard_map/ppermute | solution.py:248
  2401.1 180.5 %collective-permute-start.125 = (bf16[128,768]{1,0:T(8,128)(2,1)S(1)}, bf16[128,768]{1,0:T(8,128)(2,1)S(1)}, u32[]{:S(2)}, u32[]{:S(2)}) collective-permute-start(bf16[128,768]{1,0:T(8,128)(2,1)S(1)} %get-tuple-element.117), channel_id=1, source_target_pairs={{4,0},{24,28},{5,1},{25,29},{6,2},{26,30},{7,3},{27,31},{0,4},{28,... | collective-permute-start | bytes 589832 | tf_op jit(solution)/shard_map/ppermute | solution.py:246
  2403.0 178.0 %collective-permute-start.126 = (bf16[128,768]{1,0:T(8,128)(2,1)S(1)}, bf16[128,768]{1,0:T(8,128)(2,1)S(1)}, u32[]{:S(2)}, u32[]{:S(2)}) collective-permute-start(bf16[128,768]{1,0:T(8,128)(2,1)S(1)} %get-tuple-element.116), channel_id=1, source_target_pairs={{8,0},{20,28},{9,1},{21,29},{10,2},{22,30},{11,3},{23,31},{12,4},{... | collective-permute-start | bytes 589832 | tf_op jit(solution)/shard_map/ppermute | solution.py:247
  2644.5 255.0 %collective-permute-start.99 = (bf16[4,288,1152]{2,1,0:T(8,128)(2,1)}, bf16[4,288,1152]{2,1,0:T(8,128)(2,1)}, u32[]{:S(2)}, u32[]{:S(2)}) collective-permute-start(bf16[4,288,1152]{2,1,0:T(8,128)(2,1)} %get-tuple-element.32), channel_id=1, source_target_pairs={{0,2},{16,17},{1,3},{17,16},{2,0},{18,19},{3,1},{19,18},{4,6},{20,... | collective-permute-start | bytes 7962632 | tf_op jit(solution)/shard_map/ppermute | solution.py:240
  2707.7 218.5 %collective-permute-start.74 = (bf16[512,3456]{1,0:T(8,128)(2,1)}, bf16[512,3456]{1,0:T(8,128)(2,1)}, u32[]{:S(2)}, u32[]{:S(2)}) collective-permute-start(bf16[512,3456]{1,0:T(8,128)(2,1)} %pad_maximum_fusion.1), channel_id=1, source_target_pairs={{0,16},{16,0},{1,17},{17,1},{2,18},{18,2},{3,19},{19,3},{4,20},{20... | collective-permute-start | bytes 10616840 | tf_op jit(solution)/shard_map/ppermute | solution.py:231
  2718.2 174.3 %collective-permute-start.116 = (bf16[2,128,2048]{2,1,0:T(8,128)(2,1)}, bf16[2,128,2048]{2,1,0:T(8,128)(2,1)}, u32[]{:S(2)}, u32[]{:S(2)}) collective-permute-start(bf16[2,128,2048]{2,1,0:T(8,128)(2,1)} %get-tuple-element.73), channel_id=1, source_target_pairs={{0,1},{16,18},{1,0},{17,19},{2,3},{18,16},{3,2},{19,17},{4,5},{20,... | collective-permute-start | bytes 3145736 | tf_op jit(solution)/shard_map/ppermute | solution.py:243
  2720.1 206.1 %collective-permute-start.73 = (bf16[512,576]{0,1:T(8,128)(2,1)}, bf16[512,576]{0,1:T(8,128)(2,1)}, u32[]{:S(2)}, u32[]{:S(2)}) collective-permute-start(bf16[512,576]{0,1:T(8,128)(2,1)} %copy.207), channel_id=1, source_target_pairs={{0,16},{16,0},{1,17},{17,1},{2,18},{18,2},{3,19},{19,3},{4,20},{20... | collective-permute-start | bytes 1769480 | tf_op jit(solution)/shard_map/ppermute | solution.py:227
  2912.5 155.2 %collective-permute-start.112 = (bf16[72,2048]{1,0:T(8,128)(2,1)S(1)}, bf16[72,2048]{1,0:T(8,128)(2,1)}, u32[]{:S(2)}, u32[]{:S(2)}) collective-permute-start(bf16[72,2048]{1,0:T(8,128)(2,1)S(1)} %copy-done.72), channel_id=1, source_target_pairs={{0,16},{16,0},{1,17},{17,1},{2,18},{18,2},{3,19},{19,3},{4,20},{20... | collective-permute-start | bytes 884744 | tf_op jit(solution)/shard_map/ppermute | solution.py:253
  2923.6 176.9 %collective-permute-start.91 = (bf16[4,72,4608]{2,1,0:T(8,128)(2,1)}, bf16[4,72,4608]{2,1,0:T(8,128)(2,1)}, u32[]{:S(2)}, u32[]{:S(2)}) collective-permute-start(bf16[4,72,4608]{2,1,0:T(8,128)(2,1)} %get-tuple-element.30), channel_id=1, source_target_pairs={{0,2},{16,17},{1,3},{17,16},{2,0},{18,19},{3,1},{19,18},{4,6},{20,... | collective-permute-start | bytes 7962632 | tf_op jit(solution)/shard_map/ppermute | solution.py:240
  (243 other events, 7068.1 us)

commit v2 on v1

--- a/solution.py
+++ b/solution.py
@@ -103,75 +103,70 @@
 OUT_Y = [(0, 2), (2, 0), (1, 3), (3, 1)]
 
 
-def place_blocks(sources, table, count):
-    counts = [source.shape[0] for source in sources]
+def move_blocks(table, sources, outs, plan, name):
+    block = sources[0].shape[1:]
 
     def kernel(table_ref, *refs):
-        source_refs = refs[: len(counts)]
-        out_ref, sems = refs[len(counts) :]
-        copies = []
-        for source_ref, length in zip(source_refs, counts):
-            for at in range(length):
-                number = len(copies)
-                copies.append(
-                    pltpu.make_async_copy(
-                        source_ref.at[at], out_ref.at[table_ref[number]], sems.at[number]
-                    )
+        source_refs = refs[: len(sources)]
+        out_refs = refs[len(sources) : len(sources) + len(outs)]
+        held, sems_in, sems_out = refs[len(sources) + len(outs) :]
+        arriving, leaving = [], []
+        for number, (source_at, index, out_at, out_index) in enumerate(plan):
+            from_row = table_ref[number] if index is None else index
+            to_row = table_ref[number] if out_index is None else out_index
+            arriving.append(
+                pltpu.make_async_copy(
+                    source_refs[source_at].at[from_row], held.at[number], sems_in.at[number]
                 )
-        for copy in copies:
+            )
+            leaving.append(
+                pltpu.make_async_copy(
+                    held.at[number], out_refs[out_at].at[to_row], sems_out.at[number]
+                )
+            )
+        for copy in arriving:
             copy.start()
-        for copy in copies:
+        for copy_in, copy_out in zip(arriving, leaving):
+            copy_in.wait()
+            copy_out.start()
+        for copy in leaving:
             copy.wait()
 
-    shape = (count,) + sources[0].shape[1:]
+    count = len(plan)
+    low = sources[0].dtype
     return pl.pallas_call(
         kernel,
-        out_shape=jax.ShapeDtypeStruct(shape, sources[0].dtype),
+        out_shape=[jax.ShapeDtypeStruct((length,) + block, low) for length in outs],
         grid_spec=pltpu.PrefetchScalarGridSpec(
             num_scalar_prefetch=1,
             grid=(1,),
             in_specs=[pl.BlockSpec(memory_space=pl.ANY)] * len(sources),
-            out_specs=pl.BlockSpec(memory_space=pl.ANY),
-            scratch_shapes=[pltpu.SemaphoreType.DMA((count,))],
+            out_specs=[pl.BlockSpec(memory_space=pl.ANY)] * len(outs),
+            scratch_shapes=[
+                pltpu.VMEM((count,) + block, low),
+                pltpu.SemaphoreType.DMA((count,)),
+                pltpu.SemaphoreType.DMA((count,)),
+            ],
         ),
-        name="place_blocks",
+        compiler_params=pltpu.CompilerParams(vmem_limit_bytes=32 * 1024 * 1024),
+        name=name,
     )(table, *sources)
 
 
+def place_blocks(sources, table, count):
+    plan = [
+        (source_at, at, 0, None)
+        for source_at, source in enumerate(sources)
+        for at in range(source.shape[0])
+    ]
+    return move_blocks(table, sources, [count], plan, "place_blocks")[0]
+
+
 def pick_blocks(source, table, counts):
-    total = sum(counts)
-
-    def kernel(table_ref, source_ref, *refs):
-        out_refs = refs[: len(counts)]
-        sems = refs[len(counts)]
-        copies = []
-        for out_ref, length in zip(out_refs, counts):
-            for at in range(length):
-                number = len(copies)
-                copies.append(
-                    pltpu.make_async_copy(
-                        source_ref.at[table_ref[number]], out_ref.at[at], sems.at[number]
-                    )
-                )
-        for copy in copies:
-            copy.start()
-        for copy in copies:
-            copy.wait()
-
-    return pl.pallas_call(
-        kernel,
-        out_shape=[
-            jax.ShapeDtypeStruct((length,) + source.shape[1:], source.dtype) for length in counts
-        ],
-        grid_spec=pltpu.PrefetchScalarGridSpec(
-            num_scalar_prefetch=1,
-            grid=(1,),
-            in_specs=[pl.BlockSpec(memory_space=pl.ANY)],
-            out_specs=[pl.BlockSpec(memory_space=pl.ANY)] * len(counts),
-            scratch_shapes=[pltpu.SemaphoreType.DMA((total,))],
-        ),
-        name="pick_blocks",
-    )(table, source)
+    plan = [
+        (0, None, out_at, at) for out_at, length in enumerate(counts) for at in range(length)
+    ]
+    return move_blocks(table, [source], list(counts), plan, "pick_blocks")
 
 
 class Staged:

time: 3230 us -> 1120 us (0.35)
  Pallas kernels: 2210 us -> 69.7 us
  waiting for transfers between devices: 276 us -> 335 us
    pallas_call x14, Pallas kernels: 2210 us -> 69.7 us  [move_blocks(): pl.pallas_call(kernel, out_shape=[jax.ShapeDtypeStruct((length,) + block,...]
    ppermute x7, waiting for transfers between devices: 12 us -> 56.3 us  [gather_rows(): far_four = lax.ppermute(four, EVERY, NEAR_SECOND)]
  transfers between devices with their start and end apart: 129 -> 129, of which waited for: 35 -> 42; matrix products, arithmetic and copies ran while one was open for 8% -> 20% of each run, Pallas kernels for 69% -> 6%
where the time goes in v2:
time: 1120 us; the launch traced here: 1110 us
  waiting for transfers between devices  335 us (30%)
  starting transfers between devices  238 us (21%)
  matrix products  188 us (17%)
  local copies, waits for them, and re-layouts  154 us (14%)
  other arithmetic  121 us (11%)
  Pallas kernels  69.7 us (6%)
    pallas_call x14, Pallas kernels, move_blocks(): pl.pallas_call(kernel, out_shape=[jax.ShapeDtypeStruct((length,) + block,...  69.7 us
    ppermute x7, waiting for transfers between devices, weight_grad(): straight = lax.ppermute(first, EVERY, flipped(Z_STRAIGHT))  61.1 us
    dot_general x8, matrix products, matmul_t(): jnp.einsum('...j,ij->...i', left_arr, right_arr, preferred_element_type=j...  60.3 us
    unnamed x364, local copies, waits for them, and re-layouts  57.2 us
    ppermute x7, waiting for transfers between devices, gather_rows(): far_four = lax.ppermute(four, EVERY, NEAR_SECOND)  56.3 us
    dot_general x7, matrix products, weight_grad(): jnp.einsum('ni,nj->ij', left, both, preferred_element_type=jnp.float32)  48.7 us
    dot_general x8, matrix products, matmul(): jnp.einsum('...i,ij->...j', left_arr, right_arr, preferred_element_type=j...  47.1 us
    ppermute x7, waiting for transfers between devices, gather_rows(): four = jnp.concatenate([two, lax.ppermute(two, EVERY, NEAR_FIRST)])  40.9 us
  transfers between devices with their start and end apart: 129, of which 42 were waited for; matrix products, arithmetic and copies ran while one was open for 20% of the time, Pallas kernels for 6%

profile of v2, /device:TPU:0, one launch (start us, length us, event | category | flops | bytes accessed | tf_op | source)
XLA Modules:
  0.0 1109.6 jit_solution(3366981480269254478)
XLA Ops:
  80.3 12.9 %collective-permute-start.11 = (bf16[72,3456]{1,0:T(8,128)(2,1)}, bf16[72,3456]{1,0:T(8,128)(2,1)S(1)}, u32[]{:S(2)}, u32[]{:S(2)}) collective-permute-start(bf16[72,3456]{1,0:T(8,128)(2,1)} %reshape.1253), channel_id=1, source_target_pairs={{0,4},{28,24},{1,5},{29,25},{2,6},{30,26},{3,7},{31,27},{4,0},{24,... | collective-permute-start | bytes 1493000 | tf_op jit(solution)/shard_map/ppermute | solution.py:197
  127.4 12.3 %collective-permute-done.47 = bf16[128,2048]{1,0:T(8,128)(2,1)S(1)} collective-permute-done((bf16[128,2048]{1,0:T(8,128)(2,1)S(1)}, bf16[128,2048]{1,0:T(8,128)(2,1)S(1)}, u32[]{:S(2)}, u32[]{:S(2)}) %collective-permute-start.47) | collective-permute-done | bytes 524320 | tf_op jit(solution)/shard_map/ppermute | solution.py:197
  143.9 17.3 %collective-permute-start.8 = (f32[4,3456]{1,0:T(4,128)S(1)}, f32[4,3456]{1,0:T(4,128)S(1)}, u32[]{:S(2)}, u32[]{:S(2)}) collective-permute-start(f32[4,3456]{1,0:T(4,128)S(1)} %get-tuple-element.141), channel_id=1, source_target_pairs={{0,4},{4,8},{8,12},{12,0},{1,5},{5,9},{9,13},{13,1},{2,6},{6,10},{... | collective-permute-start | bytes 165896 | tf_op jit(solution)/shard_map/ppermute | solution.py:266
  175.5 13.9 %collective-permute-done.33 = bf16[288,1152]{1,0:T(8,128)(2,1)S(1)} collective-permute-done((bf16[288,1152]{1,0:T(8,128)(2,1)S(1)}, bf16[288,1152]{1,0:T(8,128)(2,1)S(1)}, u32[]{:S(2)}, u32[]{:S(2)}) %collective-permute-start.33) | collective-permute-done | bytes 663584 | tf_op jit(solution)/shard_map/ppermute | solution.py:197
  215.8 12.2 %collective-permute-start.25 = (bf16[4,72,1152]{2,1,0:T(8,128)(2,1)S(1)}, bf16[4,72,1152]{2,1,0:T(8,128)(2,1)S(1)}, u32[]{:S(2)}, u32[]{:S(2)}) collective-permute-start(bf16[4,72,1152]{2,1,0:T(8,128)(2,1)S(1)} %collective-permute-done.23.refs_1_), channel_id=1, source_target_pairs={{0,16},{16,0},{1,17},{17,1},{2,18},{18,2},{3,19},{19,3},{4,20},{20... | collective-permute-start | bytes 1990664 | tf_op jit(solution)/shard_map/ppermute | solution.py:206
  234.7 14.2 %collective-permute-start.45 = (bf16[4,72,2048]{2,1,0:T(8,128)(2,1)S(1)}, bf16[4,72,2048]{2,1,0:T(8,128)(2,1)}, u32[]{:S(2)}, u32[]{:S(2)}) collective-permute-start(bf16[4,72,2048]{2,1,0:T(8,128)(2,1)S(1)} %pad_maximum_fusion.9.refs_0_), channel_id=1, source_target_pairs={{0,16},{16,0},{1,17},{17,1},{2,18},{18,2},{3,19},{19,3},{4,20},{20... | collective-permute-start | bytes 3538952 | tf_op jit(solution)/shard_map/ppermute | solution.py:205
  248.9 11.1 collective-permute-done.29
  262.2 26.3 %collective-permute-done.36 = bf16[2,288,1152]{2,1,0:T(8,128)(2,1)} collective-permute-done((bf16[2,288,1152]{2,1,0:T(8,128)(2,1)}, bf16[2,288,1152]{2,1,0:T(8,128)(2,1)}, u32[]{:S(2)}, u32[]{:S(2)}) %collective-permute-start.36) | collective-permute-done | bytes 1327136 | tf_op jit(solution)/shard_map/ppermute | solution.py:203
  288.5 14.8 %collective-permute-start.16 = (bf16[4,72,3456]{2,1,0:T(8,128)(2,1)S(1)}, bf16[4,72,3456]{2,1,0:T(8,128)(2,1)S(1)}, u32[]{:S(2)}, u32[]{:S(2)}) collective-permute-start(bf16[4,72,3456]{2,1,0:T(8,128)(2,1)S(1)} %pad_maximum_fusion.7.refs_0_), channel_id=1, source_target_pairs={{0,16},{16,0},{1,17},{17,1},{2,18},{18,2},{3,19},{19,3},{4,20},{20... | collective-permute-start | bytes 5971976 | tf_op jit(solution)/shard_map/ppermute | solution.py:205
  318.8 10.0 place_blocks.7
  329.4 16.2 %collective-permute-done.30.refs_1_ = bf16[4,72,4608]{2,1,0:T(8,128)(2,1)} collective-permute-done((bf16[4,72,4608]{2,1,0:T(8,128)(2,1)}, bf16[4,72,4608]{2,1,0:T(8,128)(2,1)}, u32[]{:S(2)}, u32[]{:S(2)}) %collective-permute-start.30) | collective-permute-done | bytes 2654240 | tf_op jit(solution)/shard_map/ppermute | solution.py:204
  345.6 28.4 %collective-permute-done.37.refs_1_ = bf16[4,288,1152]{2,1,0:T(8,128)(2,1)} collective-permute-done((bf16[4,288,1152]{2,1,0:T(8,128)(2,1)}, bf16[4,288,1152]{2,1,0:T(8,128)(2,1)}, u32[]{:S(2)}, u32[]{:S(2)}) %collective-permute-start.37) | collective-permute-done | bytes 2654240 | tf_op jit(solution)/shard_map/ppermute | solution.py:204
  477.7 10.6 multiply_convert_fusion
  519.6 11.3 %convert_reduce_fusion.3 = (f32[2048]{0:T(1024)}, bf16[4,128,2048]{2,1,0:T(8,128)(2,1)S(1)}) fusion(f32[4,128,2048]{2,1,0:T(8,128)} %get-tuple-element.179, f32[2048]{0:T(1024)S(1)} %get-tuple-element.156, bf16[4,128,2048]{2,1,0:T(8,128)(2,1)S(1)} %get-tuple-element.194, bf16[2048,2048,1]{1,0,2:T(8,128)(2,1)} %bitcast.307), kind=kOutput, calls=%fused_computation.54 | convolution fusion | flops 4308596736 | bytes 16793600 | tf_op jit(solution)/shard_map/...j,ij->...i/dot_general | solution.py:347
  538.7 17.4 %convert_reduce_fusion = (f32[4608]{0:T(1024)S(1)}, bf16[4,128,4608]{2,1,0:T(8,128)(2,1)}) fusion(f32[4,128,4608]{2,1,0:T(8,128)} %get-tuple-element.175, f32[4608]{0:T(1024)S(1)} %add.1189, bf16[4,128,1152]{2,1,0:T(8,128)(2,1)} %get-tuple-element.60, bf16[4608,1152,1]{1,0,2:T(8,128)(2,1)} %bitcast.301), kind=kOutput, calls=%fused_computation.17 | convolution fusion | flops 5490077184 | bytes 25989120 | tf_op jit(solution)/shard_map/...j,ij->...i/dot_general | solution.py:347
  782.7 13.5 %collective-permute-done.67 = bf16[2,4,41728]{2,1,0:T(4,128)(2,1)} collective-permute-done((bf16[2,4,41728]{2,1,0:T(4,128)(2,1)}, bf16[2,4,41728]{2,1,0:T(4,128)(2,1)}, u32[]{:S(2)}, u32[]{:S(2)}) %collective-permute-start.67) | collective-permute-done | bytes 667680 | tf_op jit(solution)/shard_map/ppermute | solution.py:257
  831.8 25.4 %collective-permute-done.72 = f32[2,4,16,4,72]{4,3,2,1,0:T(4,128)S(1)} collective-permute-done((f32[2,4,16,4,72]{4,3,2,1,0:T(4,128)S(1)}, f32[2,4,16,4,72]{4,3,2,1,0:T(4,128)S(1)}, u32[]{:S(2)}, u32[]{:S(2)}) %collective-permute-start.72) | collective-permute-done | bytes 147488 | tf_op jit(solution)/shard_map/ppermute | solution.py:257
  922.8 11.2 %collective-permute-done.118 = bf16[128,2048]{1,0:T(8,128)(2,1)S(1)} collective-permute-done((bf16[128,2048]{1,0:T(8,128)(2,1)S(1)}, bf16[128,2048]{1,0:T(8,128)(2,1)S(1)}, u32[]{:S(2)}, u32[]{:S(2)}) %collective-permute-start.118) | collective-permute-done | bytes 524320 | tf_op jit(solution)/shard_map/ppermute | solution.py:242
  936.3 13.3 %fusion.20 = bf16[576,3456]{1,0:T(8,128)(2,1)S(1)} fusion(bf16[512,3456]{1,0:T(8,128)(2,1)} %collective-permute-done.74, bf16[512,2304]{1,0:T(8,128)(2,1)S(1)} %bitcast.332, bf16[512,1152]{1,0:T(8,128)(2,1)S(1)} %copy-done.88, bf16[512,576]{0,1:T(8,128)(2,1)} %collective-permute-done.73, bf16[512,576]{0,1:T(8,128)(2,1)S(1)} %copy-done.117), kind=kOutput, calls=%fused_computation.33 | convolution fusion | flops 4102447104 | bytes 12238848 | tf_op jit(solution)/shard_map/ni,nj->ij/dot_general | solution.py:227
  956.4 10.8 collective-permute-done.100
  974.9 10.0 collective-permute-done.103
  984.9 13.5 %collective-permute-done.102 = bf16[288,1152]{1,0:T(8,128)(2,1)S(1)} collective-permute-done((bf16[288,1152]{1,0:T(8,128)(2,1)S(1)}, bf16[288,1152]{1,0:T(8,128)(2,1)S(1)}, u32[]{:S(2)}, u32[]{:S(2)}) %collective-permute-start.102) | collective-permute-done | bytes 663584 | tf_op jit(solution)/shard_map/ppermute | solution.py:242
  1050.9 18.3 %collective-permute-done.94 = bf16[72,4608]{1,0:T(8,128)(2,1)S(1)} collective-permute-done((bf16[72,4608]{1,0:T(8,128)(2,1)S(1)}, bf16[72,4608]{1,0:T(8,128)(2,1)S(1)}, u32[]{:S(2)}, u32[]{:S(2)}) %collective-permute-start.94) | collective-permute-done | bytes 663584 | tf_op jit(solution)/shard_map/ppermute | solution.py:242
  1084.3 20.1 %add_multiply_fusion = (f32[2000896]{0:T(1024)}, f32[2000896]{0:T(1024)}, f32[2000896]{0:T(1024)}) fusion(f32[2000896]{0:T(1024)} %param.22, f32[2000896]{0:T(1024)} %param.20, f32[2000896]{0:T(1024)} %constant_dynamic-update-slice_fusion.9, f32[2000896]{0:T(1024)} %param.21), kind=kLoop, calls=%fused_computation.19 | loop fusion | flops 16007168 | bytes 56025088 | tf_op jit(solution)/shard_map/add | solution.py:622
  (901 shorter events, 740.2 us)
Async XLA Ops:
  17.1 52.0 %collective-permute-start.19 = (bf16[72,1152]{1,0:T(8,128)(2,1)}, bf16[72,1152]{1,0:T(8,128)(2,1)}, u32[]{:S(2)}, u32[]{:S(2)}) collective-permute-start(bf16[72,1152]{1,0:T(8,128)(2,1)} %reshape.1262), channel_id=1, source_target_pairs={{0,4},{28,24},{1,5},{29,25},{2,6},{30,26},{3,7},{31,27},{4,0},{24,... | collective-permute-start | bytes 497672 | tf_op jit(solution)/shard_map/ppermute | solution.py:197
  29.9 65.9 %collective-permute-start.40 = (bf16[72,2048]{1,0:T(8,128)(2,1)}, bf16[72,2048]{1,0:T(8,128)(2,1)}, u32[]{:S(2)}, u32[]{:S(2)}) collective-permute-start(bf16[72,2048]{1,0:T(8,128)(2,1)} %slice.431), channel_id=1, source_target_pairs={{0,4},{28,24},{1,5},{29,25},{2,6},{30,26},{3,7},{31,27},{4,0},{24,... | collective-permute-start | bytes 884744 | tf_op jit(solution)/shard_map/ppermute | solution.py:197
  103.3 61.5 %collective-permute-start.26 = (bf16[72,4608]{1,0:T(8,128)(2,1)}, bf16[72,4608]{1,0:T(8,128)(2,1)S(1)}, u32[]{:S(2)}, u32[]{:S(2)}) collective-permute-start(bf16[72,4608]{1,0:T(8,128)(2,1)} %reshape.1263), channel_id=1, source_target_pairs={{0,4},{28,24},{1,5},{29,25},{2,6},{30,26},{3,7},{31,27},{4,0},{24,... | collective-permute-start | bytes 1990664 | tf_op jit(solution)/shard_map/ppermute | solution.py:197
  110.1 56.6 %collective-permute-start.28 = (bf16[72,4608]{1,0:T(8,128)(2,1)S(1)}, bf16[72,4608]{1,0:T(8,128)(2,1)S(1)}, u32[]{:S(2)}, u32[]{:S(2)}) collective-permute-start(bf16[72,4608]{1,0:T(8,128)(2,1)S(1)} %copy-done.115), channel_id=1, source_target_pairs={{0,12},{28,16},{1,13},{29,17},{2,14},{30,18},{3,15},{31,19},{4,8},... | collective-permute-start | bytes 1990664 | tf_op jit(solution)/shard_map/ppermute | solution.py:199
  208.0 51.9 %collective-permute-start.29 = (bf16[2,72,4608]{2,1,0:T(8,128)(2,1)S(1)}, bf16[2,72,4608]{2,1,0:T(8,128)(2,1)S(1)}, u32[]{:S(2)}, u32[]{:S(2)}) collective-permute-start(bf16[2,72,4608]{2,1,0:T(8,128)(2,1)S(1)} %maximum_select_fusion), channel_id=1, source_target_pairs={{0,1},{16,18},{1,0},{17,19},{2,3},{18,16},{3,2},{19,17},{4,5},{20,... | collective-permute-start | bytes 3981320 | tf_op jit(solution)/shard_map/ppermute | solution.py:203
  214.6 73.9 %collective-permute-start.36 = (bf16[2,288,1152]{2,1,0:T(8,128)(2,1)}, bf16[2,288,1152]{2,1,0:T(8,128)(2,1)}, u32[]{:S(2)}, u32[]{:S(2)}) collective-permute-start(bf16[2,288,1152]{2,1,0:T(8,128)(2,1)} %maximum_select_fusion.1), channel_id=1, source_target_pairs={{0,1},{16,18},{1,0},{17,19},{2,3},{18,16},{3,2},{19,17},{4,5},{20,... | collective-permute-start | bytes 3981320 | tf_op jit(solution)/shard_map/ppermute | solution.py:203
  214.6 88.7 %collective-permute-start.44 = (bf16[4,72,2048]{2,1,0:T(8,128)(2,1)S(1)}, bf16[4,72,2048]{2,1,0:T(8,128)(2,1)}, u32[]{:S(2)}, u32[]{:S(2)}) collective-permute-start(bf16[4,72,2048]{2,1,0:T(8,128)(2,1)S(1)} %pad_maximum_fusion.9.refs_0_), channel_id=1, source_target_pairs={{0,2},{16,17},{1,3},{17,16},{2,0},{18,19},{3,1},{19,18},{4,6},{20,... | collective-permute-start | bytes 3538952 | tf_op jit(solution)/shard_map/ppermute | solution.py:204
  231.5 79.3 %collective-permute-start.15 = (bf16[4,72,3456]{2,1,0:T(8,128)(2,1)S(1)}, bf16[4,72,3456]{2,1,0:T(8,128)(2,1)}, u32[]{:S(2)}, u32[]{:S(2)}) collective-permute-start(bf16[4,72,3456]{2,1,0:T(8,128)(2,1)S(1)} %pad_maximum_fusion.7.refs_0_), channel_id=1, source_target_pairs={{0,2},{16,17},{1,3},{17,16},{2,0},{18,19},{3,1},{19,18},{4,6},{20,... | collective-permute-start | bytes 5971976 | tf_op jit(solution)/shard_map/ppermute | solution.py:204
  234.7 74.1 %collective-permute-start.45 = (bf16[4,72,2048]{2,1,0:T(8,128)(2,1)S(1)}, bf16[4,72,2048]{2,1,0:T(8,128)(2,1)}, u32[]{:S(2)}, u32[]{:S(2)}) collective-permute-start(bf16[4,72,2048]{2,1,0:T(8,128)(2,1)S(1)} %pad_maximum_fusion.9.refs_0_), channel_id=1, source_target_pairs={{0,16},{16,0},{1,17},{17,1},{2,18},{18,2},{3,19},{19,3},{4,20},{20... | collective-permute-start | bytes 3538952 | tf_op jit(solution)/shard_map/ppermute | solution.py:205
  261.0 56.2 %collective-permute-start.51 = (bf16[4,128,2048]{2,1,0:T(8,128)(2,1)}, bf16[4,128,2048]{2,1,0:T(8,128)(2,1)}, u32[]{:S(2)}, u32[]{:S(2)}) collective-permute-start(bf16[4,128,2048]{2,1,0:T(8,128)(2,1)} %pad_maximum_fusion.6.refs_0_), channel_id=1, source_target_pairs={{0,2},{16,17},{1,3},{17,16},{2,0},{18,19},{3,1},{19,18},{4,6},{20,... | collective-permute-start | bytes 6291464 | tf_op jit(solution)/shard_map/ppermute | solution.py:204
  309.9 64.2 %collective-permute-start.37 = (bf16[4,288,1152]{2,1,0:T(8,128)(2,1)}, bf16[4,288,1152]{2,1,0:T(8,128)(2,1)}, u32[]{:S(2)}, u32[]{:S(2)}) collective-permute-start(bf16[4,288,1152]{2,1,0:T(8,128)(2,1)} %pad_maximum_fusion.3.refs_0_), channel_id=1, source_target_pairs={{0,2},{16,17},{1,3},{17,16},{2,0},{18,19},{3,1},{19,18},{4,6},{20,... | collective-permute-start | bytes 7962632 | tf_op jit(solution)/shard_map/ppermute | solution.py:204
  317.3 64.5 %collective-permute-start.53 = (bf16[4,128,2048]{2,1,0:T(8,128)(2,1)}, bf16[4,128,2048]{2,1,0:T(8,128)(2,1)S(1)}, u32[]{:S(2)}, u32[]{:S(2)}) collective-permute-start(bf16[4,128,2048]{2,1,0:T(8,128)(2,1)} %collective-permute-done.51.refs_1_), channel_id=1, source_target_pairs={{0,16},{16,0},{1,17},{17,1},{2,18},{18,2},{3,19},{19,3},{4,20},{20... | collective-permute-start | bytes 6291464 | tf_op jit(solution)/shard_map/ppermute | solution.py:206
  328.8 106.6 %collective-permute-start.31 = (bf16[4,72,4608]{2,1,0:T(8,128)(2,1)}, bf16[4,72,4608]{2,1,0:T(8,128)(2,1)}, u32[]{:S(2)}, u32[]{:S(2)}) collective-permute-start(bf16[4,72,4608]{2,1,0:T(8,128)(2,1)} %pad_maximum_fusion.2.refs_0_), channel_id=1, source_target_pairs={{0,16},{16,0},{1,17},{17,1},{2,18},{18,2},{3,19},{19,3},{4,20},{20... | collective-permute-start | bytes 7962632 | tf_op jit(solution)/shard_map/ppermute | solution.py:205
  328.9 115.9 %collective-permute-start.38 = (bf16[4,288,1152]{2,1,0:T(8,128)(2,1)}, bf16[4,288,1152]{2,1,0:T(8,128)(2,1)}, u32[]{:S(2)}, u32[]{:S(2)}) collective-permute-start(bf16[4,288,1152]{2,1,0:T(8,128)(2,1)} %pad_maximum_fusion.3.refs_0_), channel_id=1, source_target_pairs={{0,16},{16,0},{1,17},{17,1},{2,18},{18,2},{3,19},{19,3},{4,20},{20... | collective-permute-start | bytes 7962632 | tf_op jit(solution)/shard_map/ppermute | solution.py:205
  345.6 89.8 %collective-permute-start.32 = (bf16[4,72,4608]{2,1,0:T(8,128)(2,1)}, bf16[4,72,4608]{2,1,0:T(8,128)(2,1)}, u32[]{:S(2)}, u32[]{:S(2)}) collective-permute-start(bf16[4,72,4608]{2,1,0:T(8,128)(2,1)} %collective-permute-done.30.refs_1_), channel_id=1, source_target_pairs={{0,16},{16,0},{1,17},{17,1},{2,18},{18,2},{3,19},{19,3},{4,20},{20... | collective-permute-start | bytes 7962632 | tf_op jit(solution)/shard_map/ppermute | solution.py:206
  374.1 70.8 %collective-permute-start.39 = (bf16[4,288,1152]{2,1,0:T(8,128)(2,1)}, bf16[4,288,1152]{2,1,0:T(8,128)(2,1)}, u32[]{:S(2)}, u32[]{:S(2)}) collective-permute-start(bf16[4,288,1152]{2,1,0:T(8,128)(2,1)} %collective-permute-done.37.refs_1_), channel_id=1, source_target_pairs={{0,16},{16,0},{1,17},{17,1},{2,18},{18,2},{3,19},{19,3},{4,20},{20... | collective-permute-start | bytes 7962632 | tf_op jit(solution)/shard_map/ppermute | solution.py:206
  383.2 71.1 %collective-permute-start.18 = (bf16[4,128,2304]{2,1,0:T(8,128)(2,1)}, bf16[4,128,2304]{2,1,0:T(8,128)(2,1)}, u32[]{:S(2)}, u32[]{:S(2)}) collective-permute-start(bf16[4,128,2304]{2,1,0:T(8,128)(2,1)} %slice.543), channel_id=1, source_target_pairs={{16,0},{0,16},{17,1},{1,17},{18,2},{2,18},{19,3},{3,19},{20,4},{4,... | collective-permute-start | bytes 7077896 | tf_op jit(solution)/shard_map/ppermute | solution.py:31
  625.0 50.5 %collective-permute-start.114 = (bf16[512,2048]{1,0:T(8,128)(2,1)}, bf16[512,2048]{1,0:T(8,128)(2,1)}, u32[]{:S(2)}, u32[]{:S(2)}) collective-permute-start(bf16[512,2048]{1,0:T(8,128)(2,1)} %bitcast.398), channel_id=1, source_target_pairs={{0,16},{16,0},{1,17},{17,1},{2,18},{18,2},{3,19},{19,3},{4,20},{20... | collective-permute-start | bytes 6291464 | tf_op jit(solution)/shard_map/ppermute | solution.py:226
  673.6 217.3 %collective-permute-start.90 = (bf16[512,4608]{1,0:T(8,128)(2,1)}, bf16[512,4608]{1,0:T(8,128)(2,1)}, u32[]{:S(2)}, u32[]{:S(2)}) collective-permute-start(bf16[512,4608]{1,0:T(8,128)(2,1)} %bitcast.394), channel_id=1, source_target_pairs={{0,16},{16,0},{1,17},{17,1},{2,18},{18,2},{3,19},{19,3},{4,20},{20... | collective-permute-start | bytes 14155784 | tf_op jit(solution)/shard_map/ppermute | solution.py:226
  713.4 66.5 %collective-permute-start.107 = (bf16[4,72,2048]{2,1,0:T(8,128)(2,1)}, bf16[4,72,2048]{2,1,0:T(8,128)(2,1)}, u32[]{:S(2)}, u32[]{:S(2)}) collective-permute-start(bf16[4,72,2048]{2,1,0:T(8,128)(2,1)} %get-tuple-element.34), channel_id=1, source_target_pairs={{0,2},{16,17},{1,3},{17,16},{2,0},{18,19},{3,1},{19,18},{4,6},{20,... | collective-permute-start | bytes 3538952 | tf_op jit(solution)/shard_map/ppermute | solution.py:235
  762.7 115.5 %collective-permute-start.115 = (bf16[4,128,2048]{2,1,0:T(8,128)(2,1)}, bf16[4,128,2048]{2,1,0:T(8,128)(2,1)}, u32[]{:S(2)}, u32[]{:S(2)}) collective-permute-start(bf16[4,128,2048]{2,1,0:T(8,128)(2,1)} %get-tuple-element.36), channel_id=1, source_target_pairs={{0,2},{16,17},{1,3},{17,16},{2,0},{18,19},{3,1},{19,18},{4,6},{20,... | collective-permute-start | bytes 6291464 | tf_op jit(solution)/shard_map/ppermute | solution.py:235
  815.9 94.0 %collective-permute-start.99 = (bf16[4,288,1152]{2,1,0:T(8,128)(2,1)}, bf16[4,288,1152]{2,1,0:T(8,128)(2,1)}, u32[]{:S(2)}, u32[]{:S(2)}) collective-permute-start(bf16[4,288,1152]{2,1,0:T(8,128)(2,1)} %copy-done.38), channel_id=1, source_target_pairs={{0,2},{16,17},{1,3},{17,16},{2,0},{18,19},{3,1},{19,18},{4,6},{20,... | collective-permute-start | bytes 7962632 | tf_op jit(solution)/shard_map/ppermute | solution.py:235
  878.2 58.0 %collective-permute-start.74 = (bf16[512,3456]{1,0:T(8,128)(2,1)}, bf16[512,3456]{1,0:T(8,128)(2,1)}, u32[]{:S(2)}, u32[]{:S(2)}) collective-permute-start(bf16[512,3456]{1,0:T(8,128)(2,1)} %pad_maximum_fusion.1), channel_id=1, source_target_pairs={{0,16},{16,0},{1,17},{17,1},{2,18},{18,2},{3,19},{19,3},{4,20},{20... | collective-permute-start | bytes 10616840 | tf_op jit(solution)/shard_map/ppermute | solution.py:226
  934.0 67.2 %collective-permute-start.91 = (bf16[4,72,4608]{2,1,0:T(8,128)(2,1)S(1)}, bf16[4,72,4608]{2,1,0:T(8,128)(2,1)S(1)}, u32[]{:S(2)}, u32[]{:S(2)}) collective-permute-start(bf16[4,72,4608]{2,1,0:T(8,128)(2,1)S(1)} %get-tuple-element.30), channel_id=1, source_target_pairs={{0,2},{16,17},{1,3},{17,16},{2,0},{18,19},{3,1},{19,18},{4,6},{20,... | collective-permute-start | bytes 7962632 | tf_op jit(solution)/shard_map/ppermute | solution.py:235
  (278 other events, 4169.4 us)

commit v3 on v2

v3 whole, which is shorter than its diff:
```python
import functools
import math

import jax
import jax.numpy as jnp
from jax import lax
from jax.experimental import pallas as pl
from jax.experimental.pallas import tpu as pltpu
from jax.sharding import PartitionSpec as P

E = 72
D = 1152
FF = 4608
PH = 2048
ZD = 768


LAMBDA_REPA = 0.5
MOMENTUM = 0.5
AVERAGE = 0.5
LR_COEF = 0.04
BIAS_FACTOR = 4.0
EPS_NORM = 1e-06
GROUP = ("inner", "outer")
EVERY = ("blk", "inner", "outer")
LOW = jnp.bfloat16


def passed_along(block, axis, distance):
    devices = range(lax.axis_size(axis))
    route = [((i - distance) % len(devices), i) for i in devices]
    return lax.ppermute(block, axis, route)


def mat_shapes():
    return [(D, 3 * D), (D, D), (D, FF), (FF, D), (D, 6 * D), (D, PH), (PH, PH), (PH, ZD)]


def bias_shapes():
    return [(D,), (D,), (D,), (FF,), (D,), (6 * D,), (PH,), (PH,), (ZD,)]


def split_shard(flat_vec, shapes, blocks):
    segments = []
    offset = 0
    for shape_now in shapes:
        rows_here = shape_now[0] // blocks
        length = rows_here * math.prod(shape_now[1:])
        segments.append(
            flat_vec[offset : offset + length].reshape((rows_here,) + tuple(shape_now[1:]))
        )
        offset += length
    return segments


def unpack_rows(line_grid, shapes):
    blocks = line_grid.shape[0]
    segments = []
    offset = 0
    for shape_now in shapes:
        length = shape_now[0] // blocks * math.prod(shape_now[1:])
        segments.append(line_grid[:, offset : offset + length].reshape(shape_now))
        offset += length
    return segments


def flat_id(core, z_at, outer_at):
    return (core * 4 + z_at) * 4 + outer_at


def route_z(pairs_core0):
    route = []
    for z_from, z_to in pairs_core0:
        for outer_at in range(4):
            route.append((flat_id(0, z_from, outer_at), flat_id(0, z_to, outer_at)))
            route.append((flat_id(1, 3 - z_from, outer_at), flat_id(1, 3 - z_to, outer_at)))
    return route


def flipped(route):
    return [(target, source) for source, target in route]


def route_xy(step_core0, step_core1):
    route = []
    for z_at in range(4):
        for outer_at in range(4):
            for core, step in ((0, step_core0), (1, step_core1)):
                route.append((flat_id(core, z_at, outer_at), flat_id(core, z_at, outer_at ^ step)))
    return route


STEP_X, STEP_Y = 1, 2
NEAR_FIRST = route_xy(STEP_X, STEP_Y)
NEAR_SECOND = route_xy(STEP_Y, STEP_X)
Z_PAIR = [(0, 1), (1, 0), (2, 3), (3, 2)]
Z_STRAIGHT = route_z([(0, 2), (1, 3)])
SWAP = [(0, 1), (1, 0)]
UP = [(0, 1), (1, 2), (2, 3), (3, 0)]
DOWN = [(1, 0), (2, 1), (3, 2), (0, 3)]
ACROSS = [(0, 2), (2, 0), (1, 3), (3, 1)]
OUT_X = [(0, 1), (1, 0), (2, 3), (3, 2)]
OUT_Y = [(0, 2), (2, 0), (1, 3), (3, 1)]
OUT_XY = [(0, 3), (3, 0), (1, 2), (2, 1)]


def after(value, *others):
    return lax.optimization_barrier((value,) + others)[0]


def columns_of(widths):
    found, start = [], 0
    for width in widths:
        found.append((start, width))
        start += width
    return found


def move_blocks(table, sources, outs, plan, name):
    rows = sources[0].shape[1]
    low = sources[0].dtype
    widths = [columns[1] for _, _, columns, _, _, _ in plan]
    total = sum(widths)

    def kernel(table_ref, *refs):
        source_refs = refs[: len(sources)]
        out_refs = refs[len(sources) : len(sources) + len(outs)]
        held, sems_in, sems_out = refs[len(sources) + len(outs) :]
        arriving, leaving = [], []
        start = 0
        for number, (source_at, index, columns, out_at, out_index, out_columns) in enumerate(plan):
            from_row = table_ref[number] if index is None else index
            to_row = table_ref[number] if out_index is None else out_index
            here = held.at[:, pl.ds(start, columns[1])]
            start += columns[1]
            arriving.append(
                pltpu.make_async_copy(
                    source_refs[source_at].at[from_row, :, pl.ds(*columns)],
                    here,
                    sems_in.at[number],
                )
            )
            leaving.append(
                pltpu.make_async_copy(
                    here,
                    out_refs[out_at].at[to_row, :, pl.ds(*out_columns)],
                    sems_out.at[number],
                )
            )
        for copy in arriving:
            copy.start()
        for copy_in, copy_out in zip(arriving, leaving):
            copy_in.wait()
            copy_out.start()
        for copy in leaving:
            copy.wait()

    count = len(plan)
    return pl.pallas_call(
        kernel,
        out_shape=[jax.ShapeDtypeStruct((length, rows, width), low) for length, width in outs],
        grid_spec=pltpu.PrefetchScalarGridSpec(
            num_scalar_prefetch=1,
            grid=(1,),
            in_specs=[pl.BlockSpec(memory_space=pl.ANY)] * len(sources),
            out_specs=[pl.BlockSpec(memory_space=pl.ANY)] * len(outs),
            scratch_shapes=[
                pltpu.VMEM((rows, total), low),
                pltpu.SemaphoreType.DMA((count,)),
                pltpu.SemaphoreType.DMA((count,)),
            ],
        ),
        compiler_params=pltpu.CompilerParams(vmem_limit_bytes=32 * 1024 * 1024),
        name=name,
    )(table, *sources)


def updated(grad, weight, momentum, average, rate):
    momentum = MOMENTUM * momentum + grad
    weight = weight - rate * (grad + MOMENTUM * momentum)
    return momentum, weight, weight.astype(LOW), AVERAGE * average + (1.0 - AVERAGE) * weight


def update_rows(pieces, state, at, rate, results):
    counts = [grad.shape[0] * width // 128 for grad, _, width in pieces]
    count = sum(counts)
    chunk = 144 if count % 144 == 0 else 128
    total = state[0].shape[0]
    given = [] if results is None else list(results)
    number_of = len(pieces)

    def kernel(*refs):
        grad_refs = refs[:number_of]
        weight_ref, momentum_ref, average_ref = refs[number_of : number_of + 3]
        refs = refs[number_of + 3 + len(given) :]
        outs, arrived = refs[:4], refs[4 : 4 + number_of]
        grad_flat, weight, momentum, average, low, sems = refs[4 + number_of :]
        window = pl.ds(at, count)
        fetched = [
            pltpu.make_async_copy(grad_ref.at[:, pl.ds(start, width)], held, sems.at[3 + number])
            for number, (grad_ref, held, (_, start, width)) in enumerate(
                zip(grad_refs, arrived, pieces)
            )
        ]
        copies = [
            pltpu.make_async_copy(weight_ref.at[window], weight, sems.at[0]),
            pltpu.make_async_copy(momentum_ref.at[window], momentum, sems.at[1]),
            pltpu.make_async_copy(average_ref.at[window], average, sems.at[2]),
        ]
        for copy in fetched + copies:
            copy.start()
        offset = 0
        for copy, held, (grad, _, width) in zip(fetched, arrived, pieces):
            copy.wait()
            rows, per_row = grad.shape[0], width // 128
            for at_now in range(per_row):
                grad_flat[pl.ds(offset + at_now, rows, stride=per_row), :] = held[
                    :, pl.ds(at_now * 128, 128)
                ].astype(jnp.float32)
            offset += rows * per_row
        for copy in copies:
            copy.wait()

        def step(number, carry):
            here = pl.ds(pl.multiple_of(number * chunk, 16), chunk)
            momentum[here], weight[here], low[here], average[here] = updated(
                grad_flat[here], weight[here], momentum[here], average[here], rate
            )
            return carry

        lax.fori_loop(0, count // chunk, step, 0)
        copies = [
            pltpu.make_async_copy(held, out.at[window], sems.at[number])
            for number, (held, out) in enumerate(zip((momentum, weight, low, average), outs))
        ]
        for copy in copies:
            copy.start()
        for copy in copies:
            copy.wait()

    flat = pltpu.VMEM((count, 128), jnp.float32)
    return pl.pallas_call(
        kernel,
        in_specs=[pl.BlockSpec(memory_space=pl.ANY)] * number_of
        + [pl.BlockSpec(memory_space=pltpu.HBM)] * (3 + len(given)),
        out_specs=[pl.BlockSpec(memory_space=pltpu.HBM)] * 4,
        out_shape=[
            jax.ShapeDtypeStruct((total, 128), kind)
            for kind in (jnp.float32, jnp.float32, LOW, jnp.float32)
        ],
        input_output_aliases={number_of + 3 + number: number for number in range(len(given))},
        scratch_shapes=[
            pltpu.VMEM((grad.shape[0], width), grad.dtype) for grad, _, width in pieces
        ]
        + [flat, flat, flat, flat, pltpu.VMEM((count, 128), LOW)]
        + [pltpu.SemaphoreType.DMA((3 + max(number_of, 1),))],
        compiler_params=pltpu.CompilerParams(vmem_limit_bytes=57 * 1024 * 1024),
        name="update_rows",
    )(*[grad for grad, _, _ in pieces], *state, *given)


def place_blocks(sources, table, widths):
    plan, places = [], []
    for out_at, columns in enumerate(columns_of(widths)):
        number = 0
        for source_at, source in enumerate(sources):
            for at in range(source.shape[0]):
                plan.append((source_at, at, columns, out_at, None, (0, columns[1])))
                places.append(table[number])
                number += 1
    outs = [(16, width) for width in widths]
    return move_blocks(jnp.stack(places).astype(jnp.int32), sources, outs, plan, "place_blocks")


def pick_blocks(sources, table):
    widths = [source.shape[-1] for source in sources]
    plan, places = [], []
    for number in range(8):
        for source_at, columns in enumerate(columns_of(widths)):
            plan.append(
                (source_at, None, (0, columns[1]), number // 4, number % 4, columns)
            )
            places.append(table[number])
    outs = [(4, sum(widths)), (4, sum(widths))]
    return move_blocks(jnp.stack(places).astype(jnp.int32), sources, outs, plan, "pick_blocks")


class Staged:
    def __init__(self):
        self.core = lax.axis_index("blk")
        self.z_at = lax.axis_index("inner")
        outer_at = lax.axis_index("outer")
        self.y_at = outer_at // 2
        self.x_at = outer_at % 2
        self.own_half = (self.z_at // 2) == self.core
        self.own_row = self.z_at * 4 + outer_at

    def z_pair(self, core):
        low_bit = self.z_at % 2
        return 2 * core + low_bit, 2 * core + 1 - low_bit

    def near_order(self, core, picks):
        found = []
        for far, near in picks:
            first = jnp.where(core == 0, self.x_at, self.y_at) ^ near
            second = jnp.where(core == 0, self.y_at, self.x_at) ^ far
            y_now = jnp.where(core == 0, second, first)
            x_now = jnp.where(core == 0, first, second)
            found.append(y_now * 2 + x_now)
        return found

    def gather_groups(self, groups, gates, early):
        packed = [
            group[0] if len(group) == 1 else jnp.concatenate(group, axis=1) for group in groups
        ]
        table = []
        for core in (self.core, 1 - self.core):
            for outer_at in self.near_order(core, [(0, 0), (0, 1), (1, 0), (1, 1)]):
                for z_now in self.z_pair(core):
                    table.append(z_now * 4 + outer_at)
        last = len(groups) - 1
        held, others, twos, fours, tokens = {}, {}, {}, {}, {}

        def first_stage(k, gates, late):
            own = after(packed[k], *gates)
            came = after(lax.ppermute(own, EVERY, Z_STRAIGHT), *late)
            held[k] = jnp.where(self.own_half, own, came)
            others[k] = lax.ppermute(held[k], "inner", Z_PAIR)

        def second_stage(k, late):
            twos[k] = jnp.stack([held[k], after(others[k], *late)])

        def third_stage(k, late):
            came = after(lax.ppermute(twos[k], EVERY, NEAR_FIRST), *late)
            fours[k] = jnp.concatenate([twos[k], came])

        first_stage(0, (), early[0]())
        second_stage(0, early[1]())
        first_stage(1, (held[0],), (twos[0],))
        third_stage(0, early[2](twos[0]))
        second_stage(1, (fours[0],))
        for k in range(len(groups)):
            if k + 1 < last:
                first_stage(k + 2, (twos[k + 1],), ())
            far_four = lax.ppermute(fours[k], EVERY, NEAR_SECOND)
            mate_four = lax.ppermute(fours[k], "blk", SWAP)
            if k < last:
                far_four = after(far_four, twos[k + 1])
            else:
                far_four = after(far_four, tokens[k - 1])
            if k < last:
                third_stage(k + 1, (far_four,))
            mate_far = lax.ppermute(far_four, "blk", SWAP)
            if k < last:
                mate_far = after(mate_far, fours[k + 1])
            sources = [fours[k], far_four, mate_four, mate_far]
            widths = [part.shape[1] for part in groups[k]]
            tokens[k] = gates[k](
                [part.reshape(-1, part.shape[-1]) for part in place_blocks(sources, table, widths)]
            )
            if k + 1 < last:
                second_stage(k + 2, (tokens[k],))

    def share_left(self, left):
        half = left.shape[-1] // 2
        tokens = left.reshape(-1, left.shape[-1])
        keep = lax.dynamic_slice_in_dim(tokens, self.core * half, half, 1)
        give = lax.dynamic_slice_in_dim(tokens, (1 - self.core) * half, half, 1)
        return jnp.concatenate([keep, lax.ppermute(give, "blk", SWAP)])

    def share_right(self, right):
        tokens = right.reshape(-1, right.shape[-1])
        return jnp.concatenate([tokens, lax.ppermute(tokens, "blk", SWAP)])

    def start_grads(self, pairs):
        return StagedGrads(self, pairs)

    def update(self, state, rate, parts):
        lanes = [array.reshape(-1, 128) for array in state]
        sizes = [rows * cols // (16 * 128) for rows, cols in mat_shapes()]
        results = None
        for entries in parts:
            if isinstance(entries[0][0], StagedGrads) and entries[0][0].stage == 3:
                entries[0][0].add(results[0])
            pieces = []
            for part, start, number in entries:
                grad = part.both if isinstance(part, StagedGrads) else part
                pieces.append((grad, start, mat_shapes()[number][1]))
            first = entries[0][2]
            results = update_rows(pieces, lanes, sum(sizes[:first]), rate, results)
        return [result.reshape(-1) for result in results]

    def gather_slots(self, own, between=None):
        four = jnp.concatenate(
            [own] + [lax.ppermute(own, "inner", route) for route in (UP, DOWN, ACROSS)]
        )
        self.token = four
        if between is not None:
            four = after(four, between())
        return jnp.concatenate(
            [four] + [lax.ppermute(four, "outer", route) for route in (OUT_X, OUT_Y, OUT_XY)]
        )

    def swap_slots(self, parts, between):
        parts = parts.reshape((4, 4) + parts.shape[1:])
        four = jnp.stack(
            [parts[0]]
            + [
                lax.ppermute(parts[1 + at], "outer", route)
                for at, route in enumerate((OUT_X, OUT_Y, OUT_XY))
            ]
        )
        four = after(four, between())
        return jnp.stack(
            [four[:, 0]]
            + [
                lax.ppermute(four[:, 1 + at], "inner", route)
                for at, route in enumerate((DOWN, UP, ACROSS))
            ],
        )

    def reduce_slots(self, parts, late):
        parts = parts.reshape((4, 4) + parts.shape[1:])
        four = parts[0]
        for at, route in enumerate((OUT_X, OUT_Y, OUT_XY)):
            four = four + after(lax.ppermute(parts[1 + at], "outer", route), late)
        self.token = four
        total = four[0]
        for at, route in enumerate((DOWN, UP, ACROSS)):
            total = total + lax.ppermute(four[1 + at], "inner", route)
        return total

    def slot_rows(self):
        found = []
        for z_now in range(4):
            away = (z_now - self.z_at) % 4
            z_slot = jnp.where(away == 0, 0, jnp.where(away == 3, 1, jnp.where(away == 1, 2, 3)))
            for outer_now in range(4):
                flip = jnp.bitwise_xor(outer_now, self.y_at * 2 + self.x_at)
                found.append((flip, z_slot))
        return found

    def rows_in_order(self, slots):
        table = [flip * 4 + z_slot for flip, z_slot in self.slot_rows()]
        return jnp.take(slots, jnp.stack(table), axis=0)

    def swapped_in_order(self, came):
        table = []
        for flip, z_slot in self.slot_rows():
            came_at = jnp.where(z_slot == 1, 2, jnp.where(z_slot == 2, 1, z_slot))
            table.append(came_at * 4 + flip)
        return jnp.take(came.reshape(16, -1), jnp.stack(table), axis=0)


class StagedGrads:
    def __init__(self, moves, pairs):
        self.moves = moves
        self.widths = [right.shape[-1] for _, right in pairs]
        blocks = []
        for left, right in pairs:
            grad = jnp.einsum("ni,nj->ij", left, right, preferred_element_type=jnp.float32)
            blocks.append(grad.astype(LOW).reshape(8, -1, grad.shape[-1]))
        low_bit = moves.z_at % 2
        table = []
        for outer_at in moves.near_order(moves.core, [(1, 1), (1, 0), (0, 1), (0, 0)]):
            for z_now in (low_bit, 1 - low_bit):
                table.append(z_now * 4 + outer_at)
        self.give, self.keep = pick_blocks(blocks, table)
        self.token = self.give
        self.stage = 0

    def send(self, *gates):
        self.give = after(self.give, *gates) if gates else self.give
        axes, route = (
            (EVERY, NEAR_SECOND),
            (EVERY, NEAR_FIRST),
            ("inner", Z_PAIR),
            (EVERY, flipped(Z_STRAIGHT)),
        )[self.stage]
        self.came = lax.ppermute(self.give, axes, route)

    def add(self, *late):
        came = after(self.came, *late) if late else self.came
        total = self.keep.astype(jnp.float32) + came.astype(jnp.float32)
        if self.stage == 0:
            self.give = total[:2].astype(LOW)
            self.keep = total[2:].astype(LOW)
        elif self.stage == 1:
            self.give = total[1].astype(LOW)
            self.keep = total[0].astype(LOW)
        else:
            self.give = self.keep = total.astype(LOW)
        if self.stage == 3:
            mate = lax.ppermute(self.give, "blk", SWAP)
            self.both = jnp.where(self.moves.own_half, self.give, mate)
        self.token = self.give
        self.stage += 1


def outer_sum(left_arr, right_arr):
    return jnp.einsum("sni,snj->ij", left_arr, right_arr, preferred_element_type=jnp.float32)


class DirectGrads:
    def __init__(self, pairs):
        self.parts = [outer_sum(left, right).astype(LOW) for left, right in pairs]
        self.token = self.parts[0]

    def send(self, *gates):
        pass

    def add(self, *late):
        pass

    @functools.cached_property
    def result(self):
        found = []
        for grad in self.parts:
            part = lax.psum_scatter(grad, GROUP, scatter_dimension=0, tiled=True)
            found.append(lax.psum(part, "blk").astype(jnp.float32))
        return found


class Direct:
    def __init__(self):
        self.core = lax.axis_index("blk")
        self.own_row = lax.axis_index("inner") * lax.axis_size("outer") + lax.axis_index("outer")

    def gather_groups(self, groups, gates, early):
        early[0]()
        early[1]()
        early[2](groups[0][0])
        for group, gate in zip(groups, gates):
            gate([lax.all_gather(part, GROUP, axis=0, tiled=True) for part in group])

    def share_left(self, left):
        return left

    def share_right(self, right):
        return right

    def start_grads(self, pairs):
        return DirectGrads(pairs)

    def update(self, state, rate, parts):
        found = {}
        for part, start, number in sum(parts, []):
            whole = jnp.concatenate(part.result, axis=1) if isinstance(part, DirectGrads) else part
            found[number] = whole[:, start : start + mat_shapes()[number][1]]
        grad = jnp.concatenate([found[number].reshape(-1) for number in sorted(found)])
        return updated(grad, *state, rate)

    def gather_slots(self, own, between=None):
        self.token = own
        if between is not None:
            between()
        return lax.all_gather(own, GROUP, axis=0, tiled=True)

    def reduce_slots(self, parts, late):
        self.token = parts
        return lax.psum_scatter(parts, GROUP, scatter_dimension=0, tiled=False)

    def swap_slots(self, parts, between):
        between()
        return lax.all_gather(parts, GROUP, axis=0)

    def rows_in_order(self, slots):
        return slots

    def swapped_in_order(self, came):
        mine = lax.dynamic_index_in_dim(came, self.own_row, 1, keepdims=False)
        return mine.reshape(mine.shape[0], -1)


def time_embed(steps_t):
    half_dim = D // 2
    frequency = jnp.exp(-math.log(10000.0) * jnp.arange(half_dim, dtype=jnp.float32) / half_dim)
    angles = steps_t.astype(jnp.float32)[:, None] * frequency[None, :]
    return jnp.concatenate([jnp.cos(angles), jnp.sin(angles)], axis=1)


def modulate(values, scale_v, shift_v):
    center = values - jnp.mean(values, axis=-1, keepdims=True)
    normed = center * lax.rsqrt(jnp.mean(center * center, axis=-1, keepdims=True) + EPS_NORM)
    return normed * (1.0 + scale_v[:, None, :]) + shift_v[:, None, :]


def gelu_tanh(values):
    return jax.nn.gelu(values, approximate=True)


def rms_unit(values):
    return values * lax.rsqrt(jnp.mean(values * values, axis=-1, keepdims=True) + EPS_NORM)


def matmul(left_arr, right_arr):
    return jnp.einsum("...i,ij->...j", left_arr, right_arr, preferred_element_type=jnp.float32)


def matmul_t(left_arr, right_arr):
    return jnp.einsum("...j,ij->...i", left_arr, right_arr, preferred_element_type=jnp.float32)


def column_sum(tensor):
    return jnp.sum(tensor.astype(jnp.float32), axis=(0, 1))


def attention(queries, near_kv, far_kv):
    images, rows, _ = queries.shape
    heads = D // E

    def kernel(q_ref, near_ref, far_ref, out_ref):
        for head in range(heads):
            own = pl.ds(head * E, E)
            other = pl.ds(D + head * E, E)
            q_now = q_ref[0, :, own]
            keys = jnp.concatenate([near_ref[0, :, own], far_ref[0, :, own]], axis=0)
            values = jnp.concatenate([near_ref[0, :, other], far_ref[0, :, other]], axis=0)
            scores = dot_nt(keys, q_now) * E ** (-0.5)
            top = jnp.max(scores, axis=0, keepdims=True)
            weight = jnp.exp(scores - top)
            probs = weight * (1.0 / jnp.sum(weight, axis=0, keepdims=True))
            out_ref[0, :, own] = dot_tn(probs.astype(LOW), values).astype(LOW)

    block = pl.BlockSpec((1, rows, D), lambda i: (i, 0, 0))
    block_kv = pl.BlockSpec((1, rows, 2 * D), lambda i: (i, 0, 0))
    return pl.pallas_call(
        kernel,
        grid=(images,),
        in_specs=[block, block_kv, block_kv],
        out_specs=block,
        out_shape=jax.ShapeDtypeStruct(queries.shape, LOW),
        compiler_params=pltpu.CompilerParams(vmem_limit_bytes=32 * 1024 * 1024),
        name="attention",
    )(queries, near_kv, far_kv)


def attention_grads(queries, near_kv, far_kv, grad_att):
    images, rows, _ = queries.shape
    heads = D // E

    def kernel(q_ref, near_ref, far_ref, grad_ref, dq_ref, dnear_ref, dfar_ref):
        for head in range(heads):
            own = pl.ds(head * E, E)
            other = pl.ds(D + head * E, E)
            q_now = q_ref[0, :, own]
            g_now = grad_ref[0, :, own]
            keys = jnp.concatenate([near_ref[0, :, own], far_ref[0, :, own]], axis=0)
            values = jnp.concatenate([near_ref[0, :, other], far_ref[0, :, other]], axis=0)
            scores = dot_nt(keys, q_now) * E ** (-0.5)
            top = jnp.max(scores, axis=0, keepdims=True)
            weight = jnp.exp(scores - top)
            probs = weight * (1.0 / jnp.sum(weight, axis=0, keepdims=True))
            grad_probs = dot_nt(values, g_now)
            delta = jnp.sum(probs * grad_probs, axis=0, keepdims=True)
            grad_scores = (probs * (grad_probs - delta)).astype(LOW)
            dq_ref[0, :, own] = (dot_tn(grad_scores, keys) * E ** (-0.5)).astype(LOW)
            grad_keys = dot_nn(grad_scores, q_now) * E ** (-0.5)
            grad_values = dot_nn(probs.astype(LOW), g_now)
            dnear_ref[0, :, own] = grad_keys[:rows]
            dnear_ref[0, :, other] = grad_values[:rows]
            dfar_ref[0, :, own] = grad_keys[rows:].astype(LOW)
            dfar_ref[0, :, other] = grad_values[rows:].astype(LOW)

    block = pl.BlockSpec((1, rows, D), lambda i: (i, 0, 0))
    block_kv = pl.BlockSpec((1, rows, 2 * D), lambda i: (i, 0, 0))
    return pl.pallas_call(
        kernel,
        grid=(images,),
        in_specs=[block, block_kv, block_kv, block],
        out_specs=[block, block_kv, block_kv],
        out_shape=[
            jax.ShapeDtypeStruct(queries.shape, LOW),
            jax.ShapeDtypeStruct(near_kv.shape, jnp.float32),
            jax.ShapeDtypeStruct(far_kv.shape, LOW),
        ],
        compiler_params=pltpu.CompilerParams(vmem_limit_bytes=32 * 1024 * 1024),
        name="attention_grads",
    )(queries, near_kv, far_kv, grad_att)


def dot_nn(left, right):
    return lax.dot_general(
        left, right, (((1,), (0,)), ((), ())), preferred_element_type=jnp.float32
    )


def dot_nt(left, right):
    return lax.dot_general(
        left, right, (((1,), (1,)), ((), ())), preferred_element_type=jnp.float32
    )


def dot_tn(left, right):
    return lax.dot_general(
        left, right, (((0,), (0,)), ((), ())), preferred_element_type=jnp.float32
    )


def body(
    hidden,
    labels,
    steps_t,
    live_slots,
    label_table,
    targets,
    cotangent,
    weights,
    weight_momentum,
    weight_average,
    biases,
    bias_momentum,
    bias_average,
):
    n_inner = lax.axis_size("inner")
    n_outer = lax.axis_size("outer")
    blocks = n_inner * n_outer
    slots = hidden.shape[0]
    local_tok = hidden.shape[1]
    moves = Staged() if (n_inner, n_outer) == (4, 4) else Direct()
    p_qkv, p_proj, p_up, p_down, p_ada, p_one, p_two, p_three = split_shard(
        weights.astype(LOW), mat_shapes(), blocks
    )
    bias_low = biases.astype(LOW)
    condition = label_table[labels].astype(jnp.float32) + time_embed(steps_t)
    cond_act, silu_cond = jax.vjp(jax.nn.silu, condition)
    cond_low = cond_act.astype(LOW)
    kept = {}
    rows_d = D // blocks
    half_ada = 3 * D

    def early_gather():
        packed = jnp.concatenate([cond_low, bias_low.reshape(slots, -1)], axis=1)
        kept["packed"] = moves.gather_slots(packed)
        return (moves.token,)

    def early_product():
        packed_all = kept["packed"]
        cond_own = lax.dynamic_slice_in_dim(
            packed_all[:, :D], moves.own_row * rows_d, rows_d, 1
        )
        ada_half = lax.dynamic_slice_in_dim(p_ada, moves.core * half_ada, half_ada, 1)
        mod_part = matmul(cond_own, ada_half).reshape(blocks, slots, half_ada)
        kept.update(cond_own=cond_own, mod_part=mod_part)
        return (mod_part,)

    def early_modulation(gate):
        mod_half = moves.reduce_slots(kept["mod_part"], gate)
        late = moves.token
        mod_mate = lax.ppermute(mod_half, "blk", SWAP)
        bias_all = moves.rows_in_order(kept["packed"][:, D:].reshape(blocks, -1))
        biases_now = unpack_rows(bias_all.astype(jnp.float32), bias_shapes())
        b_ada = biases_now[5]
        kept["biases"] = biases_now
        modulation = (
            jnp.concatenate(
                [
                    jnp.where(moves.core == 0, mod_half, mod_mate),
                    jnp.where(moves.core == 0, mod_mate, mod_half),
                ],
                axis=1,
            )
            + b_ada
        )
        shift_a, scale_a, gate_a, shift_m, scale_m, gate_m = [
            modulation[:, part_idx * D : (part_idx + 1) * D] for part_idx in range(6)
        ]
        hidden_f = hidden.astype(jnp.float32)
        mixed_a, pull_a = jax.vjp(modulate, hidden_f, scale_a, shift_a)
        mixed_a_low = mixed_a.astype(LOW)
        left_qkv = moves.share_left(mixed_a_low)
        kept.update(
            gates=(gate_a, gate_m), scale_m=scale_m, shift_m=shift_m, hidden_f=hidden_f,
            mixed_a_low=mixed_a_low, pull_a=pull_a, left_qkv=left_qkv,
        )
        return (late,)

    def use_first(arrived):
        b_q, b_v = kept["biases"][:2]
        (w_qkv,) = arrived
        qkv_bias = jnp.concatenate([b_q, jnp.zeros((D,), jnp.float32), b_v])
        qkv_low = (matmul(kept["mixed_a_low"], w_qkv) + qkv_bias).astype(LOW)
        near_kv = qkv_low[..., D:]
        far_kv = passed_along(near_kv, "blk", 1)
        kept.update(w_qkv=w_qkv, queries=qkv_low[..., :D], near_kv=near_kv, far_kv=far_kv)
        return far_kv
    def use_second(arrived):
        w_proj, w_one = arrived
        b_proj = kept["biases"][2]
        queries, near_kv, far_kv = kept["queries"], kept["near_kv"], kept["far_kv"]
        queries = after(queries, w_proj)
        att_low = attention(queries, near_kv, far_kv)
        left_proj = moves.share_left(att_low)
        branch_a = matmul(att_low, w_proj) + b_proj
        residual = kept["hidden_f"] + kept["gates"][0][:, None, :] * branch_a
        mixed_m, pull_m = jax.vjp(modulate, residual, kept["scale_m"], kept["shift_m"])
        mixed_m_low = mixed_m.astype(LOW)
        left_up = moves.share_left(mixed_m_low)
        kept.update(
            w_proj=w_proj, w_one=w_one, left_proj=left_proj,
            branch_a=branch_a, residual=residual, pull_m=pull_m, left_up=left_up,
            mixed_m_low=mixed_m_low,
        )
        return mixed_m_low

    def use_third(arrived):
        (w_up,) = arrived
        b_up = kept["biases"][3]
        pre_act = matmul(kept["mixed_m_low"], w_up) + b_up
        activated, gelu_pull = jax.vjp(gelu_tanh, pre_act)
        act_low = activated.astype(LOW)
        left_down = moves.share_left(act_low)
        kept.update(w_up=w_up, gelu_pull=gelu_pull, act_low=act_low, left_down=left_down)
        return act_low

    def use_fourth(arrived):
        (w_down,) = arrived
        b_down, c_one = kept["biases"][4], kept["biases"][6]
        branch_m = matmul(kept["act_low"], w_down) + b_down
        output = kept["residual"] + kept["gates"][1][:, None, :] * branch_m
        out_low = output.astype(LOW)
        left_one = moves.share_left(out_low)
        hid_one = matmul(out_low, kept["w_one"]) + c_one
        act_one, silu_one = jax.vjp(jax.nn.silu, hid_one)
        one_low = act_one.astype(LOW)
        left_two = moves.share_left(one_low)
        kept.update(
            w_down=w_down, branch_m=branch_m, out_low=out_low, left_one=left_one,
            silu_one=silu_one, one_low=one_low, left_two=left_two,
        )
        return one_low

    def use_fifth(arrived):
        w_two, w_three = arrived
        c_two, c_three = kept["biases"][7:]
        hid_two = matmul(kept["one_low"], w_two) + c_two
        act_two, silu_two = jax.vjp(jax.nn.silu, hid_two)
        two_low = act_two.astype(LOW)
        left_three = moves.share_left(two_low)
        projection = matmul(two_low, w_three) + c_three
        kept.update(
            w_two=w_two, w_three=w_three, silu_two=silu_two, left_three=left_three,
            projection=projection,
        )

    moves.gather_groups(
        [[p_qkv], [p_proj, p_one], [p_up], [p_down], [p_two, p_three]],
        [use_first, use_second, use_third, use_fourth, use_fifth],
        [early_gather, early_product, early_modulation],
    )
    w_qkv, w_proj, w_up, w_down, w_one, w_two, w_three = [
        kept[name] for name in ("w_qkv", "w_proj", "w_up", "w_down", "w_one", "w_two", "w_three")
    ]
    gate_a, gate_m = kept["gates"]
    cond_own = kept["cond_own"]
    pull_a, left_qkv = kept["pull_a"], kept["left_qkv"]
    queries, near_kv, far_kv = [kept[name] for name in ("queries", "near_kv", "far_kv")]
    branch_a, branch_m, out_low, projection = [
        kept[name] for name in ("branch_a", "branch_m", "out_low", "projection")
    ]
    pull_m, gelu_pull, silu_one, silu_two = [
        kept[name] for name in ("pull_m", "gelu_pull", "silu_one", "silu_two")
    ]
    live_f = live_slots.astype(jnp.float32)[:, None, None]
    unit_proj, unit_pull = jax.vjp(rms_unit, projection)
    grad_proj = unit_pull(-LAMBDA_REPA * live_f * rms_unit(targets.astype(jnp.float32)))[0].astype(
        LOW
    )
    right_three = moves.share_right(grad_proj)
    grad_cthree = column_sum(grad_proj)
    grad_htwo = silu_two(matmul_t(grad_proj, w_three))[0].astype(LOW)
    right_two = moves.share_right(grad_htwo)
    grad_ctwo = column_sum(grad_htwo)
    grad_hone = silu_one(matmul_t(grad_htwo, w_two))[0].astype(LOW)
    right_one = moves.share_right(grad_hone)
    grads_fourth = moves.start_grads(
        [(kept["left_two"], right_two), (kept["left_three"], right_three)]
    )
    grad_cone = column_sum(grad_hone)
    grads_fourth.send()
    right_one = after(right_one, grads_fourth.token)
    grads_one = moves.start_grads([(kept["left_one"], right_one)])
    grads_one.send()
    grad_hone = after(grad_hone, grads_one.token)
    grad_output = cotangent.astype(jnp.float32) * live_f + matmul_t(grad_hone, w_one)
    grad_gate_m = jnp.sum(grad_output * branch_m, axis=1)
    grad_bm = (gate_m[:, None, :] * grad_output).astype(LOW)
    right_down = moves.share_right(grad_bm)
    grad_bdown = column_sum(grad_bm)
    grad_pre = gelu_pull(matmul_t(grad_bm, w_down))[0].astype(LOW)
    right_up = moves.share_right(grad_pre)
    grads_down = moves.start_grads([(kept["left_down"], right_down)])
    grad_bup = column_sum(grad_pre)
    grads_down.send()
    grads_fourth.add(grads_down.token)
    grads_fourth.send()
    grad_pre = after(grad_pre, grads_down.token, grads_fourth.token)
    grad_res_m, grad_scale_m, grad_shift_m = pull_m(matmul_t(grad_pre, w_up))
    grad_residual = grad_output + grad_res_m
    grad_gate_a = jnp.sum(grad_residual * branch_a, axis=1)
    grad_ba = (gate_a[:, None, :] * grad_residual).astype(LOW)
    right_proj = moves.share_right(grad_ba)
    grad_bproj = column_sum(grad_ba)
    grad_att = matmul_t(grad_ba, w_proj).astype(LOW)
    grads_one.add(grad_att)
    grads_one.send()
    grads_fourth.add(grad_att)
    grads_fourth.send()
    right_up = after(right_up, grads_fourth.token, grads_one.token)
    grads_up = moves.start_grads([(kept["left_up"], right_up), (kept["left_proj"], right_proj)])
    grads_up.send()
    grads_down.add(grads_up.token)
    grads_down.send()
    grads_one.add(grads_up.token)
    grads_one.send()
    grad_att = after(grad_att, grads_up.token, grads_down.token, grads_one.token)
    grad_query, near_dkv, far_dkv = attention_grads(queries, near_kv, far_kv, grad_att)
    home_dkv = passed_along(far_dkv, "blk", -1)
    grads_down.add(grad_query)
    grads_down.send()
    grads_fourth.add(grad_query)
    grads_fourth.send()
    grads_one.add(grad_query)
    grads_one.send()
    home_dkv = after(home_dkv, grads_down.token, grads_one.token, grads_fourth.token)
    grad_kv = (near_dkv + home_dkv.astype(jnp.float32)).astype(LOW)
    grad_qkv = jnp.concatenate([grad_query, grad_kv], axis=-1)
    grads_up.add(grad_kv)
    grads_up.send()
    right_qkv = after(moves.share_right(grad_qkv), grads_up.token)
    grads_first = moves.start_grads([(left_qkv, right_qkv)])
    qkv_sums = column_sum(grad_qkv)
    grads_first.send()
    grads_up.add(grads_first.token)
    grads_up.send()
    grads_down.add(grads_first.token)
    grads_down.send()
    grads_fourth.add(grads_first.token)
    grads_one.add(grads_first.token)
    grad_qkv = after(
        grad_qkv, grads_up.token, grads_down.token, grads_fourth.token, grads_one.token
    )
    grad_hid_a, grad_scale_a, grad_shift_a = pull_a(matmul_t(grad_qkv, w_qkv))
    grad_input = grad_residual + grad_hid_a
    grad_mod_part = jnp.concatenate(
        [grad_shift_a, grad_scale_a, grad_gate_a, grad_shift_m, grad_scale_m, grad_gate_m], axis=1
    )
    bias_terms = (
        qkv_sums[:D],
        qkv_sums[2 * D :],
        grad_bproj,
        grad_bup,
        grad_bdown,
        grad_cone,
        grad_ctwo,
        grad_cthree,
    )
    bias_grid = jnp.concatenate(
        [segment.reshape(blocks, -1) for segment in bias_terms], axis=1
    ).reshape(slots, -1)
    grad_small = jnp.concatenate([grad_mod_part, bias_grid], axis=1)
    small_came = lax.ppermute(grad_small, "blk", SWAP)
    grads_first.add(grad_small)
    grads_first.send()
    grad_small = (grad_small + after(small_came, grads_first.token)).astype(LOW)

    def between_levels():
        grads_up.add(grad_small)
        grads_up.send()
        grads_first.add(moves.token)
        grads_first.send()
        return lax.optimization_barrier((grads_first.token, grads_up.token))[0]

    def between_swaps():
        grads_up.add()
        return grads_up.token

    small_all = moves.gather_slots(grad_small, between_levels)
    grads_first.add()
    grads_first.send()
    small_all = after(small_all, grads_first.token)
    grad_mod = small_all[:, : 6 * D]
    cond_cols = matmul_t(grad_mod, p_ada).reshape(blocks, slots, rows_d)
    cond_rows = moves.swapped_in_order(moves.swap_slots(cond_cols, between_swaps))
    grad_cond = silu_cond(
        cond_rows.reshape(blocks, slots, rows_d).transpose(1, 0, 2).reshape(slots, D)
    )[0]
    grad_wada = jnp.einsum("si,sj->ij", cond_own, grad_mod, preferred_element_type=jnp.float32)
    grad_bada = lax.dynamic_index_in_dim(
        jnp.sum(grad_mod.astype(jnp.float32), axis=0).reshape(blocks, -1),
        moves.own_row,
        0,
        keepdims=False,
    )
    bias_sums = jnp.sum(
        small_all[:, 6 * D :].astype(jnp.float32).reshape(blocks, slots, -1), axis=0
    )
    bias_own = lax.dynamic_index_in_dim(
        bias_sums.reshape(blocks, -1), moves.own_row, 0, keepdims=False
    )
    ada_at = (3 * D + FF + D) // blocks
    grad_b_flat = jnp.concatenate([bias_own[:ada_at], grad_bada, bias_own[ada_at:]])
    grads_down.add(grad_mod_part)
    images_all = slots * blocks
    tokens_img = local_tok * lax.axis_size("blk")
    rate_w = LR_COEF / math.sqrt(images_all * tokens_img)
    rate_b = BIAS_FACTOR * rate_w
    mom_w, new_w, low_w, avg_w = moves.update(
        (weights, weight_momentum, weight_average),
        rate_w,
        [
            [(grads_fourth, 0, 6)],
            [(grads_fourth, PH, 7)],
            [(grads_one, 0, 5)],
            [(grads_down, 0, 3)],
            [(grad_wada, 0, 4)],
            [(grads_up, 0, 2)],
            [(grads_first, 0, 0), (grads_up, FF, 1)],
        ],
    )
    mom_b = MOMENTUM * bias_momentum + grad_b_flat
    new_b = biases - rate_b * (grad_b_flat + MOMENTUM * mom_b)
    avg_b = AVERAGE * bias_average + (1.0 - AVERAGE) * new_b
    return (
        out_low,
        grad_input,
        grad_cond,
        mom_w,
        new_w,
        low_w,
        avg_w,
        mom_b,
        new_b,
        new_b.astype(LOW),
        avg_b,
    )


def solution(mesh):
    in_specs = (
        P(("inner", "outer"), "blk", None),
        P(("inner", "outer")),
        P(("inner", "outer")),
        P(("inner", "outer")),
        P(),
        P(("inner", "outer"), "blk", None),
        P(("inner", "outer"), "blk", None),
        P(("inner", "outer")),
        P(("inner", "outer")),
        P(("inner", "outer")),
        P(("inner", "outer")),
        P(("inner", "outer")),
        P(("inner", "outer")),
    )
    out_specs = (
        P(("inner", "outer"), "blk", None),
        P(("inner", "outer"), "blk", None),
        P(("inner", "outer"), None),
        P(("inner", "outer")),
        P(("inner", "outer")),
        P(("inner", "outer")),
        P(("inner", "outer")),
        P(("inner", "outer")),
        P(("inner", "outer")),
        P(("inner", "outer")),
        P(("inner", "outer")),
    )
    return jax.shard_map(body, mesh=mesh, in_specs=in_specs, out_specs=out_specs, check_vma=False)
```

time: 1120 us -> 770 us (0.69)
  waiting for transfers between devices: 335 us -> 191 us
  starting transfers between devices: 238 us -> 114 us
  local copies, waits for them, and re-layouts: 154 us -> 79.2 us
  Pallas kernels: 69.7 us -> 104 us
  matrix products: 188 us -> 155 us
    ppermute x111 -> x82, waiting for transfers between devices: 330 us -> 191 us  [the longest x20 42.5 us: send(): self.came = lax.ppermute(self.give, axes, route)]
    ppermute x111 -> x82, starting transfers between devices: 213 us -> 98.7 us  [the longest x20 23.1 us: send(): self.came = lax.ppermute(self.give, axes, route)]
    pallas_call x14 -> x19, Pallas kernels: 69.7 us -> 104 us  [the longest x10 36.7 us: move_blocks(): pl.pallas_call(kernel, out_shape=[jax.ShapeDtypeStruct((length, rows, wid...]
    dot_general x19 -> x7, matrix products: 77.9 us -> 43.9 us  [__init__(): jnp.einsum('ni,nj->ij', left, right, preferred_element_type=jnp.float32)]
    concatenate x11 -> x16, other arithmetic: 11.1 us -> 38.7 us  [the longest x3 18.7 us: share_right(): return jnp.concatenate([tokens, lax.ppermute(tokens, 'blk', SWAP)])]
    unnamed x364 -> x254, local copies, waits for them, and re-layouts: 57.2 us -> 30.9 us
    convert_element_type x27 -> x15, other arithmetic: 38.5 us -> 15 us  [the longest x10 9.78 us: add(): self.give = self.keep = total.astype(LOW)]
    reshape x17 -> x6, local copies, waits for them, and re-layouts: 22.4 us -> 0.75 us  [the longest x1 0.27 us: body(): small_all[:, 6 * D:].astype(jnp.float32).reshape(blocks, slots, -1)]
  transfers between devices with their start and end apart: 129 -> 97, of which waited for: 42 -> 31; matrix products, arithmetic and copies ran while one was open for 20% -> 44% of each run, Pallas kernels for 6% -> 13%
where the time goes in v3:
time: 770 us; the launch traced here: 761 us
  waiting for transfers between devices  191 us (25%)
  matrix products  155 us (20%)
  other arithmetic  114 us (15%)
  starting transfers between devices  114 us (15%)
  Pallas kernels  104 us (14%)
  local copies, waits for them, and re-layouts  79.2 us (10%)
    dot_general x8, matrix products, matmul_t(): jnp.einsum('...j,ij->...i', left_arr, right_arr, preferred_element_type=j...  61.9 us
    dot_general x8, matrix products, matmul(): jnp.einsum('...i,ij->...j', left_arr, right_arr, preferred_element_type=j...  46.2 us
    dot_general x7, matrix products, __init__(): jnp.einsum('ni,nj->ij', left, right, preferred_element_type=jnp.float32)  43.9 us
    ppermute x20, waiting for transfers between devices, send(): self.came = lax.ppermute(self.give, axes, route)  42.5 us
    ppermute x5, waiting for transfers between devices, gather_groups(): far_four = lax.ppermute(fours[k], EVERY, NEAR_SECOND)  40.8 us
    ppermute x5, waiting for transfers between devices, first_stage(): others[k] = lax.ppermute(held[k], 'inner', Z_PAIR)  37 us
    pallas_call x10, Pallas kernels, move_blocks(): pl.pallas_call(kernel, out_shape=[jax.ShapeDtypeStruct((length, rows, wid...  36.7 us
    ppermute x5, waiting for transfers between devices, third_stage(): came = after(lax.ppermute(twos[k], EVERY, NEAR_FIRST), *late)  35.6 us
  transfers between devices with their start and end apart: 97, of which 31 were waited for; matrix products, arithmetic and copies ran while one was open for 44% of the time, Pallas kernels for 13%

profile of v3, /device:TPU:0, one launch (start us, length us, event | category | flops | bytes accessed | tf_op | source)
XLA Modules:
  0.0 760.6 jit_solution(1664834797502755118)
XLA Ops:
  51.4 9.1 %collective-permute-done.8 = bf16[72,3456]{1,0:T(8,128)(2,1)S(1)} collective-permute-done((bf16[72,3456]{1,0:T(8,128)(2,1)S(1)}, bf16[72,3456]{1,0:T(8,128)(2,1)S(1)}, u32[]{:S(2)}, u32[]{:S(2)}) %collective-permute-start.8) | collective-permute-done | bytes 497696 | tf_op jit(solution)/shard_map/ppermute | solution.py:328
  79.4 8.8 %collective-permute-done.18 = bf16[72,3200]{1,0:T(8,128)(2,1)S(1)} collective-permute-done((bf16[72,3200]{1,0:T(8,128)(2,1)S(1)}, bf16[72,3200]{1,0:T(8,128)(2,1)S(1)}, u32[]{:S(2)}, u32[]{:S(2)}) %collective-permute-start.18) | collective-permute-done | bytes 460832 | tf_op jit(solution)/shard_map/ppermute | solution.py:328
  88.3 14.2 %collective-permute-done.16.refs_1_ = bf16[4,72,3456]{2,1,0:T(8,128)(2,1)S(1)} collective-permute-done((bf16[4,72,3456]{2,1,0:T(8,128)(2,1)S(1)}, bf16[4,72,3456]{2,1,0:T(8,128)(2,1)S(1)}, u32[]{:S(2)}, u32[]{:S(2)}) %collective-permute-start.16) | collective-permute-done | bytes 1990688 | tf_op jit(solution)/shard_map/ppermute | solution.py:345
  129.9 14.6 %collective-permute-done.24 = bf16[72,4608]{1,0:T(8,128)(2,1)S(1)} collective-permute-done((bf16[72,4608]{1,0:T(8,128)(2,1)S(1)}, bf16[72,4608]{1,0:T(8,128)(2,1)S(1)}, u32[]{:S(2)}, u32[]{:S(2)}) %collective-permute-start.24) | collective-permute-done | bytes 663584 | tf_op jit(solution)/shard_map/ppermute | solution.py:328
  173.8 14.2 %attention.1 = bf16[4,128,1152]{2,1,0:T(8,128)(2,1)S(1)} custom-call(bf16[4,128,1152]{2,1,0:T(8,128)(2,1)S(1)} %slice.379.q_ref, bf16[4,128,2304]{2,1,0:T(8,128)(2,1)S(1)} %slice.380.near_ref, bf16[4,128,2304]{2,1,0:T(8,128)(2,1)S(1)} %copy-done.7), custom_call_target="tpu_custom_call" | custom-call | tf_op jit(solution)/shard_map/attention/pallas_call | solution.py:627
  241.0 10.6 %multiply_convert_fusion = (bf16[4,128,4608]{2,1,0:T(8,128)(2,1)}, f32[4,128,4608]{2,1,0:T(8,128)}) fusion(f32[4608]{0:T(1024)S(1)} %add.765, bf16[4,128,1152]{2,1,0:T(8,128)(2,1)S(1)} %copy-done.37, bf16[1152,4608,1]{1,0,2:T(8,128)(2,1)S(1)} %bitcast.264), kind=kOutput, calls=%fused_computation.15 | convolution fusion | flops 5459410944 | bytes 25970688 | tf_op jit(solution)/shard_map/...i,ij->...j/dot_general | solution.py:597
  252.3 9.2 %collective-permute-done.35.refs_1_ = bf16[4,288,1152]{2,1,0:T(8,128)(2,1)} collective-permute-done((bf16[4,288,1152]{2,1,0:T(8,128)(2,1)}, bf16[4,288,1152]{2,1,0:T(8,128)(2,1)}, u32[]{:S(2)}, u32[]{:S(2)}) %collective-permute-start.35) | collective-permute-done | bytes 2654240 | tf_op jit(solution)/shard_map/ppermute | solution.py:345
  267.5 17.3 %collective-permute-done.40 = bf16[2,128,2816]{2,1,0:T(8,128)(2,1)S(1)} collective-permute-done((bf16[2,128,2816]{2,1,0:T(8,128)(2,1)S(1)}, bf16[2,128,2816]{2,1,0:T(8,128)(2,1)S(1)}, u32[]{:S(2)}, u32[]{:S(2)}) %collective-permute-start.40) | collective-permute-done | bytes 1441824 | tf_op jit(solution)/shard_map/ppermute | solution.py:334
  293.9 11.3 %add_convert_fusion.10 = (bf16[4,128,1152]{2,1,0:T(8,128)(2,1)S(1)}, f32[4,128,1152]{2,1,0:T(8,128)}) fusion(f32[4,128,1152]{2,1,0:T(8,128)S(1)} %copy-done.22, f32[4,1152]{1,0:T(4,128)S(1)} %copy-done.95, f32[1152]{0:T(1024)S(1)} %add.770, bf16[4,128,4608]{2,1,0:T(8,128)(2,1)} %get-tuple-element.287, bf16[4608,1152,1]{1,0,2:T(8,128)(2,1)S(1)} %bitcast.268), kind=kOutput, calls=%fused_computation.96 | convolution fusion | flops 5438177280 | bytes 21256704 | tf_op jit(solution)/shard_map/...i,ij->...j/dot_general | solution.py:597
  310.6 10.8 %collective-permute-done.41.refs_1_ = bf16[4,128,2816]{2,1,0:T(8,128)(2,1)} collective-permute-done((bf16[4,128,2816]{2,1,0:T(8,128)(2,1)}, bf16[4,128,2816]{2,1,0:T(8,128)(2,1)}, u32[]{:S(2)}, u32[]{:S(2)}) %collective-permute-start.41) | collective-permute-done | bytes 2883616 | tf_op jit(solution)/shard_map/ppermute | solution.py:345
  327.0 8.4 %place_blocks.9 = (bf16[16,128,2048]{2,1,0:T(8,128)(2,1)}, bf16[16,128,768]{2,1,0:T(8,128)(2,1)S(1)}) custom-call(s32[32]{0:T(128)S(1)} %stack.530.table_ref, bf16[4,128,2816]{2,1,0:T(8,128)(2,1)} %pad_maximum_fusion.4.refs_0_, bf16[4,128,2816]{2,1,0:T(8,128)(2,1)} %collective-permute-done.41.refs_1_, bf16[4,128,2816]{2,1,0:T(8,128)(2,1)} %collective-permute-done.42.refs_2_, ...), custom_call_target="tpu_custom_call" | custom-call | tf_op jit(solution)/shard_map/place_blocks/pallas_call | solution.py:159
  335.4 7.7 %multiply_convert_fusion.1 = (bf16[4,128,2048]{2,1,0:T(8,128)(2,1)S(1)}, f32[4,128,2048]{2,1,0:T(8,128)S(1)}) fusion(f32[2048]{0:T(1024)S(1)} %get-tuple-element.267, bf16[4,128,2048]{2,1,0:T(8,128)(2,1)S(1)} %copy-done.47, bf16[2048,2048,1]{1,0,2:T(8,128)(2,1)} %bitcast.365), kind=kOutput, calls=%fused_computation.43 | convolution fusion | flops 4301258752 | bytes 16785408 | tf_op jit(solution)/shard_map/...i,ij->...j/dot_general | solution.py:597
  355.2 10.0 %convert_reduce_fusion.3 = (f32[2048]{0:T(1024)}, bf16[4,128,2048]{2,1,0:T(8,128)(2,1)}) fusion(f32[4,128,2048]{2,1,0:T(8,128)} %get-tuple-element.292, f32[2048]{0:T(1024)S(1)} %get-tuple-element.268, bf16[4,128,2048]{2,1,0:T(8,128)(2,1)} %get-tuple-element.306, bf16[2048,2048,1]{1,0,2:T(8,128)(2,1)S(1)} %bitcast.368), kind=kOutput, calls=%fused_computation.42 | convolution fusion | flops 4308596736 | bytes 16793600 | tf_op jit(solution)/shard_map/...j,ij->...i/dot_general | solution.py:601
  405.0 17.8 %convert_reduce_fusion = (f32[4608]{0:T(1024)}, bf16[4,128,4608]{2,1,0:T(8,128)(2,1)}) fusion(f32[4,128,4608]{2,1,0:T(8,128)} %get-tuple-element.288, f32[4608]{0:T(1024)S(1)} %copy-done.90, bf16[4,128,1152]{2,1,0:T(8,128)(2,1)} %get-tuple-element.227, bf16[4608,1152,1]{1,0,2:T(8,128)(2,1)} %bitcast.269), kind=kOutput, calls=%fused_computation.14 | convolution fusion | flops 5490077184 | bytes 25989120 | tf_op jit(solution)/shard_map/...j,ij->...i/dot_general | solution.py:601
  424.7 9.1 %convolution_convert_fusion = bf16[2304,1152]{1,0:T(8,128)(2,1)S(1)} fusion(bf16[512,2304]{1,0:T(8,128)(2,1)} %copy-done.102, bf16[512,2304]{1,0:T(8,128)(2,1)} %get-tuple-element.233, bf16[512,1152]{1,0:T(8,128)(2,1)} %collective-permute-done.51, bf16[512,1152]{1,0:T(8,128)(2,1)} %bitcast.98), kind=kOutput, calls=%fused_computation.5 | convolution fusion | flops 5452627968 | bytes 12386304 | tf_op jit(solution)/shard_map/ni,nj->ij/dot_general | solution.py:461
  444.0 9.6 %multiply_reduce_fusion.3 = (f32[4,128]{1,0:T(4,128)S(1)}, f32[4,128,1152]{2,1,0:T(8,128)}) fusion(f32[4,128,1152]{2,1,0:T(8,128)} %copy-done.21, f32[4,1152]{1,0:T(4,128)S(1)} %copy-done.61, f32[4,128]{1,0:T(4,128)S(1)} %copy-done.79, bf16[4,128,4608]{2,1,0:T(8,128)(2,1)} %get-tuple-element.151, bf16[1152,4608,1]{1,0,2:T(8,128)(2,1)S(1)} %bitcast.267), kind=kOutput, calls=%fused_computation.94 | convolution fusion | flops 5438176768 | bytes 20076544 | tf_op jit(solution)/shard_map/...j,ij->...i/dot_general | solution.py:601
  491.2 9.4 %pad_maximum_fusion = bf16[1024,4608]{1,0:T(8,128)(2,1)} fusion(bf16[512,4608]{1,0:T(8,128)(2,1)} %collective-permute-done.54, bf16[512,4608]{1,0:T(8,128)(2,1)S(1)} %bitcast.331), kind=kLoop, calls=%fused_computation.13 | loop fusion | flops 18874368 | bytes 18874368 | tf_op jit(solution)/shard_map/concatenate | solution.py:373
  500.6 9.6 %convolution_convert_fusion.1 = bf16[576,4608]{1,0:T(8,128)(2,1)S(1)} fusion(bf16[1024,4608]{1,0:T(8,128)(2,1)} %pad_maximum_fusion, bf16[512,576]{0,1:T(8,128)(2,1)S(1)} %collective-permute-done.53, bf16[512,576]{0,1:T(8,128)(2,1)S(1)} %copy-done.54), kind=kOutput, calls=%fused_computation.16 | convolution fusion | flops 5440831488 | bytes 15925248 | tf_op jit(solution)/shard_map/ni,nj->ij/dot_general | solution.py:461
  513.4 7.6 collective-permute-done.59
  526.4 21.1 %attention_grads.1 = (bf16[4,128,1152]{2,1,0:T(8,128)(2,1)S(1)}, f32[4,128,2304]{2,1,0:T(8,128)S(1)}, bf16[4,128,2304]{2,1,0:T(8,128)(2,1)S(1)}) custom-call(bf16[4,128,1152]{2,1,0:T(8,128)(2,1)S(1)} %copy-done.3, bf16[4,128,2304]{2,1,0:T(8,128)(2,1)S(1)} %slice.380.near_ref, bf16[4,128,2304]{2,1,0:T(8,128)(2,1)S(1)} %copy-done.8, ...), custom_call_target="tpu_custom_call" | custom-call | tf_op jit(solution)/shard_map/attention_grads/pallas_call | solution.py:667
  571.4 15.7 %collective-permute-done.65 = bf16[4,72,5760]{2,1,0:T(8,128)(2,1)} collective-permute-done((bf16[4,72,5760]{2,1,0:T(8,128)(2,1)}, bf16[4,72,5760]{2,1,0:T(8,128)(2,1)}, u32[]{:S(2)}, u32[]{:S(2)}) %collective-permute-start.65) | collective-permute-done | bytes 3317792 | tf_op jit(solution)/shard_map/ppermute | solution.py:480
  601.1 7.7 %convolution_convert_fusion.2 = bf16[576,3456]{1,0:T(8,128)(2,1)S(1)} fusion(bf16[1024,3456]{1,0:T(8,128)(2,1)} %pad_maximum_fusion.1, bf16[512,576]{0,1:T(8,128)(2,1)} %collective-permute-done.67, bf16[512,576]{0,1:T(8,128)(2,1)S(1)} %copy-done.53), kind=kOutput, calls=%fused_computation.23 | convolution fusion | flops 4081213440 | bytes 12238848 | tf_op jit(solution)/shard_map/ni,nj->ij/dot_general | solution.py:461
  682.7 17.1 %collective-permute-done.79 = bf16[16,10432]{1,0:T(8,128)(2,1)S(1)} collective-permute-done((bf16[16,10432]{1,0:T(8,128)(2,1)S(1)}, bf16[16,10432]{1,0:T(8,128)(2,1)S(1)}, u32[]{:S(2)}, u32[]{:S(2)}) %collective-permute-start.79) | collective-permute-done | bytes 333856 | tf_op jit(solution)/shard_map/ppermute | solution.py:401
  705.8 11.0 %collective-permute-done.81 = bf16[72,3456]{1,0:T(8,128)(2,1)S(1)} collective-permute-done((bf16[72,3456]{1,0:T(8,128)(2,1)S(1)}, bf16[72,3456]{1,0:T(8,128)(2,1)S(1)}, u32[]{:S(2)}, u32[]{:S(2)}) %collective-permute-start.81) | collective-permute-done | bytes 497696 | tf_op jit(solution)/shard_map/ppermute | solution.py:480
  (675 shorter events, 475.3 us)
Async XLA Ops:
  79.3 38.2 %collective-permute-start.19 = (bf16[4,72,3456]{2,1,0:T(8,128)(2,1)S(1)}, bf16[4,72,3456]{2,1,0:T(8,128)(2,1)S(1)}, u32[]{:S(2)}, u32[]{:S(2)}) collective-permute-start(bf16[4,72,3456]{2,1,0:T(8,128)(2,1)S(1)} %pad_maximum_fusion.7.refs_0_), channel_id=1, source_target_pairs={{0,16},{16,0},{1,17},{17,1},{2,18},{18,2},{3,19},{19,3},{4,20},{20... | collective-permute-start | bytes 5971976 | tf_op jit(solution)/shard_map/ppermute | solution.py:346
  155.2 34.3 %collective-permute-start.27 = (bf16[4,72,3200]{2,1,0:T(8,128)(2,1)}, bf16[4,72,3200]{2,1,0:T(8,128)(2,1)}, u32[]{:S(2)}, u32[]{:S(2)}) collective-permute-start(bf16[4,72,3200]{2,1,0:T(8,128)(2,1)} %collective-permute-done.22.refs_1_), channel_id=1, source_target_pairs={{0,16},{16,0},{1,17},{17,1},{2,18},{18,2},{3,19},{19,3},{4,20},{20... | collective-permute-start | bytes 5529608 | tf_op jit(solution)/shard_map/ppermute | solution.py:353
  155.2 34.3 %collective-permute-start.26 = (bf16[4,72,3200]{2,1,0:T(8,128)(2,1)}, bf16[4,72,3200]{2,1,0:T(8,128)(2,1)}, u32[]{:S(2)}, u32[]{:S(2)}) collective-permute-start(bf16[4,72,3200]{2,1,0:T(8,128)(2,1)} %pad_maximum_fusion.8.refs_0_), channel_id=1, source_target_pairs={{0,16},{16,0},{1,17},{17,1},{2,18},{18,2},{3,19},{19,3},{4,20},{20... | collective-permute-start | bytes 5529608 | tf_op jit(solution)/shard_map/ppermute | solution.py:346
  168.8 37.4 %collective-permute-start.29 = (bf16[4,72,4608]{2,1,0:T(8,128)(2,1)}, bf16[4,72,4608]{2,1,0:T(8,128)(2,1)}, u32[]{:S(2)}, u32[]{:S(2)}) collective-permute-start(bf16[4,72,4608]{2,1,0:T(8,128)(2,1)} %pad_maximum_fusion.5.refs_0_), channel_id=1, source_target_pairs={{0,2},{16,17},{1,3},{17,16},{2,0},{18,19},{3,1},{19,18},{4,6},{20,... | collective-permute-start | bytes 7962632 | tf_op jit(solution)/shard_map/ppermute | solution.py:345
  286.6 34.8 %collective-permute-start.41 = (bf16[4,128,2816]{2,1,0:T(8,128)(2,1)}, bf16[4,128,2816]{2,1,0:T(8,128)(2,1)}, u32[]{:S(2)}, u32[]{:S(2)}) collective-permute-start(bf16[4,128,2816]{2,1,0:T(8,128)(2,1)} %pad_maximum_fusion.4.refs_0_), channel_id=1, source_target_pairs={{0,2},{16,17},{1,3},{17,16},{2,0},{18,19},{3,1},{19,18},{4,6},{20,... | collective-permute-start | bytes 8650760 | tf_op jit(solution)/shard_map/ppermute | solution.py:345
  288.5 37.1 %collective-permute-start.42 = (bf16[4,128,2816]{2,1,0:T(8,128)(2,1)}, bf16[4,128,2816]{2,1,0:T(8,128)(2,1)}, u32[]{:S(2)}, u32[]{:S(2)}) collective-permute-start(bf16[4,128,2816]{2,1,0:T(8,128)(2,1)} %pad_maximum_fusion.4.refs_0_), channel_id=1, source_target_pairs={{0,16},{16,0},{1,17},{17,1},{2,18},{18,2},{3,19},{19,3},{4,20},{20... | collective-permute-start | bytes 8650760 | tf_op jit(solution)/shard_map/ppermute | solution.py:346
  325.1 52.1 %collective-permute-start.46 = (bf16[512,1024]{1,0:T(8,128)(2,1)}, bf16[512,1024]{1,0:T(8,128)(2,1)}, u32[]{:S(2)}, u32[]{:S(2)}) collective-permute-start(bf16[512,1024]{1,0:T(8,128)(2,1)} %get-tuple-element.243), channel_id=1, source_target_pairs={{0,16},{16,0},{1,17},{17,1},{2,18},{18,2},{3,19},{19,3},{4,20},{20... | collective-permute-start | bytes 3145736 | tf_op jit(solution)/shard_map/ppermute | solution.py:369
  372.7 50.5 %collective-permute-start.50 = (bf16[512,2304]{1,0:T(8,128)(2,1)}, bf16[512,2304]{1,0:T(8,128)(2,1)S(1)}, u32[]{:S(2)}, u32[]{:S(2)}) collective-permute-start(bf16[512,2304]{1,0:T(8,128)(2,1)} %get-tuple-element.234), channel_id=1, source_target_pairs={{0,16},{16,0},{1,17},{17,1},{2,18},{18,2},{3,19},{19,3},{4,20},{20... | collective-permute-start | bytes 7077896 | tf_op jit(solution)/shard_map/ppermute | solution.py:369
  387.3 48.4 %collective-permute-start.52 = (bf16[4,128,2816]{2,1,0:T(8,128)(2,1)}, bf16[4,128,2816]{2,1,0:T(8,128)(2,1)}, u32[]{:S(2)}, u32[]{:S(2)}) collective-permute-start(bf16[4,128,2816]{2,1,0:T(8,128)(2,1)} %get-tuple-element.144), channel_id=1, source_target_pairs={{0,2},{16,17},{1,3},{17,16},{2,0},{18,19},{3,1},{19,18},{4,6},{20,... | collective-permute-start | bytes 8650760 | tf_op jit(solution)/shard_map/ppermute | solution.py:480
  396.7 84.1 %collective-permute-start.56 = (bf16[4,72,2048]{2,1,0:T(8,128)(2,1)}, bf16[4,72,2048]{2,1,0:T(8,128)(2,1)}, u32[]{:S(2)}, u32[]{:S(2)}) collective-permute-start(bf16[4,72,2048]{2,1,0:T(8,128)(2,1)} %get-tuple-element.146), channel_id=1, source_target_pairs={{0,2},{16,17},{1,3},{17,16},{2,0},{18,19},{3,1},{19,18},{4,6},{20,... | collective-permute-start | bytes 3538952 | tf_op jit(solution)/shard_map/ppermute | solution.py:480
  422.8 68.5 %collective-permute-start.54 = (bf16[512,4608]{1,0:T(8,128)(2,1)}, bf16[512,4608]{1,0:T(8,128)(2,1)}, u32[]{:S(2)}, u32[]{:S(2)}) collective-permute-start(bf16[512,4608]{1,0:T(8,128)(2,1)} %bitcast.328), channel_id=1, source_target_pairs={{0,16},{16,0},{1,17},{17,1},{2,18},{18,2},{3,19},{19,3},{4,20},{20... | collective-permute-start | bytes 14155784 | tf_op jit(solution)/shard_map/ppermute | solution.py:373
  442.2 46.1 %collective-permute-start.55 = (bf16[2,128,2816]{2,1,0:T(8,128)(2,1)}, bf16[2,128,2816]{2,1,0:T(8,128)(2,1)}, u32[]{:S(2)}, u32[]{:S(2)}) collective-permute-start(bf16[2,128,2816]{2,1,0:T(8,128)(2,1)} %slice.394), channel_id=1, source_target_pairs={{0,1},{16,18},{1,0},{17,19},{2,3},{18,16},{3,2},{19,17},{4,5},{20,... | collective-permute-start | bytes 4325384 | tf_op jit(solution)/shard_map/ppermute | solution.py:480
  483.0 38.0 %collective-permute-start.59 = (bf16[4,288,1152]{2,1,0:T(8,128)(2,1)S(1)}, bf16[4,288,1152]{2,1,0:T(8,128)(2,1)}, u32[]{:S(2)}, u32[]{:S(2)}) collective-permute-start(bf16[4,288,1152]{2,1,0:T(8,128)(2,1)S(1)} %copy-done.20), channel_id=1, source_target_pairs={{0,2},{16,17},{1,3},{17,16},{2,0},{18,19},{3,1},{19,18},{4,6},{20,... | collective-permute-start | bytes 7962632 | tf_op jit(solution)/shard_map/ppermute | solution.py:480
  484.0 37.0 %collective-permute-start.60 = (bf16[2,72,2048]{2,1,0:T(8,128)(2,1)S(1)}, bf16[2,72,2048]{2,1,0:T(8,128)(2,1)S(1)}, u32[]{:S(2)}, u32[]{:S(2)}) collective-permute-start(bf16[2,72,2048]{2,1,0:T(8,128)(2,1)S(1)} %slice.397), channel_id=1, source_target_pairs={{0,1},{16,18},{1,0},{17,19},{2,3},{18,16},{3,2},{19,17},{4,5},{20,... | collective-permute-start | bytes 1769480 | tf_op jit(solution)/shard_map/ppermute | solution.py:480
  490.1 59.2 %collective-permute-start.64 = (bf16[128,2816]{1,0:T(8,128)(2,1)S(1)}, bf16[128,2816]{1,0:T(8,128)(2,1)S(1)}, u32[]{:S(2)}, u32[]{:S(2)}) collective-permute-start(bf16[128,2816]{1,0:T(8,128)(2,1)S(1)} %slice_bitcast_fusion.3), channel_id=1, source_target_pairs={{0,4},{4,0},{8,12},{12,8},{1,5},{5,1},{9,13},{13,9},{2,6},{6,2},{1... | collective-permute-start | bytes 2162696 | tf_op jit(solution)/shard_map/ppermute | solution.py:480
  547.6 39.5 %collective-permute-start.65 = (bf16[4,72,5760]{2,1,0:T(8,128)(2,1)}, bf16[4,72,5760]{2,1,0:T(8,128)(2,1)}, u32[]{:S(2)}, u32[]{:S(2)}) collective-permute-start(bf16[4,72,5760]{2,1,0:T(8,128)(2,1)} %get-tuple-element.156), channel_id=1, source_target_pairs={{0,2},{16,17},{1,3},{17,16},{2,0},{18,19},{3,1},{19,18},{4,6},{20,... | collective-permute-start | bytes 9953288 | tf_op jit(solution)/shard_map/ppermute | solution.py:480
  554.9 38.5 %collective-permute-start.68 = (bf16[512,3456]{1,0:T(8,128)(2,1)}, bf16[512,3456]{1,0:T(8,128)(2,1)}, u32[]{:S(2)}, u32[]{:S(2)}) collective-permute-start(bf16[512,3456]{1,0:T(8,128)(2,1)} %bitcast.114), channel_id=1, source_target_pairs={{0,16},{16,0},{1,17},{17,1},{2,18},{18,2},{3,19},{19,3},{4,20},{20... | collective-permute-start | bytes 10616840 | tf_op jit(solution)/shard_map/ppermute | solution.py:373
  560.2 40.9 %collective-permute-start.67 = (bf16[512,576]{0,1:T(8,128)(2,1)}, bf16[512,576]{0,1:T(8,128)(2,1)}, u32[]{:S(2)}, u32[]{:S(2)}) collective-permute-start(bf16[512,576]{0,1:T(8,128)(2,1)} %copy.85), channel_id=1, source_target_pairs={{0,16},{16,0},{1,17},{17,1},{2,18},{18,2},{3,19},{19,3},{4,20},{20... | collective-permute-start | bytes 1769480 | tf_op jit(solution)/shard_map/ppermute | solution.py:369
  566.8 55.6 %collective-permute-start.71 = (bf16[72,2048]{1,0:T(8,128)(2,1)}, bf16[72,2048]{1,0:T(8,128)(2,1)}, u32[]{:S(2)}, u32[]{:S(2)}) collective-permute-start(bf16[72,2048]{1,0:T(8,128)(2,1)} %fusion.80), channel_id=1, source_target_pairs={{8,0},{20,28},{9,1},{21,29},{10,2},{22,30},{11,3},{23,31},{12,4},{... | collective-permute-start | bytes 884744 | tf_op jit(solution)/shard_map/ppermute | solution.py:480
  568.3 51.4 %collective-permute-start.70 = (bf16[128,2816]{1,0:T(8,128)(2,1)}, bf16[128,2816]{1,0:T(8,128)(2,1)}, u32[]{:S(2)}, u32[]{:S(2)}) collective-permute-start(bf16[128,2816]{1,0:T(8,128)(2,1)} %fusion.60), channel_id=1, source_target_pairs={{8,0},{20,28},{9,1},{21,29},{10,2},{22,30},{11,3},{23,31},{12,4},{... | collective-permute-start | bytes 2162696 | tf_op jit(solution)/shard_map/ppermute | solution.py:480
  610.4 47.5 %collective-permute-start.73 = (bf16[4,72,3456]{2,1,0:T(8,128)(2,1)S(1)}, bf16[4,72,3456]{2,1,0:T(8,128)(2,1)}, u32[]{:S(2)}, u32[]{:S(2)}) collective-permute-start(bf16[4,72,3456]{2,1,0:T(8,128)(2,1)S(1)} %get-tuple-element.171), channel_id=1, source_target_pairs={{0,2},{16,17},{1,3},{17,16},{2,0},{18,19},{3,1},{19,18},{4,6},{20,... | collective-permute-start | bytes 5971976 | tf_op jit(solution)/shard_map/ppermute | solution.py:480
  623.5 51.7 %collective-permute-start.85 = (bf16[72,5760]{1,0:T(8,128)(2,1)S(1)}, bf16[72,5760]{1,0:T(8,128)(2,1)}, u32[]{:S(2)}, u32[]{:S(2)}) collective-permute-start(bf16[72,5760]{1,0:T(8,128)(2,1)S(1)} %slice_bitcast_fusion.1), channel_id=1, source_target_pairs={{0,4},{4,0},{8,12},{12,8},{1,5},{5,1},{9,13},{13,9},{2,6},{6,2},{1... | collective-permute-start | bytes 2488328 | tf_op jit(solution)/shard_map/ppermute | solution.py:480
  705.7 39.4 %collective-permute-start.91 = (bf16[72,5760]{1,0:T(8,128)(2,1)S(1)}, bf16[72,5760]{1,0:T(8,128)(2,1)}, u32[]{:S(2)}, u32[]{:S(2)}) collective-permute-start(bf16[72,5760]{1,0:T(8,128)(2,1)S(1)} %add_convert_fusion.13), channel_id=1, source_target_pairs={{0,16},{16,0},{1,17},{17,1},{2,18},{18,2},{3,19},{19,3},{4,20},{20... | collective-permute-start | bytes 2488328 | tf_op jit(solution)/shard_map/ppermute | solution.py:494
  716.9 34.3 %collective-permute-start.90 = (bf16[72,3456]{1,0:T(8,128)(2,1)S(1)}, bf16[72,3456]{1,0:T(8,128)(2,1)}, u32[]{:S(2)}, u32[]{:S(2)}) collective-permute-start(bf16[72,3456]{1,0:T(8,128)(2,1)S(1)} %fusion.74), channel_id=1, source_target_pairs={{8,0},{20,28},{9,1},{21,29},{10,2},{22,30},{11,3},{23,31},{12,4},{... | collective-permute-start | bytes 1493000 | tf_op jit(solution)/shard_map/ppermute | solution.py:480
  (198 other events, 2400.9 us)

commit v4 on v3

--- a/solution.py
+++ b/solution.py
@@ -106,6 +106,14 @@
 
 def after(value, *others):
     return lax.optimization_barrier((value,) + others)[0]
+
+
+def after_all(values, *others):
+    return lax.optimization_barrier(tuple(values) + others)[: len(values)]
+
+
+def about(micros):
+    return pl.CostEstimate(flops=0, transcendentals=0, bytes_accessed=int(micros * 3.3e6))
 
 
 def columns_of(widths):
@@ -171,6 +179,7 @@
             ],
         ),
         compiler_params=pltpu.CompilerParams(vmem_limit_bytes=32 * 1024 * 1024),
+        cost_estimate=about(1 + 5e-7 * count * rows * total / len(plan)),
         name=name,
     )(table, *sources)
 
@@ -255,6 +264,7 @@
         + [flat, flat, flat, flat, pltpu.VMEM((count, 128), LOW)]
         + [pltpu.SemaphoreType.DMA((3 + max(number_of, 1),))],
         compiler_params=pltpu.CompilerParams(vmem_limit_bytes=57 * 1024 * 1024),
+        cost_estimate=about(1 + count * 0.0016),
         name="update_rows",
     )(*[grad for grad, _, _ in pieces], *state, *given)
 
@@ -272,17 +282,51 @@
     return move_blocks(jnp.stack(places).astype(jnp.int32), sources, outs, plan, "place_blocks")
 
 
-def pick_blocks(sources, table):
-    widths = [source.shape[-1] for source in sources]
-    plan, places = [], []
-    for number in range(8):
-        for source_at, columns in enumerate(columns_of(widths)):
-            plan.append(
-                (source_at, None, (0, columns[1]), number // 4, number % 4, columns)
-            )
-            places.append(table[number])
-    outs = [(4, sum(widths)), (4, sum(widths))]
-    return move_blocks(jnp.stack(places).astype(jnp.int32), sources, outs, plan, "pick_blocks")
+def half_grads(table, left, right, start, total, given):
+    tokens, features = left[0].shape
+    width = right[0].shape[-1]
+    half = features // 2
+    rows = half // 8
+    tile = next(t for t in (1152, 768, 512, 384, 256) if width % t == 0 and start % t == 0)
+    if half > 1152:
+        tile = 384
+    given = [] if given is None else list(given)
+
+    def kernel(table_ref, own_left, mate_left, own_right, mate_right, *refs):
+        give_ref, keep_ref, total_ref = refs[len(given) :]
+        for core in range(2):
+
+            @pl.when(table_ref[0] == core)
+            def _():
+                mine = pl.ds(core * half, half)
+                total_ref[...] = dot_tn(own_left[:, mine], own_right[...]) + dot_tn(
+                    mate_left[:, mine], mate_right[...]
+                )
+
+        for number in range(8):
+            block = total_ref[pl.ds(pl.multiple_of(table_ref[1 + number] * rows, 8), rows), :]
+            (give_ref, keep_ref)[number // 4][number % 4] = block.astype(LOW)
+
+    first = start // tile
+    whole = pl.BlockSpec((tokens, features), lambda i, table: (0, 0))
+    part = pl.BlockSpec((tokens, tile), lambda i, table: (0, i))
+    out = pl.BlockSpec((4, rows, tile), lambda i, table: (0, 0, first + i))
+    return pl.pallas_call(
+        kernel,
+        grid_spec=pltpu.PrefetchScalarGridSpec(
+            num_scalar_prefetch=1,
+            grid=(width // tile,),
+            in_specs=[whole, whole, part, part]
+            + [pl.BlockSpec(memory_space=pl.ANY)] * len(given),
+            out_specs=[out, out],
+            scratch_shapes=[pltpu.VMEM((half, tile), jnp.float32)],
+        ),
+        out_shape=[jax.ShapeDtypeStruct((4, rows, total), LOW)] * 2,
+        input_output_aliases={5 + number: number for number in range(len(given))},
+        compiler_params=pltpu.CompilerParams(vmem_limit_bytes=48 * 1024 * 1024),
+        cost_estimate=about(3 + 1.6e-6 * features * width),
+        name="half_grads",
+    )(table, *left, *right, *given)
 
 
 class Staged:
@@ -361,16 +405,9 @@
             if k + 1 < last:
                 second_stage(k + 2, (tokens[k],))
 
-    def share_left(self, left):
-        half = left.shape[-1] // 2
-        tokens = left.reshape(-1, left.shape[-1])
-        keep = lax.dynamic_slice_in_dim(tokens, self.core * half, half, 1)
-        give = lax.dynamic_slice_in_dim(tokens, (1 - self.core) * half, half, 1)
-        return jnp.concatenate([keep, lax.ppermute(give, "blk", SWAP)])
-
-    def share_right(self, right):
-        tokens = right.reshape(-1, right.shape[-1])
-        return jnp.concatenate([tokens, lax.ppermute(tokens, "blk", SWAP)])
+    def share(self, value):
+        tokens = value.reshape(-1, value.shape[-1])
+        return tokens, lax.ppermute(tokens, "blk", SWAP)
 
     def start_grads(self, pairs):
         return StagedGrads(self, pairs)
@@ -455,17 +492,18 @@
 class StagedGrads:
     def __init__(self, moves, pairs):
         self.moves = moves
-        self.widths = [right.shape[-1] for _, right in pairs]
-        blocks = []
-        for left, right in pairs:
-            grad = jnp.einsum("ni,nj->ij", left, right, preferred_element_type=jnp.float32)
-            blocks.append(grad.astype(LOW).reshape(8, -1, grad.shape[-1]))
         low_bit = moves.z_at % 2
-        table = []
+        table = [moves.core]
         for outer_at in moves.near_order(moves.core, [(1, 1), (1, 0), (0, 1), (0, 0)]):
             for z_now in (low_bit, 1 - low_bit):
                 table.append(z_now * 4 + outer_at)
-        self.give, self.keep = pick_blocks(blocks, table)
+        table = jnp.stack(table).astype(jnp.int32)
+        total = sum(right[0].shape[-1] for _, right in pairs)
+        start, found = 0, None
+        for left, right in pairs:
+            found = half_grads(table, left, right, start, total, found)
+            start += right[0].shape[-1]
+        self.give, self.keep = found
         self.token = self.give
         self.stage = 0
 
@@ -503,7 +541,7 @@
 
 class DirectGrads:
     def __init__(self, pairs):
-        self.parts = [outer_sum(left, right).astype(LOW) for left, right in pairs]
+        self.parts = [outer_sum(left[0], right[0]).astype(LOW) for left, right in pairs]
         self.token = self.parts[0]
 
     def send(self, *gates):
@@ -533,11 +571,8 @@
         for group, gate in zip(groups, gates):
             gate([lax.all_gather(part, GROUP, axis=0, tiled=True) for part in group])
 
-    def share_left(self, left):
-        return left
-
-    def share_right(self, right):
-        return right
+    def share(self, value):
+        return (value,)
 
     def start_grads(self, pairs):
         return DirectGrads(pairs)
@@ -631,6 +666,7 @@
         out_specs=block,
         out_shape=jax.ShapeDtypeStruct(queries.shape, LOW),
         compiler_params=pltpu.CompilerParams(vmem_limit_bytes=32 * 1024 * 1024),
+        cost_estimate=about(14 * images / 4),
         name="attention",
     )(queries, near_kv, far_kv)
 
@@ -675,6 +711,7 @@
             jax.ShapeDtypeStruct(far_kv.shape, LOW),
         ],
         compiler_params=pltpu.CompilerParams(vmem_limit_bytes=32 * 1024 * 1024),
+        cost_estimate=about(21 * images / 4),
         name="attention_grads",
     )(queries, near_kv, far_kv, grad_att)
 
@@ -768,7 +805,7 @@
         hidden_f = hidden.astype(jnp.float32)
         mixed_a, pull_a = jax.vjp(modulate, hidden_f, scale_a, shift_a)
         mixed_a_low = mixed_a.astype(LOW)
-        left_qkv = moves.share_left(mixed_a_low)
+        left_qkv = moves.share(mixed_a_low)
         kept.update(
             gates=(gate_a, gate_m), scale_m=scale_m, shift_m=shift_m, hidden_f=hidden_f,
             mixed_a_low=mixed_a_low, pull_a=pull_a, left_qkv=left_qkv,
@@ -790,12 +827,12 @@
         queries, near_kv, far_kv = kept["queries"], kept["near_kv"], kept["far_kv"]
         queries = after(queries, w_proj)
         att_low = attention(queries, near_kv, far_kv)
-        left_proj = moves.share_left(att_low)
+        left_proj = moves.share(att_low)
         branch_a = matmul(att_low, w_proj) + b_proj
         residual = kept["hidden_f"] + kept["gates"][0][:, None, :] * branch_a
         mixed_m, pull_m = jax.vjp(modulate, residual, kept["scale_m"], kept["shift_m"])
         mixed_m_low = mixed_m.astype(LOW)
-        left_up = moves.share_left(mixed_m_low)
+        left_up = moves.share(mixed_m_low)
         kept.update(
             w_proj=w_proj, w_one=w_one, left_proj=left_proj,
             branch_a=branch_a, residual=residual, pull_m=pull_m, left_up=left_up,
@@ -809,8 +846,10 @@
         pre_act = matmul(kept["mixed_m_low"], w_up) + b_up
         activated, gelu_pull = jax.vjp(gelu_tanh, pre_act)
         act_low = activated.astype(LOW)
-        left_down = moves.share_left(act_low)
-        kept.update(w_up=w_up, gelu_pull=gelu_pull, act_low=act_low, left_down=left_down)
+        gelu_slope = gelu_pull(jnp.ones_like(pre_act))[0]
+        left_down = moves.share(act_low)
+        act_low, gelu_slope = lax.optimization_barrier((act_low, gelu_slope))
+        kept.update(w_up=w_up, gelu_slope=gelu_slope, act_low=act_low, left_down=left_down)
         return act_low
 
     def use_fourth(arrived):
@@ -819,11 +858,11 @@
         branch_m = matmul(kept["act_low"], w_down) + b_down
         output = kept["residual"] + kept["gates"][1][:, None, :] * branch_m
         out_low = output.astype(LOW)
-        left_one = moves.share_left(out_low)
+        left_one = moves.share(out_low)
         hid_one = matmul(out_low, kept["w_one"]) + c_one
         act_one, silu_one = jax.vjp(jax.nn.silu, hid_one)
         one_low = act_one.astype(LOW)
-        left_two = moves.share_left(one_low)
+        left_two = moves.share(one_low)
         kept.update(
             w_down=w_down, branch_m=branch_m, out_low=out_low, left_one=left_one,
             silu_one=silu_one, one_low=one_low, left_two=left_two,
@@ -836,7 +875,7 @@
         hid_two = matmul(kept["one_low"], w_two) + c_two
         act_two, silu_two = jax.vjp(jax.nn.silu, hid_two)
         two_low = act_two.astype(LOW)
-        left_three = moves.share_left(two_low)
+        left_three = moves.share(two_low)
         projection = matmul(two_low, w_three) + c_three
         kept.update(
             w_two=w_two, w_three=w_three, silu_two=silu_two, left_three=left_three,
@@ -858,37 +897,37 @@
     branch_a, branch_m, out_low, projection = [
         kept[name] for name in ("branch_a", "branch_m", "out_low", "projection")
     ]
-    pull_m, gelu_pull, silu_one, silu_two = [
-        kept[name] for name in ("pull_m", "gelu_pull", "silu_one", "silu_two")
+    pull_m, gelu_slope, silu_one, silu_two = [
+        kept[name] for name in ("pull_m", "gelu_slope", "silu_one", "silu_two")
     ]
     live_f = live_slots.astype(jnp.float32)[:, None, None]
     unit_proj, unit_pull = jax.vjp(rms_unit, projection)
     grad_proj = unit_pull(-LAMBDA_REPA * live_f * rms_unit(targets.astype(jnp.float32)))[0].astype(
         LOW
     )
-    right_three = moves.share_right(grad_proj)
+    right_three = moves.share(grad_proj)
     grad_cthree = column_sum(grad_proj)
     grad_htwo = silu_two(matmul_t(grad_proj, w_three))[0].astype(LOW)
-    right_two = moves.share_right(grad_htwo)
+    right_two = moves.share(grad_htwo)
     grad_ctwo = column_sum(grad_htwo)
     grad_hone = silu_one(matmul_t(grad_htwo, w_two))[0].astype(LOW)
-    right_one = moves.share_right(grad_hone)
+    right_one = moves.share(grad_hone)
     grads_fourth = moves.start_grads(
         [(kept["left_two"], right_two), (kept["left_three"], right_three)]
     )
     grad_cone = column_sum(grad_hone)
     grads_fourth.send()
-    right_one = after(right_one, grads_fourth.token)
+    right_one = after_all(right_one, grads_fourth.token)
     grads_one = moves.start_grads([(kept["left_one"], right_one)])
     grads_one.send()
     grad_hone = after(grad_hone, grads_one.token)
     grad_output = cotangent.astype(jnp.float32) * live_f + matmul_t(grad_hone, w_one)
     grad_gate_m = jnp.sum(grad_output * branch_m, axis=1)
     grad_bm = (gate_m[:, None, :] * grad_output).astype(LOW)
-    right_down = moves.share_right(grad_bm)
+    right_down = moves.share(grad_bm)
     grad_bdown = column_sum(grad_bm)
-    grad_pre = gelu_pull(matmul_t(grad_bm, w_down))[0].astype(LOW)
-    right_up = moves.share_right(grad_pre)
+    grad_pre = (matmul_t(grad_bm, w_down) * gelu_slope).astype(LOW)
+    right_up = moves.share(grad_pre)
     grads_down = moves.start_grads([(kept["left_down"], right_down)])
     grad_bup = column_sum(grad_pre)
     grads_down.send()
@@ -899,47 +938,42 @@
     grad_residual = grad_output + grad_res_m
     grad_gate_a = jnp.sum(grad_residual * branch_a, axis=1)
     grad_ba = (gate_a[:, None, :] * grad_residual).astype(LOW)
-    right_proj = moves.share_right(grad_ba)
+    right_proj = moves.share(grad_ba)
     grad_bproj = column_sum(grad_ba)
     grad_att = matmul_t(grad_ba, w_proj).astype(LOW)
     grads_one.add(grad_att)
     grads_one.send()
     grads_fourth.add(grad_att)
     grads_fourth.send()
-    right_up = after(right_up, grads_fourth.token, grads_one.token)
+    right_up = after_all(right_up, grads_fourth.token, grads_one.token)
     grads_up = moves.start_grads([(kept["left_up"], right_up), (kept["left_proj"], right_proj)])
     grads_up.send()
     grads_down.add(grads_up.token)
     grads_down.send()
     grads_one.add(grads_up.token)
     grads_one.send()
-    grad_att = after(grad_att, grads_up.token, grads_down.token, grads_one.token)
+    grads_fourth.add(grads_up.token)
+    grads_fourth.send()
+    grad_att = after(
+        grad_att, grads_up.token, grads_down.token, grads_one.token, grads_fourth.token
+    )
     grad_query, near_dkv, far_dkv = attention_grads(queries, near_kv, far_kv, grad_att)
     home_dkv = passed_along(far_dkv, "blk", -1)
     grads_down.add(grad_query)
     grads_down.send()
     grads_fourth.add(grad_query)
-    grads_fourth.send()
     grads_one.add(grad_query)
     grads_one.send()
     home_dkv = after(home_dkv, grads_down.token, grads_one.token, grads_fourth.token)
     grad_kv = (near_dkv + home_dkv.astype(jnp.float32)).astype(LOW)
     grad_qkv = jnp.concatenate([grad_query, grad_kv], axis=-1)
-    grads_up.add(grad_kv)
-    grads_up.send()
-    right_qkv = after(moves.share_right(grad_qkv), grads_up.token)
-    grads_first = moves.start_grads([(left_qkv, right_qkv)])
+    grads_first = moves.start_grads([(left_qkv, moves.share(grad_qkv))])
     qkv_sums = column_sum(grad_qkv)
     grads_first.send()
-    grads_up.add(grads_first.token)
-    grads_up.send()
     grads_down.add(grads_first.token)
     grads_down.send()
-    grads_fourth.add(grads_first.token)
     grads_one.add(grads_first.token)
-    grad_qkv = after(
-        grad_qkv, grads_up.token, grads_down.token, grads_fourth.token, grads_one.token
-    )
+    grad_qkv = after(grad_qkv, grads_first.token, grads_down.token, grads_one.token)
     grad_hid_a, grad_scale_a, grad_shift_a = pull_a(matmul_t(grad_qkv, w_qkv))
     grad_input = grad_residual + grad_hid_a
     grad_mod_part = jnp.concatenate(
@@ -960,25 +994,26 @@
     ).reshape(slots, -1)
     grad_small = jnp.concatenate([grad_mod_part, bias_grid], axis=1)
     small_came = lax.ppermute(grad_small, "blk", SWAP)
-    grads_first.add(grad_small)
+    grads_up.add(grad_small)
+    grads_up.send()
+    grads_first.add(grads_up.token)
     grads_first.send()
-    grad_small = (grad_small + after(small_came, grads_first.token)).astype(LOW)
-
-    def between_levels():
-        grads_up.add(grad_small)
+    small_came = after(small_came, grads_up.token, grads_first.token)
+    grad_small = (grad_small + small_came).astype(LOW)
+    small_all = moves.gather_slots(grad_small)
+    grads_first.add(small_all)
+    grads_first.send()
+    grads_up.add(small_all)
+    grads_up.send()
+    small_all = after(small_all, grads_first.token, grads_up.token)
+
+    def between_swaps():
+        grads_first.add()
+        grads_first.send()
+        grads_up.add()
         grads_up.send()
-        grads_first.add(moves.token)
-        grads_first.send()
-        return lax.optimization_barrier((grads_first.token, grads_up.token))[0]
-
-    def between_swaps():
-        grads_up.add()
-        return grads_up.token
-
-    small_all = moves.gather_slots(grad_small, between_levels)
-    grads_first.add()
-    grads_first.send()
-    small_all = after(small_all, grads_first.token)
+        return lax.optimization_barrier((grads_up.token, grads_first.token))[0]
+
     grad_mod = small_all[:, : 6 * D]
     cond_cols = matmul_t(grad_mod, p_ada).reshape(blocks, slots, rows_d)
     cond_rows = moves.swapped_in_order(moves.swap_slots(cond_cols, between_swaps))
@@ -1001,6 +1036,7 @@
     ada_at = (3 * D + FF + D) // blocks
     grad_b_flat = jnp.concatenate([bias_own[:ada_at], grad_bada, bias_own[ada_at:]])
     grads_down.add(grad_mod_part)
+    grads_up.add()
     images_all = slots * blocks
     tokens_img = local_tok * lax.axis_size("blk")
     rate_w = LR_COEF / math.sqrt(images_all * tokens_img)
@@ -1013,8 +1049,8 @@
             [(grads_fourth, PH, 7)],
             [(grads_one, 0, 5)],
             [(grads_down, 0, 3)],
+            [(grads_up, 0, 2)],
             [(grad_wada, 0, 4)],
-            [(grads_up, 0, 2)],
             [(grads_first, 0, 0), (grads_up, FF, 1)],
         ],
     )

time: 770 us -> 749 us (0.973)
  Pallas kernels: 104 us -> 156 us
  matrix products: 155 us -> 117 us
  other arithmetic: 114 us -> 91.6 us
  waiting for transfers between devices: 191 us -> 174 us
  starting transfers between devices: 114 us -> 126 us
  local copies, waits for them, and re-layouts: 79.2 us -> 71.5 us
    pallas_call x0 -> x7, Pallas kernels: none -> 62.3 us  [half_grads(): pl.pallas_call(kernel, grid_spec=pltpu.PrefetchScalarGridSpec(num_scalar_...]
    dot_general x7 -> x0, matrix products: 43.9 us -> none  [__init__(): jnp.einsum('ni,nj->ij', left, right, preferred_element_type=jnp.float32)]
    concatenate x4 -> x0, other arithmetic: 18.8 us -> none  [the longest x3 18.7 us: share_right(): return jnp.concatenate([tokens, lax.ppermute(tokens, 'blk', SWAP)])]
    dynamic_slice x7 -> x0, local copies, waits for them, and re-layouts: 16.1 us -> none  [share_left(): keep = lax.dynamic_slice_in_dim(tokens, self.core * half, half, 1)]
    ppermute x6, waiting for transfers between devices: 20.9 us -> 6.15 us  [gather_slots(): lax.ppermute(four, 'outer', route)]
    ppermute x5, waiting for transfers between devices: 40.8 us -> 26.4 us  [gather_groups(): far_four = lax.ppermute(fours[k], EVERY, NEAR_SECOND)]
    pallas_call x10 -> x5, Pallas kernels: 36.7 us -> 25.5 us  [move_blocks(): pl.pallas_call(kernel, out_shape=[jax.ShapeDtypeStruct((length, rows, wid...]
    dot_general x8, matrix products: 46.2 us -> 57.2 us  [matmul(): jnp.einsum('...i,ij->...j', left_arr, right_arr, preferred_element_type=j...]
  transfers between devices with their start and end apart: 97 -> 97, of which waited for: 31 -> 34; matrix products, arithmetic and copies ran while one was open for 44% -> 34% of each run, Pallas kernels for 13% -> 20%
where the time goes in v4:
time: 749 us; the launch traced here: 739 us
  waiting for transfers between devices  174 us (23%)
  Pallas kernels  156 us (21%)
  starting transfers between devices  126 us (17%)
  matrix products  117 us (16%)
  other arithmetic  91.6 us (12%)
  local copies, waits for them, and re-layouts  71.5 us (10%)
    pallas_call x7, Pallas kernels, half_grads(): pl.pallas_call(kernel, grid_spec=pltpu.PrefetchScalarGridSpec(num_scalar_...  62.3 us
    dot_general x8, matrix products, matmul_t(): jnp.einsum('...j,ij->...i', left_arr, right_arr, preferred_element_type=j...  57.6 us
    dot_general x8, matrix products, matmul(): jnp.einsum('...i,ij->...j', left_arr, right_arr, preferred_element_type=j...  57.2 us
    ppermute x20, waiting for transfers between devices, send(): self.came = lax.ppermute(self.give, axes, route)  45.4 us
    ppermute x5, waiting for transfers between devices, first_stage(): others[k] = lax.ppermute(held[k], 'inner', Z_PAIR)  38.3 us
    ppermute x5, waiting for transfers between devices, third_stage(): came = after(lax.ppermute(twos[k], EVERY, NEAR_FIRST), *late)  32.4 us
    pallas_call x7, Pallas kernels, update_rows(): pl.pallas_call(kernel, in_specs=[pl.BlockSpec(memory_space=pl.ANY)] * num...  32.2 us
    ppermute x5, waiting for transfers between devices, gather_groups(): far_four = lax.ppermute(fours[k], EVERY, NEAR_SECOND)  26.4 us
  transfers between devices with their start and end apart: 97, of which 34 were waited for; matrix products, arithmetic and copies ran while one was open for 34% of the time, Pallas kernels for 20%

profile of v4, /device:TPU:0, one launch (start us, length us, event | category | flops | bytes accessed | tf_op | source)
XLA Modules:
  0.0 739.3 jit_solution(5513514366584630484)
XLA Ops:
  51.8 9.3 %collective-permute-done.8 = bf16[72,3456]{1,0:T(8,128)(2,1)S(1)} collective-permute-done((bf16[72,3456]{1,0:T(8,128)(2,1)S(1)}, bf16[72,3456]{1,0:T(8,128)(2,1)S(1)}, u32[]{:S(2)}, u32[]{:S(2)}) %collective-permute-start.8) | collective-permute-done | bytes 497696 | tf_op jit(solution)/shard_map/ppermute | solution.py:372
  81.3 8.4 %collective-permute-done.18 = bf16[72,3200]{1,0:T(8,128)(2,1)S(1)} collective-permute-done((bf16[72,3200]{1,0:T(8,128)(2,1)S(1)}, bf16[72,3200]{1,0:T(8,128)(2,1)S(1)}, u32[]{:S(2)}, u32[]{:S(2)}) %collective-permute-start.18) | collective-permute-done | bytes 460832 | tf_op jit(solution)/shard_map/ppermute | solution.py:372
  89.8 13.6 %collective-permute-done.16.refs_1_ = bf16[4,72,3456]{2,1,0:T(8,128)(2,1)S(1)} collective-permute-done((bf16[4,72,3456]{2,1,0:T(8,128)(2,1)S(1)}, bf16[4,72,3456]{2,1,0:T(8,128)(2,1)S(1)}, u32[]{:S(2)}, u32[]{:S(2)}) %collective-permute-start.16) | collective-permute-done | bytes 1990688 | tf_op jit(solution)/shard_map/ppermute | solution.py:389
  129.6 15.7 %collective-permute-done.24 = bf16[72,4608]{1,0:T(8,128)(2,1)S(1)} collective-permute-done((bf16[72,4608]{1,0:T(8,128)(2,1)S(1)}, bf16[72,4608]{1,0:T(8,128)(2,1)S(1)}, u32[]{:S(2)}, u32[]{:S(2)}) %collective-permute-start.24) | collective-permute-done | bytes 663584 | tf_op jit(solution)/shard_map/ppermute | solution.py:372
  173.9 14.9 %attention.1 = bf16[4,128,1152]{2,1,0:T(8,128)(2,1)} custom-call(bf16[4,128,1152]{2,1,0:T(8,128)(2,1)S(1)} %slice.379.q_ref, bf16[4,128,2304]{2,1,0:T(8,128)(2,1)S(1)} %slice.380.near_ref, bf16[4,128,2304]{2,1,0:T(8,128)(2,1)S(1)} %copy-done.7), custom_call_target="tpu_custom_call" | custom-call | bytes 46200000 | tf_op jit(solution)/shard_map/attention/pallas_call | solution.py:662
  248.3 13.9 %fusion.5 = (f32[4,128,4608]{2,1,0:T(8,128)}, bf16[4,128,4608]{2,1,0:T(8,128)(2,1)}) fusion(f32[4608]{0:T(1024)S(1)} %copy-done.91, bf16[4,128,1152]{2,1,0:T(8,128)(2,1)S(1)} %add_convert_fusion.11, bf16[1152,4608,1]{1,0,2:T(8,128)(2,1)S(1)} %bitcast.261), kind=kOutput, calls=%fused_computation.10 | convolution fusion | flops 5483003904 | bytes 25970688 | tf_op jit(solution)/shard_map/...i,ij->...j/dot_general | solution.py:632
  273.3 17.4 %collective-permute-done.40 = bf16[2,128,2816]{2,1,0:T(8,128)(2,1)S(1)} collective-permute-done((bf16[2,128,2816]{2,1,0:T(8,128)(2,1)S(1)}, bf16[2,128,2816]{2,1,0:T(8,128)(2,1)S(1)}, u32[]{:S(2)}, u32[]{:S(2)}) %collective-permute-start.40) | collective-permute-done | bytes 1441824 | tf_op jit(solution)/shard_map/ppermute | solution.py:378
  302.4 11.3 %add_convert_fusion.10 = (bf16[4,128,1152]{2,1,0:T(8,128)(2,1)}, f32[4,128,1152]{2,1,0:T(8,128)}) fusion(f32[4,128,1152]{2,1,0:T(8,128)S(1)} %copy-done.26, f32[4,1152]{1,0:T(4,128)S(1)} %copy-done.96, f32[1152]{0:T(1024)S(1)} %copy-done.103, bf16[4,128,4608]{2,1,0:T(8,128)(2,1)} %get-tuple-element.140, bf16[4608,1152,1]{1,0,2:T(8,128)(2,1)S(1)} %bitcast.265), kind=kOutput, calls=%fused_computation.74 | convolution fusion | flops 5438177280 | bytes 21256704 | tf_op jit(solution)/shard_map/...i,ij->...j/dot_general | solution.py:632
  333.0 8.5 %place_blocks.9 = (bf16[16,128,2048]{2,1,0:T(8,128)(2,1)}, bf16[16,128,768]{2,1,0:T(8,128)(2,1)S(1)}) custom-call(s32[32]{0:T(128)S(1)} %stack.519.table_ref, bf16[4,128,2816]{2,1,0:T(8,128)(2,1)} %pad_maximum_fusion.1.refs_0_, bf16[4,128,2816]{2,1,0:T(8,128)(2,1)} %collective-permute-done.41.refs_1_, bf16[4,128,2816]{2,1,0:T(8,128)(2,1)} %collective-permute-done.42.refs_2_, ...), custom_call_target="tpu_custom_call" | custom-call | bytes 12815827 | tf_op jit(solution)/shard_map/place_blocks/pallas_call | solution.py:167
  341.6 9.8 %multiply_convert_fusion.2 = (bf16[4,128,2048]{2,1,0:T(8,128)(2,1)}, f32[4,128,2048]{2,1,0:T(8,128)S(1)}) fusion(f32[2048]{0:T(1024)S(1)} %copy-done.106, bf16[4,128,2048]{2,1,0:T(8,128)(2,1)S(1)} %copy-done.15, bf16[2048,2048,1]{1,0,2:T(8,128)(2,1)} %bitcast.354), kind=kOutput, calls=%fused_computation.30 | convolution fusion | flops 4301258752 | bytes 16785408 | tf_op jit(solution)/shard_map/...i,ij->...j/dot_general | solution.py:632
  362.5 11.2 %convert_reduce_fusion.3 = (f32[2048]{0:T(1024)}, bf16[4,128,2048]{2,1,0:T(8,128)(2,1)}) fusion(f32[4,128,2048]{2,1,0:T(8,128)S(1)} %copy-done.112, f32[2048]{0:T(1024)S(1)} %copy-done.105, bf16[4,128,2048]{2,1,0:T(8,128)(2,1)S(1)} %get-tuple-element.303, bf16[2048,2048,1]{1,0,2:T(8,128)(2,1)} %bitcast.355), kind=kOutput, calls=%fused_computation.29 | convolution fusion | flops 4308596736 | bytes 16793600 | tf_op jit(solution)/shard_map/...j,ij->...i/dot_general | solution.py:636
  380.5 8.8 %half_grads.7 = (bf16[4,128,2816]{2,1,0:T(8,128)(2,1)}, bf16[4,128,2816]{2,1,0:T(8,128)(2,1)}) custom-call(s32[9]{0:T(128)S(1)} %stack.538.table_ref, bf16[512,2048]{1,0:T(8,128)(2,1)S(1)} %bitcast.278, bf16[512,2048]{1,0:T(8,128)(2,1)S(1)} %copy-done.18, bf16[512,2048]{1,0:T(8,128)(2,1)} %bitcast.333, bf16[512,2048]{1,0:T(8,128)(2,1)} %copy-done.58), custom_call_target="tpu_custom_call" | custom-call | bytes 32045924 | tf_op jit(solution)/shard_map/half_grads/pallas_call | solution.py:314
  406.9 8.9 %convert_reduce_fusion.5 = (f32[1152]{0:T(1024)}, bf16[4,128,1152]{2,1,0:T(8,128)(2,1)}, f32[4,128,1152]{2,1,0:T(8,128)}) fusion(f32[4,1152]{1,0:T(4,128)S(1)} %copy-done.97, bf16[4,128,2048]{2,1,0:T(8,128)(2,1)} %get-tuple-element.156, bf16[1152,2048,1]{1,0,2:T(8,128)(2,1)} %bitcast.279, f32[4]{0:T(128)S(1)} %convert_element_type.327, ...), kind=kOutput, calls=%fused_computation.63 | convolution fusion | flops 2420046848 | bytes 11557392 | tf_op jit(solution)/shard_map/...j,ij->...i/dot_general | solution.py:636
  417.8 11.2 %convert_reduce_fusion = (f32[4608]{0:T(1024)}, bf16[4,128,4608]{2,1,0:T(8,128)(2,1)}) fusion(f32[4,128,4608]{2,1,0:T(8,128)} %get-tuple-element.157, bf16[4,128,1152]{2,1,0:T(8,128)(2,1)} %get-tuple-element.237, bf16[4608,1152,1]{1,0,2:T(8,128)(2,1)S(1)} %bitcast.268), kind=kOutput, calls=%fused_computation.11 | convolution fusion | flops 5445250560 | bytes 25970688 | tf_op jit(solution)/shard_map/...j,ij->...i/dot_general | solution.py:636
  429.0 15.3 %half_grads.10 = (bf16[4,288,1152]{2,1,0:T(8,128)(2,1)}, bf16[4,288,1152]{2,1,0:T(8,128)(2,1)}) custom-call(s32[9]{0:T(128)S(1)} %stack.538.table_ref, bf16[512,4608]{1,0:T(8,128)(2,1)} %bitcast.319, bf16[512,4608]{1,0:T(8,128)(2,1)} %collective-permute-done.50.mate_left, bf16[512,1152]{1,0:T(8,128)(2,1)} %bitcast.96.own_right, ...), custom_call_target="tpu_custom_call" | custom-call | bytes 37928436 | tf_op jit(solution)/shard_map/half_grads/pallas_call | solution.py:314
  452.7 9.6 %multiply_reduce_fusion.3 = (f32[4,128]{1,0:T(4,128)S(1)}, f32[4,128,1152]{2,1,0:T(8,128)}) fusion(f32[4,128,1152]{2,1,0:T(8,128)} %copy-done.25, f32[4,1152]{1,0:T(4,128)S(1)} %copy-done.66, f32[4,128]{1,0:T(4,128)S(1)} %broadcast_multiply_fusion, bf16[4,128,4608]{2,1,0:T(8,128)(2,1)} %get-tuple-element.161, bf16[1152,4608,1]{1,0,2:T(8,128)(2,1)S(1)} %bitcast.264), kind=kOutput, calls=%fused_computation.72 | convolution fusion | flops 5438176768 | bytes 20076544 | tf_op jit(solution)/shard_map/...j,ij->...i/dot_general | solution.py:636
  476.4 11.1 %collective-permute-done.57 = bf16[2,128,2816]{2,1,0:T(8,128)(2,1)} collective-permute-done((bf16[2,128,2816]{2,1,0:T(8,128)(2,1)}, bf16[2,128,2816]{2,1,0:T(8,128)(2,1)}, u32[]{:S(2)}, u32[]{:S(2)}) %collective-permute-start.57) | collective-permute-done | bytes 1441824 | tf_op jit(solution)/shard_map/ppermute | solution.py:518
  491.7 10.8 %half_grads.11 = (bf16[4,72,5760]{2,1,0:T(8,128)(2,1)S(1)}, bf16[4,72,5760]{2,1,0:T(8,128)(2,1)}) custom-call(s32[9]{0:T(128)S(1)} %stack.538.table_ref, bf16[512,1152]{1,0:T(8,128)(2,1)S(1)} %bitcast.272, bf16[512,1152]{1,0:T(8,128)(2,1)S(1)} %collective-permute-done.55.mate_left, bf16[512,4608]{1,0:T(8,128)(2,1)} %bitcast.321, ...), custom_call_target="tpu_custom_call" | custom-call | bytes 37928436 | tf_op jit(solution)/shard_map/half_grads/pallas_call | solution.py:314
  515.5 20.9 %attention_grads.1 = (bf16[4,128,1152]{2,1,0:T(8,128)(2,1)S(1)}, f32[4,128,2304]{2,1,0:T(8,128)S(1)}, bf16[4,128,2304]{2,1,0:T(8,128)(2,1)S(1)}) custom-call(bf16[4,128,1152]{2,1,0:T(8,128)(2,1)S(1)} %copy-done.3, bf16[4,128,2304]{2,1,0:T(8,128)(2,1)S(1)} %slice.380.near_ref, bf16[4,128,2304]{2,1,0:T(8,128)(2,1)S(1)} %copy-done.8, ...), custom_call_target="tpu_custom_call" | custom-call | bytes 69300000 | tf_op jit(solution)/shard_map/attention_grads/pallas_call | solution.py:703
  568.7 8.9 %half_grads.13 = (bf16[4,72,3456]{2,1,0:T(8,128)(2,1)S(1)}, bf16[4,72,3456]{2,1,0:T(8,128)(2,1)}) custom-call(s32[9]{0:T(128)S(1)} %stack.538.table_ref, bf16[512,1152]{1,0:T(8,128)(2,1)S(1)} %bitcast.274, bf16[512,1152]{1,0:T(8,128)(2,1)S(1)} %collective-permute-done.66.mate_left, bf16[512,3456]{1,0:T(8,128)(2,1)} %bitcast.109.own_right, ...), custom_call_target="tpu_custom_call" | custom-call | bytes 30921328 | tf_op jit(solution)/shard_map/half_grads/pallas_call | solution.py:314
  583.0 9.5 %fusion.22 = (f32[4,128]{1,0:T(4,128)S(1)}, f32[4,128,1152]{2,1,0:T(8,128)S(1)}) fusion(bf16[4,128,1152]{2,1,0:T(8,128)(2,1)S(1)} %copy-done.29, f32[4,1152]{1,0:T(4,128)S(1)} %copy-done.68, f32[4,128]{1,0:T(4,128)S(1)} %copy-done.84, bf16[4,128,3456]{2,1,0:T(8,128)(2,1)} %pad_maximum_fusion, bf16[1152,3456,1]{1,0,2:T(8,128)(2,1)} %bitcast.270), kind=kOutput, calls=%fused_computation.62 | convolution fusion | flops 4079812096 | bytes 15063040 | tf_op jit(solution)/shard_map/...j,ij->...i/dot_general | solution.py:636
  607.7 15.5 %collective-permute-done.72 = bf16[4,72,3456]{2,1,0:T(8,128)(2,1)} collective-permute-done((bf16[4,72,3456]{2,1,0:T(8,128)(2,1)S(1)}, bf16[4,72,3456]{2,1,0:T(8,128)(2,1)}, u32[]{:S(2)}, u32[]{:S(2)}) %collective-permute-start.72) | collective-permute-done | bytes 1990688 | tf_op jit(solution)/shard_map/ppermute | solution.py:518
  666.6 13.5 %collective-permute-done.89 = bf16[72,5760]{1,0:T(8,128)(2,1)S(1)} collective-permute-done((bf16[72,5760]{1,0:T(8,128)(2,1)S(1)}, bf16[72,5760]{1,0:T(8,128)(2,1)S(1)}, u32[]{:S(2)}, u32[]{:S(2)}) %collective-permute-start.89) | collective-permute-done | bytes 829472 | tf_op jit(solution)/shard_map/ppermute | solution.py:518
  688.6 8.6 %collective-permute-start.86 = (f32[4,4,72]{2,1,0:T(4,128)S(1)}, f32[4,4,72]{2,1,0:T(4,128)S(1)}, u32[]{:S(2)}, u32[]{:S(2)}) collective-permute-start(f32[4,4,72]{2,1,0:T(4,128)S(1)} %get-tuple-element.273), channel_id=1, source_target_pairs={{0,8},{8,0},{4,12},{12,4},{1,9},{9,1},{5,13},{13,5},{2,10},{10,2},... | collective-permute-start | bytes 13832 | tf_op jit(solution)/shard_map/ppermute | solution.py:454
  (647 shorter events, 449.5 us)
Async XLA Ops:
  81.2 37.2 %collective-permute-start.19 = (bf16[4,72,3456]{2,1,0:T(8,128)(2,1)S(1)}, bf16[4,72,3456]{2,1,0:T(8,128)(2,1)S(1)}, u32[]{:S(2)}, u32[]{:S(2)}) collective-permute-start(bf16[4,72,3456]{2,1,0:T(8,128)(2,1)S(1)} %pad_maximum_fusion.4.refs_0_), channel_id=1, source_target_pairs={{0,16},{16,0},{1,17},{17,1},{2,18},{18,2},{3,19},{19,3},{4,20},{20... | collective-permute-start | bytes 5971976 | tf_op jit(solution)/shard_map/ppermute | solution.py:390
  152.7 37.4 %collective-permute-start.27 = (bf16[4,72,3200]{2,1,0:T(8,128)(2,1)}, bf16[4,72,3200]{2,1,0:T(8,128)(2,1)}, u32[]{:S(2)}, u32[]{:S(2)}) collective-permute-start(bf16[4,72,3200]{2,1,0:T(8,128)(2,1)} %collective-permute-done.22.refs_1_), channel_id=1, source_target_pairs={{0,16},{16,0},{1,17},{17,1},{2,18},{18,2},{3,19},{19,3},{4,20},{20... | collective-permute-start | bytes 5529608 | tf_op jit(solution)/shard_map/ppermute | solution.py:397
  152.7 37.4 %collective-permute-start.26 = (bf16[4,72,3200]{2,1,0:T(8,128)(2,1)}, bf16[4,72,3200]{2,1,0:T(8,128)(2,1)}, u32[]{:S(2)}, u32[]{:S(2)}) collective-permute-start(bf16[4,72,3200]{2,1,0:T(8,128)(2,1)} %pad_maximum_fusion.5.refs_0_), channel_id=1, source_target_pairs={{0,16},{16,0},{1,17},{17,1},{2,18},{18,2},{3,19},{19,3},{4,20},{20... | collective-permute-start | bytes 5529608 | tf_op jit(solution)/shard_map/ppermute | solution.py:390
  155.7 33.0 %collective-permute-start.30 = (bf16[288,1152]{1,0:T(8,128)(2,1)}, bf16[288,1152]{1,0:T(8,128)(2,1)}, u32[]{:S(2)}, u32[]{:S(2)}) collective-permute-start(bf16[288,1152]{1,0:T(8,128)(2,1)} %reshape.1748), channel_id=1, source_target_pairs={{0,8},{28,20},{1,9},{29,21},{2,10},{30,22},{3,11},{31,23},{4,12},{... | collective-permute-start | bytes 1990664 | tf_op jit(solution)/shard_map/ppermute | solution.py:370
  169.5 38.3 %collective-permute-start.29 = (bf16[4,72,4608]{2,1,0:T(8,128)(2,1)}, bf16[4,72,4608]{2,1,0:T(8,128)(2,1)}, u32[]{:S(2)}, u32[]{:S(2)}) collective-permute-start(bf16[4,72,4608]{2,1,0:T(8,128)(2,1)} %pad_maximum_fusion.2.refs_0_), channel_id=1, source_target_pairs={{0,2},{16,17},{1,3},{17,16},{2,0},{18,19},{3,1},{19,18},{4,6},{20,... | collective-permute-start | bytes 7962632 | tf_op jit(solution)/shard_map/ppermute | solution.py:389
  207.9 35.5 %collective-permute-start.33 = (bf16[4,72,4608]{2,1,0:T(8,128)(2,1)}, bf16[4,72,4608]{2,1,0:T(8,128)(2,1)}, u32[]{:S(2)}, u32[]{:S(2)}) collective-permute-start(bf16[4,72,4608]{2,1,0:T(8,128)(2,1)} %collective-permute-done.29.refs_1_), channel_id=1, source_target_pairs={{0,16},{16,0},{1,17},{17,1},{2,18},{18,2},{3,19},{19,3},{4,20},{20... | collective-permute-start | bytes 7962632 | tf_op jit(solution)/shard_map/ppermute | solution.py:397
  207.9 35.4 %collective-permute-start.32 = (bf16[4,72,4608]{2,1,0:T(8,128)(2,1)}, bf16[4,72,4608]{2,1,0:T(8,128)(2,1)}, u32[]{:S(2)}, u32[]{:S(2)}) collective-permute-start(bf16[4,72,4608]{2,1,0:T(8,128)(2,1)} %pad_maximum_fusion.2.refs_0_), channel_id=1, source_target_pairs={{0,16},{16,0},{1,17},{17,1},{2,18},{18,2},{3,19},{19,3},{4,20},{20... | collective-permute-start | bytes 7962632 | tf_op jit(solution)/shard_map/ppermute | solution.py:390
  232.6 32.3 %collective-permute-start.35 = (bf16[4,288,1152]{2,1,0:T(8,128)(2,1)}, bf16[4,288,1152]{2,1,0:T(8,128)(2,1)}, u32[]{:S(2)}, u32[]{:S(2)}) collective-permute-start(bf16[4,288,1152]{2,1,0:T(8,128)(2,1)} %pad_maximum_fusion.3.refs_0_), channel_id=1, source_target_pairs={{0,2},{16,17},{1,3},{17,16},{2,0},{18,19},{3,1},{19,18},{4,6},{20,... | collective-permute-start | bytes 7962632 | tf_op jit(solution)/shard_map/ppermute | solution.py:389
  292.6 34.8 %collective-permute-start.41 = (bf16[4,128,2816]{2,1,0:T(8,128)(2,1)}, bf16[4,128,2816]{2,1,0:T(8,128)(2,1)}, u32[]{:S(2)}, u32[]{:S(2)}) collective-permute-start(bf16[4,128,2816]{2,1,0:T(8,128)(2,1)} %pad_maximum_fusion.1.refs_0_), channel_id=1, source_target_pairs={{0,2},{16,17},{1,3},{17,16},{2,0},{18,19},{3,1},{19,18},{4,6},{20,... | collective-permute-start | bytes 8650760 | tf_op jit(solution)/shard_map/ppermute | solution.py:389
  297.0 34.4 %collective-permute-start.42 = (bf16[4,128,2816]{2,1,0:T(8,128)(2,1)}, bf16[4,128,2816]{2,1,0:T(8,128)(2,1)}, u32[]{:S(2)}, u32[]{:S(2)}) collective-permute-start(bf16[4,128,2816]{2,1,0:T(8,128)(2,1)} %pad_maximum_fusion.1.refs_0_), channel_id=1, source_target_pairs={{0,16},{16,0},{1,17},{17,1},{2,18},{18,2},{3,19},{19,3},{4,20},{20... | collective-permute-start | bytes 8650760 | tf_op jit(solution)/shard_map/ppermute | solution.py:390
  330.9 98.1 %collective-permute-start.50 = (bf16[512,4608]{1,0:T(8,128)(2,1)}, bf16[512,4608]{1,0:T(8,128)(2,1)}, u32[]{:S(2)}, u32[]{:S(2)}) collective-permute-start(bf16[512,4608]{1,0:T(8,128)(2,1)} %bitcast.318), channel_id=1, source_target_pairs={{0,16},{16,0},{1,17},{17,1},{2,18},{18,2},{3,19},{19,3},{4,20},{20... | collective-permute-start | bytes 14155784 | tf_op jit(solution)/shard_map/ppermute | solution.py:410
  331.4 42.7 %collective-permute-start.48 = (bf16[512,2048]{1,0:T(8,128)(2,1)}, bf16[512,2048]{1,0:T(8,128)(2,1)S(1)}, u32[]{:S(2)}, u32[]{:S(2)}) collective-permute-start(bf16[512,2048]{1,0:T(8,128)(2,1)} %bitcast.277), channel_id=1, source_target_pairs={{0,16},{16,0},{1,17},{17,1},{2,18},{18,2},{3,19},{19,3},{4,20},{20... | collective-permute-start | bytes 6291464 | tf_op jit(solution)/shard_map/ppermute | solution.py:410
  351.4 37.9 %collective-permute-start.46 = (bf16[512,2048]{1,0:T(8,128)(2,1)}, bf16[512,2048]{1,0:T(8,128)(2,1)}, u32[]{:S(2)}, u32[]{:S(2)}) collective-permute-start(bf16[512,2048]{1,0:T(8,128)(2,1)} %bitcast.90.own_left), channel_id=1, source_target_pairs={{0,16},{16,0},{1,17},{17,1},{2,18},{18,2},{3,19},{19,3},{4,20},{20... | collective-permute-start | bytes 6291464 | tf_op jit(solution)/shard_map/ppermute | solution.py:410
  396.0 50.3 %collective-permute-start.52 = (bf16[4,128,2816]{2,1,0:T(8,128)(2,1)}, bf16[4,128,2816]{2,1,0:T(8,128)(2,1)}, u32[]{:S(2)}, u32[]{:S(2)}) collective-permute-start(bf16[4,128,2816]{2,1,0:T(8,128)(2,1)} %get-tuple-element.152), channel_id=1, source_target_pairs={{0,2},{16,17},{1,3},{17,16},{2,0},{18,19},{3,1},{19,18},{4,6},{20,... | collective-permute-start | bytes 8650760 | tf_op jit(solution)/shard_map/ppermute | solution.py:518
  397.6 106.5 %collective-permute-start.53 = (bf16[512,1152]{1,0:T(8,128)(2,1)}, bf16[512,1152]{1,0:T(8,128)(2,1)}, u32[]{:S(2)}, u32[]{:S(2)}) collective-permute-start(bf16[512,1152]{1,0:T(8,128)(2,1)} %bitcast.99.own_left), channel_id=1, source_target_pairs={{0,16},{16,0},{1,17},{17,1},{2,18},{18,2},{3,19},{19,3},{4,20},{20... | collective-permute-start | bytes 3538952 | tf_op jit(solution)/shard_map/ppermute | solution.py:410
  406.4 67.0 %collective-permute-start.58 = (bf16[4,72,2048]{2,1,0:T(8,128)(2,1)}, bf16[4,72,2048]{2,1,0:T(8,128)(2,1)}, u32[]{:S(2)}, u32[]{:S(2)}) collective-permute-start(bf16[4,72,2048]{2,1,0:T(8,128)(2,1)} %copy-done.24), channel_id=1, source_target_pairs={{0,2},{16,17},{1,3},{17,16},{2,0},{18,19},{3,1},{19,18},{4,6},{20,... | collective-permute-start | bytes 3538952 | tf_op jit(solution)/shard_map/ppermute | solution.py:518
  429.0 60.2 %collective-permute-start.56 = (bf16[512,4608]{1,0:T(8,128)(2,1)}, bf16[512,4608]{1,0:T(8,128)(2,1)}, u32[]{:S(2)}, u32[]{:S(2)}) collective-permute-start(bf16[512,4608]{1,0:T(8,128)(2,1)} %bitcast.320), channel_id=1, source_target_pairs={{0,16},{16,0},{1,17},{17,1},{2,18},{18,2},{3,19},{19,3},{4,20},{20... | collective-permute-start | bytes 14155784 | tf_op jit(solution)/shard_map/ppermute | solution.py:410
  444.3 64.9 %collective-permute-start.59 = (bf16[4,288,1152]{2,1,0:T(8,128)(2,1)}, bf16[4,288,1152]{2,1,0:T(8,128)(2,1)}, u32[]{:S(2)}, u32[]{:S(2)}) collective-permute-start(bf16[4,288,1152]{2,1,0:T(8,128)(2,1)} %get-tuple-element.158), channel_id=1, source_target_pairs={{0,2},{16,17},{1,3},{17,16},{2,0},{18,19},{3,1},{19,18},{4,6},{20,... | collective-permute-start | bytes 7962632 | tf_op jit(solution)/shard_map/ppermute | solution.py:518
  452.6 34.8 %collective-permute-start.57 = (bf16[2,128,2816]{2,1,0:T(8,128)(2,1)}, bf16[2,128,2816]{2,1,0:T(8,128)(2,1)}, u32[]{:S(2)}, u32[]{:S(2)}) collective-permute-start(bf16[2,128,2816]{2,1,0:T(8,128)(2,1)} %slice.394), channel_id=1, source_target_pairs={{0,1},{16,18},{1,0},{17,19},{2,3},{18,16},{3,2},{19,17},{4,5},{20,... | collective-permute-start | bytes 4325384 | tf_op jit(solution)/shard_map/ppermute | solution.py:518
  509.7 32.8 %collective-permute-start.65 = (bf16[128,2816]{1,0:T(8,128)(2,1)S(1)}, bf16[128,2816]{1,0:T(8,128)(2,1)S(1)}, u32[]{:S(2)}, u32[]{:S(2)}) collective-permute-start(bf16[128,2816]{1,0:T(8,128)(2,1)S(1)} %fusion.30), channel_id=1, source_target_pairs={{8,0},{20,28},{9,1},{21,29},{10,2},{22,30},{11,3},{23,31},{12,4},{... | collective-permute-start | bytes 2162696 | tf_op jit(solution)/shard_map/ppermute | solution.py:518
  554.0 43.3 %collective-permute-start.71 = (bf16[4,72,5760]{2,1,0:T(8,128)(2,1)}, bf16[4,72,5760]{2,1,0:T(8,128)(2,1)}, u32[]{:S(2)}, u32[]{:S(2)}) collective-permute-start(bf16[4,72,5760]{2,1,0:T(8,128)(2,1)} %get-tuple-element.169), channel_id=1, source_target_pairs={{0,2},{16,17},{1,3},{17,16},{2,0},{18,19},{3,1},{19,18},{4,6},{20,... | collective-permute-start | bytes 9953288 | tf_op jit(solution)/shard_map/ppermute | solution.py:518
  577.5 45.7 %collective-permute-start.72 = (bf16[4,72,3456]{2,1,0:T(8,128)(2,1)S(1)}, bf16[4,72,3456]{2,1,0:T(8,128)(2,1)}, u32[]{:S(2)}, u32[]{:S(2)}) collective-permute-start(bf16[4,72,3456]{2,1,0:T(8,128)(2,1)S(1)} %get-tuple-element.182), channel_id=1, source_target_pairs={{0,2},{16,17},{1,3},{17,16},{2,0},{18,19},{3,1},{19,18},{4,6},{20,... | collective-permute-start | bytes 5971976 | tf_op jit(solution)/shard_map/ppermute | solution.py:518
  603.1 53.9 %collective-permute-start.80 = (bf16[2,72,5760]{2,1,0:T(8,128)(2,1)}, bf16[2,72,5760]{2,1,0:T(8,128)(2,1)}, u32[]{:S(2)}, u32[]{:S(2)}) collective-permute-start(bf16[2,72,5760]{2,1,0:T(8,128)(2,1)} %slice.408), channel_id=1, source_target_pairs={{0,1},{16,18},{1,0},{17,19},{2,3},{18,16},{3,2},{19,17},{4,5},{20,... | collective-permute-start | bytes 4976648 | tf_op jit(solution)/shard_map/ppermute | solution.py:518
  663.4 49.1 %collective-permute-start.87 = (bf16[72,3456]{1,0:T(8,128)(2,1)}, bf16[72,3456]{1,0:T(8,128)(2,1)}, u32[]{:S(2)}, u32[]{:S(2)}) collective-permute-start(bf16[72,3456]{1,0:T(8,128)(2,1)} %slice_bitcast_fusion.7), channel_id=1, source_target_pairs={{0,4},{4,0},{8,12},{12,8},{1,5},{5,1},{9,13},{13,9},{2,6},{6,2},{1... | collective-permute-start | bytes 1493000 | tf_op jit(solution)/shard_map/ppermute | solution.py:518
  (198 other events, 2272.0 us)

commit v5 on v4

--- a/solution.py
+++ b/solution.py
@@ -379,7 +379,7 @@
             fours[k] = jnp.concatenate([twos[k], came])
 
         first_stage(0, (), early[0]())
-        second_stage(0, early[1]())
+        second_stage(0, early[1](held[0]))
         first_stage(1, (held[0],), (twos[0],))
         third_stage(0, early[2](twos[0]))
         second_stage(1, (fours[0],))
@@ -418,7 +418,9 @@
         results = None
         for entries in parts:
             if isinstance(entries[0][0], StagedGrads) and entries[0][0].stage == 3:
-                entries[0][0].add(results[0])
+                for part, _, _ in sum(parts, []):
+                    if isinstance(part, StagedGrads) and part.stage == 3:
+                        part.add(results[0])
             pieces = []
             for part, start, number in entries:
                 grad = part.both if isinstance(part, StagedGrads) else part
@@ -566,7 +568,7 @@
 
     def gather_groups(self, groups, gates, early):
         early[0]()
-        early[1]()
+        early[1](groups[0][0])
         early[2](groups[0][0])
         for group, gate in zip(groups, gates):
             gate([lax.all_gather(part, GROUP, axis=0, tiled=True) for part in group])
@@ -771,8 +773,8 @@
         kept["packed"] = moves.gather_slots(packed)
         return (moves.token,)
 
-    def early_product():
-        packed_all = kept["packed"]
+    def early_product(gate):
+        packed_all = after(kept["packed"], gate)
         cond_own = lax.dynamic_slice_in_dim(
             packed_all[:, :D], moves.own_row * rows_d, rows_d, 1
         )
@@ -1036,7 +1038,6 @@
     ada_at = (3 * D + FF + D) // blocks
     grad_b_flat = jnp.concatenate([bias_own[:ada_at], grad_bada, bias_own[ada_at:]])
     grads_down.add(grad_mod_part)
-    grads_up.add()
     images_all = slots * blocks
     tokens_img = local_tok * lax.axis_size("blk")
     rate_w = LR_COEF / math.sqrt(images_all * tokens_img)
@@ -1049,8 +1050,8 @@
             [(grads_fourth, PH, 7)],
             [(grads_one, 0, 5)],
             [(grads_down, 0, 3)],
+            [(grad_wada, 0, 4)],
             [(grads_up, 0, 2)],
-            [(grad_wada, 0, 4)],
             [(grads_first, 0, 0), (grads_up, FF, 1)],
         ],
     )

time: 749 us -> 746 us (level)
    ppermute x20, waiting for transfers between devices: 45.4 us -> 61 us  [send(): self.came = lax.ppermute(self.give, axes, route)]
    ppermute x5, waiting for transfers between devices: 38.3 us -> 28.7 us  [first_stage(): others[k] = lax.ppermute(held[k], 'inner', Z_PAIR)]
    ppermute x3, waiting for transfers between devices: 7.76 us -> 0.01 us  [swap_slots(): lax.ppermute(four[:, 1 + at], 'inner', route)]
    unnamed x248 -> x254, local copies, waits for them, and re-layouts: 20.6 us -> 20.7 us
  transfers between devices with their start and end apart: 97 -> 97, of which waited for: 34 -> 33; matrix products, arithmetic and copies ran while one was open for 34% -> 35% of each run, Pallas kernels for 20% -> 20%
where the time goes in v5:
time: 746 us; the launch traced here: 736 us
  waiting for transfers between devices  169 us (23%)
  Pallas kernels  156 us (21%)
  starting transfers between devices  123 us (16%)
  matrix products  118 us (16%)
  other arithmetic  91.6 us (12%)
  local copies, waits for them, and re-layouts  76.1 us (10%)
    pallas_call x7, Pallas kernels, half_grads(): pl.pallas_call(kernel, grid_spec=pltpu.PrefetchScalarGridSpec(num_scalar_...  62.4 us
    ppermute x20, waiting for transfers between devices, send(): self.came = lax.ppermute(self.give, axes, route)  61 us
    dot_general x8, matrix products, matmul_t(): jnp.einsum('...j,ij->...i', left_arr, right_arr, preferred_element_type=j...  57.8 us
    dot_general x8, matrix products, matmul(): jnp.einsum('...i,ij->...j', left_arr, right_arr, preferred_element_type=j...  57.2 us
    pallas_call x7, Pallas kernels, update_rows(): pl.pallas_call(kernel, in_specs=[pl.BlockSpec(memory_space=pl.ANY)] * num...  32.2 us
    ppermute x5, waiting for transfers between devices, first_stage(): others[k] = lax.ppermute(held[k], 'inner', Z_PAIR)  28.7 us
    ppermute x5, waiting for transfers between devices, third_stage(): came = after(lax.ppermute(twos[k], EVERY, NEAR_FIRST), *late)  27 us
    ppermute x5, waiting for transfers between devices, gather_groups(): far_four = lax.ppermute(fours[k], EVERY, NEAR_SECOND)  26.7 us
  transfers between devices with their start and end apart: 97, of which 33 were waited for; matrix products, arithmetic and copies ran while one was open for 35% of the time, Pallas kernels for 20%

profile of v5, /device:TPU:0, one launch (start us, length us, event | category | flops | bytes accessed | tf_op | source)
XLA Modules:
  0.0 736.3 jit_solution(16988058367673426589)
XLA Ops:
  78.9 9.4 %collective-permute-done.18 = bf16[72,3200]{1,0:T(8,128)(2,1)S(1)} collective-permute-done((bf16[72,3200]{1,0:T(8,128)(2,1)S(1)}, bf16[72,3200]{1,0:T(8,128)(2,1)S(1)}, u32[]{:S(2)}, u32[]{:S(2)}) %collective-permute-start.18) | collective-permute-done | bytes 460832 | tf_op jit(solution)/shard_map/ppermute | solution.py:372
  88.5 10.8 %collective-permute-done.16.refs_1_ = bf16[4,72,3456]{2,1,0:T(8,128)(2,1)S(1)} collective-permute-done((bf16[4,72,3456]{2,1,0:T(8,128)(2,1)S(1)}, bf16[4,72,3456]{2,1,0:T(8,128)(2,1)S(1)}, u32[]{:S(2)}, u32[]{:S(2)}) %collective-permute-start.16) | collective-permute-done | bytes 1990688 | tf_op jit(solution)/shard_map/ppermute | solution.py:389
  127.2 14.2 %collective-permute-done.24 = bf16[72,4608]{1,0:T(8,128)(2,1)S(1)} collective-permute-done((bf16[72,4608]{1,0:T(8,128)(2,1)S(1)}, bf16[72,4608]{1,0:T(8,128)(2,1)S(1)}, u32[]{:S(2)}, u32[]{:S(2)}) %collective-permute-start.24) | collective-permute-done | bytes 663584 | tf_op jit(solution)/shard_map/ppermute | solution.py:372
  170.6 14.9 %attention.1 = bf16[4,128,1152]{2,1,0:T(8,128)(2,1)} custom-call(bf16[4,128,1152]{2,1,0:T(8,128)(2,1)S(1)} %slice.378.q_ref, bf16[4,128,2304]{2,1,0:T(8,128)(2,1)S(1)} %slice.379.near_ref, bf16[4,128,2304]{2,1,0:T(8,128)(2,1)S(1)} %copy-done.7), custom_call_target="tpu_custom_call" | custom-call | bytes 46200000 | tf_op jit(solution)/shard_map/attention/pallas_call | solution.py:664
  232.9 8.6 %collective-permute-start.37 = (bf16[128,2816]{1,0:T(8,128)(2,1)S(1)}, bf16[128,2816]{1,0:T(8,128)(2,1)S(1)}, u32[]{:S(2)}, u32[]{:S(2)}) collective-permute-start(bf16[128,2816]{1,0:T(8,128)(2,1)S(1)} %broadcast_select_fusion.2), channel_id=1, source_target_pairs={{0,4},{4,0},{8,12},{12,8},{1,5},{5,1},{9,13},{13,9},{2,6},{6,2},{1... | collective-permute-start | bytes 2162696 | tf_op jit(solution)/shard_map/ppermute | solution.py:372
  246.5 14.0 %fusion.5 = (f32[4,128,4608]{2,1,0:T(8,128)}, bf16[4,128,4608]{2,1,0:T(8,128)(2,1)}) fusion(f32[4608]{0:T(1024)S(1)} %copy-done.94, bf16[4,128,1152]{2,1,0:T(8,128)(2,1)S(1)} %add_convert_fusion.11, bf16[1152,4608,1]{1,0,2:T(8,128)(2,1)S(1)} %bitcast.261), kind=kOutput, calls=%fused_computation.10 | convolution fusion | flops 5483003904 | bytes 25970688 | tf_op jit(solution)/shard_map/...i,ij->...j/dot_general | solution.py:634
  270.0 17.7 %collective-permute-done.40 = bf16[2,128,2816]{2,1,0:T(8,128)(2,1)S(1)} collective-permute-done((bf16[2,128,2816]{2,1,0:T(8,128)(2,1)S(1)}, bf16[2,128,2816]{2,1,0:T(8,128)(2,1)S(1)}, u32[]{:S(2)}, u32[]{:S(2)}) %collective-permute-start.40) | collective-permute-done | bytes 1441824 | tf_op jit(solution)/shard_map/ppermute | solution.py:378
  299.1 11.3 %add_convert_fusion.10 = (bf16[4,128,1152]{2,1,0:T(8,128)(2,1)}, f32[4,128,1152]{2,1,0:T(8,128)}) fusion(f32[4,128,1152]{2,1,0:T(8,128)S(1)} %copy-done.26, f32[4,1152]{1,0:T(4,128)S(1)} %copy-done.99, f32[1152]{0:T(1024)S(1)} %copy-done.106, bf16[4,128,4608]{2,1,0:T(8,128)(2,1)} %get-tuple-element.143, bf16[4608,1152,1]{1,0,2:T(8,128)(2,1)S(1)} %bitcast.265), kind=kOutput, calls=%fused_computation.74 | convolution fusion | flops 5438177280 | bytes 21256704 | tf_op jit(solution)/shard_map/...i,ij->...j/dot_general | solution.py:634
  329.9 8.5 %place_blocks.9 = (bf16[16,128,2048]{2,1,0:T(8,128)(2,1)}, bf16[16,128,768]{2,1,0:T(8,128)(2,1)S(1)}) custom-call(s32[32]{0:T(128)S(1)} %stack.519.table_ref, bf16[4,128,2816]{2,1,0:T(8,128)(2,1)} %pad_maximum_fusion.1.refs_0_, bf16[4,128,2816]{2,1,0:T(8,128)(2,1)} %collective-permute-done.41.refs_1_, bf16[4,128,2816]{2,1,0:T(8,128)(2,1)} %collective-permute-done.42.refs_2_, ...), custom_call_target="tpu_custom_call" | custom-call | bytes 12815827 | tf_op jit(solution)/shard_map/place_blocks/pallas_call | solution.py:167
  338.5 9.8 %multiply_convert_fusion.2 = (bf16[4,128,2048]{2,1,0:T(8,128)(2,1)}, f32[4,128,2048]{2,1,0:T(8,128)S(1)}) fusion(f32[2048]{0:T(1024)S(1)} %copy-done.109, bf16[4,128,2048]{2,1,0:T(8,128)(2,1)S(1)} %copy-done.15, bf16[2048,2048,1]{1,0,2:T(8,128)(2,1)} %bitcast.355), kind=kOutput, calls=%fused_computation.30 | convolution fusion | flops 4301258752 | bytes 16785408 | tf_op jit(solution)/shard_map/...i,ij->...j/dot_general | solution.py:634
  359.4 11.2 %convert_reduce_fusion.3 = (f32[2048]{0:T(1024)}, bf16[4,128,2048]{2,1,0:T(8,128)(2,1)}) fusion(f32[4,128,2048]{2,1,0:T(8,128)S(1)} %copy-done.115, f32[2048]{0:T(1024)S(1)} %copy-done.108, bf16[4,128,2048]{2,1,0:T(8,128)(2,1)S(1)} %get-tuple-element.307, bf16[2048,2048,1]{1,0,2:T(8,128)(2,1)} %bitcast.356), kind=kOutput, calls=%fused_computation.29 | convolution fusion | flops 4308596736 | bytes 16793600 | tf_op jit(solution)/shard_map/...j,ij->...i/dot_general | solution.py:638
  377.4 8.8 %half_grads.7 = (bf16[4,128,2816]{2,1,0:T(8,128)(2,1)}, bf16[4,128,2816]{2,1,0:T(8,128)(2,1)}) custom-call(s32[9]{0:T(128)S(1)} %stack.538.table_ref, bf16[512,2048]{1,0:T(8,128)(2,1)S(1)} %bitcast.278, bf16[512,2048]{1,0:T(8,128)(2,1)S(1)} %copy-done.18, bf16[512,2048]{1,0:T(8,128)(2,1)} %bitcast.333, bf16[512,2048]{1,0:T(8,128)(2,1)} %copy-done.60), custom_call_target="tpu_custom_call" | custom-call | bytes 32045924 | tf_op jit(solution)/shard_map/half_grads/pallas_call | solution.py:314
  404.0 9.1 %convert_reduce_fusion.5 = (f32[1152]{0:T(1024)}, bf16[4,128,1152]{2,1,0:T(8,128)(2,1)}, f32[4,128,1152]{2,1,0:T(8,128)}) fusion(f32[4,1152]{1,0:T(4,128)S(1)} %copy-done.100, bf16[4,128,2048]{2,1,0:T(8,128)(2,1)} %get-tuple-element.159, bf16[1152,2048,1]{1,0,2:T(8,128)(2,1)} %bitcast.279, f32[4]{0:T(128)S(1)} %convert_element_type.327, ...), kind=kOutput, calls=%fused_computation.63 | convolution fusion | flops 2420046848 | bytes 11557392 | tf_op jit(solution)/shard_map/...j,ij->...i/dot_general | solution.py:638
  415.3 11.2 %convert_reduce_fusion = (f32[4608]{0:T(1024)}, bf16[4,128,4608]{2,1,0:T(8,128)(2,1)}) fusion(f32[4,128,4608]{2,1,0:T(8,128)} %get-tuple-element.160, bf16[4,128,1152]{2,1,0:T(8,128)(2,1)} %get-tuple-element.241, bf16[4608,1152,1]{1,0,2:T(8,128)(2,1)S(1)} %bitcast.268), kind=kOutput, calls=%fused_computation.11 | convolution fusion | flops 5445250560 | bytes 25970688 | tf_op jit(solution)/shard_map/...j,ij->...i/dot_general | solution.py:638
  426.5 15.4 %half_grads.10 = (bf16[4,288,1152]{2,1,0:T(8,128)(2,1)}, bf16[4,288,1152]{2,1,0:T(8,128)(2,1)}) custom-call(s32[9]{0:T(128)S(1)} %stack.538.table_ref, bf16[512,4608]{1,0:T(8,128)(2,1)} %bitcast.319, bf16[512,4608]{1,0:T(8,128)(2,1)} %collective-permute-done.50.mate_left, bf16[512,1152]{1,0:T(8,128)(2,1)} %bitcast.96.own_right, ...), custom_call_target="tpu_custom_call" | custom-call | bytes 37928436 | tf_op jit(solution)/shard_map/half_grads/pallas_call | solution.py:314
  449.6 9.6 %multiply_reduce_fusion.3 = (f32[4,128]{1,0:T(4,128)S(1)}, f32[4,128,1152]{2,1,0:T(8,128)}) fusion(f32[4,128,1152]{2,1,0:T(8,128)} %copy-done.25, f32[4,1152]{1,0:T(4,128)S(1)} %copy-done.68, f32[4,128]{1,0:T(4,128)S(1)} %broadcast_multiply_fusion, bf16[4,128,4608]{2,1,0:T(8,128)(2,1)} %get-tuple-element.164, bf16[1152,4608,1]{1,0,2:T(8,128)(2,1)S(1)} %bitcast.264), kind=kOutput, calls=%fused_computation.72 | convolution fusion | flops 5438176768 | bytes 20076544 | tf_op jit(solution)/shard_map/...j,ij->...i/dot_general | solution.py:638
  473.1 10.8 %collective-permute-done.57 = bf16[2,128,2816]{2,1,0:T(8,128)(2,1)} collective-permute-done((bf16[2,128,2816]{2,1,0:T(8,128)(2,1)}, bf16[2,128,2816]{2,1,0:T(8,128)(2,1)}, u32[]{:S(2)}, u32[]{:S(2)}) %collective-permute-start.57) | collective-permute-done | bytes 1441824 | tf_op jit(solution)/shard_map/ppermute | solution.py:520
  489.9 10.8 %half_grads.11 = (bf16[4,72,5760]{2,1,0:T(8,128)(2,1)S(1)}, bf16[4,72,5760]{2,1,0:T(8,128)(2,1)}) custom-call(s32[9]{0:T(128)S(1)} %stack.538.table_ref, bf16[512,1152]{1,0:T(8,128)(2,1)S(1)} %bitcast.272, bf16[512,1152]{1,0:T(8,128)(2,1)S(1)} %collective-permute-done.55.mate_left, bf16[512,4608]{1,0:T(8,128)(2,1)} %bitcast.321, ...), custom_call_target="tpu_custom_call" | custom-call | bytes 37928436 | tf_op jit(solution)/shard_map/half_grads/pallas_call | solution.py:314
  513.3 20.9 %attention_grads.1 = (bf16[4,128,1152]{2,1,0:T(8,128)(2,1)S(1)}, f32[4,128,2304]{2,1,0:T(8,128)S(1)}, bf16[4,128,2304]{2,1,0:T(8,128)(2,1)S(1)}) custom-call(bf16[4,128,1152]{2,1,0:T(8,128)(2,1)S(1)} %copy-done.3, bf16[4,128,2304]{2,1,0:T(8,128)(2,1)S(1)} %slice.379.near_ref, bf16[4,128,2304]{2,1,0:T(8,128)(2,1)S(1)} %copy-done.8, ...), custom_call_target="tpu_custom_call" | custom-call | bytes 69300000 | tf_op jit(solution)/shard_map/attention_grads/pallas_call | solution.py:705
  567.0 8.9 %half_grads.13 = (bf16[4,72,3456]{2,1,0:T(8,128)(2,1)S(1)}, bf16[4,72,3456]{2,1,0:T(8,128)(2,1)}) custom-call(s32[9]{0:T(128)S(1)} %stack.538.table_ref, bf16[512,1152]{1,0:T(8,128)(2,1)S(1)} %bitcast.274, bf16[512,1152]{1,0:T(8,128)(2,1)S(1)} %collective-permute-done.66.mate_left, bf16[512,3456]{1,0:T(8,128)(2,1)} %bitcast.109.own_right, ...), custom_call_target="tpu_custom_call" | custom-call | bytes 30921328 | tf_op jit(solution)/shard_map/half_grads/pallas_call | solution.py:314
  581.3 9.5 %fusion.22 = (f32[4,128]{1,0:T(4,128)S(1)}, f32[4,128,1152]{2,1,0:T(8,128)S(1)}) fusion(bf16[4,128,1152]{2,1,0:T(8,128)(2,1)S(1)} %copy-done.29, f32[4,1152]{1,0:T(4,128)S(1)} %copy-done.70, f32[4,128]{1,0:T(4,128)S(1)} %copy-done.86, bf16[4,128,3456]{2,1,0:T(8,128)(2,1)} %pad_maximum_fusion, bf16[1152,3456,1]{1,0,2:T(8,128)(2,1)} %bitcast.270), kind=kOutput, calls=%fused_computation.62 | convolution fusion | flops 4079812096 | bytes 15063040 | tf_op jit(solution)/shard_map/...j,ij->...i/dot_general | solution.py:638
  606.0 15.5 %collective-permute-done.72 = bf16[4,72,3456]{2,1,0:T(8,128)(2,1)} collective-permute-done((bf16[4,72,3456]{2,1,0:T(8,128)(2,1)S(1)}, bf16[4,72,3456]{2,1,0:T(8,128)(2,1)}, u32[]{:S(2)}, u32[]{:S(2)}) %collective-permute-start.72) | collective-permute-done | bytes 1990688 | tf_op jit(solution)/shard_map/ppermute | solution.py:520
  692.4 20.7 %collective-permute-done.88 = bf16[72,3456]{1,0:T(8,128)(2,1)S(1)} collective-permute-done((bf16[72,3456]{1,0:T(8,128)(2,1)S(1)}, bf16[72,3456]{1,0:T(8,128)(2,1)S(1)}, u32[]{:S(2)}, u32[]{:S(2)}) %collective-permute-start.88) | collective-permute-done | bytes 497696 | tf_op jit(solution)/shard_map/ppermute | solution.py:520
  713.2 8.7 %collective-permute-done.95 = bf16[72,5760]{1,0:T(8,128)(2,1)S(1)} collective-permute-done((bf16[72,5760]{1,0:T(8,128)(2,1)S(1)}, bf16[72,5760]{1,0:T(8,128)(2,1)S(1)}, u32[]{:S(2)}, u32[]{:S(2)}) %collective-permute-start.95) | collective-permute-done | bytes 829472 | tf_op jit(solution)/shard_map/ppermute | solution.py:520
  (652 shorter events, 442.9 us)
Async XLA Ops:
  78.9 35.4 %collective-permute-start.19 = (bf16[4,72,3456]{2,1,0:T(8,128)(2,1)S(1)}, bf16[4,72,3456]{2,1,0:T(8,128)(2,1)S(1)}, u32[]{:S(2)}, u32[]{:S(2)}) collective-permute-start(bf16[4,72,3456]{2,1,0:T(8,128)(2,1)S(1)} %pad_maximum_fusion.4.refs_0_), channel_id=1, source_target_pairs={{0,16},{16,0},{1,17},{17,1},{2,18},{18,2},{3,19},{19,3},{4,20},{20... | collective-permute-start | bytes 5971976 | tf_op jit(solution)/shard_map/ppermute | solution.py:390
  151.9 34.7 %collective-permute-start.27 = (bf16[4,72,3200]{2,1,0:T(8,128)(2,1)}, bf16[4,72,3200]{2,1,0:T(8,128)(2,1)}, u32[]{:S(2)}, u32[]{:S(2)}) collective-permute-start(bf16[4,72,3200]{2,1,0:T(8,128)(2,1)} %collective-permute-done.22.refs_1_), channel_id=1, source_target_pairs={{0,16},{16,0},{1,17},{17,1},{2,18},{18,2},{3,19},{19,3},{4,20},{20... | collective-permute-start | bytes 5529608 | tf_op jit(solution)/shard_map/ppermute | solution.py:397
  151.9 34.7 %collective-permute-start.26 = (bf16[4,72,3200]{2,1,0:T(8,128)(2,1)}, bf16[4,72,3200]{2,1,0:T(8,128)(2,1)}, u32[]{:S(2)}, u32[]{:S(2)}) collective-permute-start(bf16[4,72,3200]{2,1,0:T(8,128)(2,1)} %pad_maximum_fusion.5.refs_0_), channel_id=1, source_target_pairs={{0,16},{16,0},{1,17},{17,1},{2,18},{18,2},{3,19},{19,3},{4,20},{20... | collective-permute-start | bytes 5529608 | tf_op jit(solution)/shard_map/ppermute | solution.py:390
  166.4 38.1 %collective-permute-start.29 = (bf16[4,72,4608]{2,1,0:T(8,128)(2,1)}, bf16[4,72,4608]{2,1,0:T(8,128)(2,1)}, u32[]{:S(2)}, u32[]{:S(2)}) collective-permute-start(bf16[4,72,4608]{2,1,0:T(8,128)(2,1)} %pad_maximum_fusion.2.refs_0_), channel_id=1, source_target_pairs={{0,2},{16,17},{1,3},{17,16},{2,0},{18,19},{3,1},{19,18},{4,6},{20,... | collective-permute-start | bytes 7962632 | tf_op jit(solution)/shard_map/ppermute | solution.py:389
  204.5 37.0 %collective-permute-start.33 = (bf16[4,72,4608]{2,1,0:T(8,128)(2,1)}, bf16[4,72,4608]{2,1,0:T(8,128)(2,1)}, u32[]{:S(2)}, u32[]{:S(2)}) collective-permute-start(bf16[4,72,4608]{2,1,0:T(8,128)(2,1)} %collective-permute-done.29.refs_1_), channel_id=1, source_target_pairs={{0,16},{16,0},{1,17},{17,1},{2,18},{18,2},{3,19},{19,3},{4,20},{20... | collective-permute-start | bytes 7962632 | tf_op jit(solution)/shard_map/ppermute | solution.py:397
  204.7 36.8 %collective-permute-start.32 = (bf16[4,72,4608]{2,1,0:T(8,128)(2,1)}, bf16[4,72,4608]{2,1,0:T(8,128)(2,1)}, u32[]{:S(2)}, u32[]{:S(2)}) collective-permute-start(bf16[4,72,4608]{2,1,0:T(8,128)(2,1)} %pad_maximum_fusion.2.refs_0_), channel_id=1, source_target_pairs={{0,16},{16,0},{1,17},{17,1},{2,18},{18,2},{3,19},{19,3},{4,20},{20... | collective-permute-start | bytes 7962632 | tf_op jit(solution)/shard_map/ppermute | solution.py:390
  230.3 32.3 %collective-permute-start.35 = (bf16[4,288,1152]{2,1,0:T(8,128)(2,1)}, bf16[4,288,1152]{2,1,0:T(8,128)(2,1)}, u32[]{:S(2)}, u32[]{:S(2)}) collective-permute-start(bf16[4,288,1152]{2,1,0:T(8,128)(2,1)} %pad_maximum_fusion.3.refs_0_), channel_id=1, source_target_pairs={{0,2},{16,17},{1,3},{17,16},{2,0},{18,19},{3,1},{19,18},{4,6},{20,... | collective-permute-start | bytes 7962632 | tf_op jit(solution)/shard_map/ppermute | solution.py:389
  289.5 34.8 %collective-permute-start.41 = (bf16[4,128,2816]{2,1,0:T(8,128)(2,1)}, bf16[4,128,2816]{2,1,0:T(8,128)(2,1)}, u32[]{:S(2)}, u32[]{:S(2)}) collective-permute-start(bf16[4,128,2816]{2,1,0:T(8,128)(2,1)} %pad_maximum_fusion.1.refs_0_), channel_id=1, source_target_pairs={{0,2},{16,17},{1,3},{17,16},{2,0},{18,19},{3,1},{19,18},{4,6},{20,... | collective-permute-start | bytes 8650760 | tf_op jit(solution)/shard_map/ppermute | solution.py:389
  293.7 34.7 %collective-permute-start.42 = (bf16[4,128,2816]{2,1,0:T(8,128)(2,1)}, bf16[4,128,2816]{2,1,0:T(8,128)(2,1)}, u32[]{:S(2)}, u32[]{:S(2)}) collective-permute-start(bf16[4,128,2816]{2,1,0:T(8,128)(2,1)} %pad_maximum_fusion.1.refs_0_), channel_id=1, source_target_pairs={{0,16},{16,0},{1,17},{17,1},{2,18},{18,2},{3,19},{19,3},{4,20},{20... | collective-permute-start | bytes 8650760 | tf_op jit(solution)/shard_map/ppermute | solution.py:390
  327.9 98.7 %collective-permute-start.50 = (bf16[512,4608]{1,0:T(8,128)(2,1)}, bf16[512,4608]{1,0:T(8,128)(2,1)}, u32[]{:S(2)}, u32[]{:S(2)}) collective-permute-start(bf16[512,4608]{1,0:T(8,128)(2,1)} %bitcast.318), channel_id=1, source_target_pairs={{0,16},{16,0},{1,17},{17,1},{2,18},{18,2},{3,19},{19,3},{4,20},{20... | collective-permute-start | bytes 14155784 | tf_op jit(solution)/shard_map/ppermute | solution.py:410
  328.4 42.6 %collective-permute-start.48 = (bf16[512,2048]{1,0:T(8,128)(2,1)}, bf16[512,2048]{1,0:T(8,128)(2,1)S(1)}, u32[]{:S(2)}, u32[]{:S(2)}) collective-permute-start(bf16[512,2048]{1,0:T(8,128)(2,1)} %bitcast.277), channel_id=1, source_target_pairs={{0,16},{16,0},{1,17},{17,1},{2,18},{18,2},{3,19},{19,3},{4,20},{20... | collective-permute-start | bytes 6291464 | tf_op jit(solution)/shard_map/ppermute | solution.py:410
  348.3 37.9 %collective-permute-start.46 = (bf16[512,2048]{1,0:T(8,128)(2,1)}, bf16[512,2048]{1,0:T(8,128)(2,1)}, u32[]{:S(2)}, u32[]{:S(2)}) collective-permute-start(bf16[512,2048]{1,0:T(8,128)(2,1)} %bitcast.90.own_left), channel_id=1, source_target_pairs={{0,16},{16,0},{1,17},{17,1},{2,18},{18,2},{3,19},{19,3},{4,20},{20... | collective-permute-start | bytes 6291464 | tf_op jit(solution)/shard_map/ppermute | solution.py:410
  392.9 49.9 %collective-permute-start.52 = (bf16[4,128,2816]{2,1,0:T(8,128)(2,1)}, bf16[4,128,2816]{2,1,0:T(8,128)(2,1)}, u32[]{:S(2)}, u32[]{:S(2)}) collective-permute-start(bf16[4,128,2816]{2,1,0:T(8,128)(2,1)} %get-tuple-element.155), channel_id=1, source_target_pairs={{0,2},{16,17},{1,3},{17,16},{2,0},{18,19},{3,1},{19,18},{4,6},{20,... | collective-permute-start | bytes 8650760 | tf_op jit(solution)/shard_map/ppermute | solution.py:520
  394.3 108.0 %collective-permute-start.53 = (bf16[512,1152]{1,0:T(8,128)(2,1)}, bf16[512,1152]{1,0:T(8,128)(2,1)}, u32[]{:S(2)}, u32[]{:S(2)}) collective-permute-start(bf16[512,1152]{1,0:T(8,128)(2,1)} %bitcast.99.own_left), channel_id=1, source_target_pairs={{0,16},{16,0},{1,17},{17,1},{2,18},{18,2},{3,19},{19,3},{4,20},{20... | collective-permute-start | bytes 3538952 | tf_op jit(solution)/shard_map/ppermute | solution.py:410
  403.1 67.2 %collective-permute-start.58 = (bf16[4,72,2048]{2,1,0:T(8,128)(2,1)}, bf16[4,72,2048]{2,1,0:T(8,128)(2,1)}, u32[]{:S(2)}, u32[]{:S(2)}) collective-permute-start(bf16[4,72,2048]{2,1,0:T(8,128)(2,1)} %copy-done.24), channel_id=1, source_target_pairs={{0,2},{16,17},{1,3},{17,16},{2,0},{18,19},{3,1},{19,18},{4,6},{20,... | collective-permute-start | bytes 3538952 | tf_op jit(solution)/shard_map/ppermute | solution.py:520
  426.5 59.2 %collective-permute-start.56 = (bf16[512,4608]{1,0:T(8,128)(2,1)}, bf16[512,4608]{1,0:T(8,128)(2,1)}, u32[]{:S(2)}, u32[]{:S(2)}) collective-permute-start(bf16[512,4608]{1,0:T(8,128)(2,1)} %bitcast.320), channel_id=1, source_target_pairs={{0,16},{16,0},{1,17},{17,1},{2,18},{18,2},{3,19},{19,3},{4,20},{20... | collective-permute-start | bytes 14155784 | tf_op jit(solution)/shard_map/ppermute | solution.py:410
  441.9 65.7 %collective-permute-start.59 = (bf16[4,288,1152]{2,1,0:T(8,128)(2,1)}, bf16[4,288,1152]{2,1,0:T(8,128)(2,1)}, u32[]{:S(2)}, u32[]{:S(2)}) collective-permute-start(bf16[4,288,1152]{2,1,0:T(8,128)(2,1)} %get-tuple-element.161), channel_id=1, source_target_pairs={{0,2},{16,17},{1,3},{17,16},{2,0},{18,19},{3,1},{19,18},{4,6},{20,... | collective-permute-start | bytes 7962632 | tf_op jit(solution)/shard_map/ppermute | solution.py:520
  449.1 34.8 %collective-permute-start.57 = (bf16[2,128,2816]{2,1,0:T(8,128)(2,1)}, bf16[2,128,2816]{2,1,0:T(8,128)(2,1)}, u32[]{:S(2)}, u32[]{:S(2)}) collective-permute-start(bf16[2,128,2816]{2,1,0:T(8,128)(2,1)} %slice.393), channel_id=1, source_target_pairs={{0,1},{16,18},{1,0},{17,19},{2,3},{18,16},{3,2},{19,17},{4,5},{20,... | collective-permute-start | bytes 4325384 | tf_op jit(solution)/shard_map/ppermute | solution.py:520
  507.7 32.3 %collective-permute-start.64 = (bf16[72,2048]{1,0:T(8,128)(2,1)S(1)}, bf16[72,2048]{1,0:T(8,128)(2,1)S(1)}, u32[]{:S(2)}, u32[]{:S(2)}) collective-permute-start(bf16[72,2048]{1,0:T(8,128)(2,1)S(1)} %slice_bitcast_fusion.9), channel_id=1, source_target_pairs={{0,4},{4,0},{8,12},{12,8},{1,5},{5,1},{9,13},{13,9},{2,6},{6,2},{1... | collective-permute-start | bytes 884744 | tf_op jit(solution)/shard_map/ppermute | solution.py:520
  508.0 32.9 %collective-permute-start.65 = (bf16[128,2816]{1,0:T(8,128)(2,1)S(1)}, bf16[128,2816]{1,0:T(8,128)(2,1)S(1)}, u32[]{:S(2)}, u32[]{:S(2)}) collective-permute-start(bf16[128,2816]{1,0:T(8,128)(2,1)S(1)} %fusion.30), channel_id=1, source_target_pairs={{8,0},{20,28},{9,1},{21,29},{10,2},{22,30},{11,3},{23,31},{12,4},{... | collective-permute-start | bytes 2162696 | tf_op jit(solution)/shard_map/ppermute | solution.py:520
  552.3 43.3 %collective-permute-start.71 = (bf16[4,72,5760]{2,1,0:T(8,128)(2,1)}, bf16[4,72,5760]{2,1,0:T(8,128)(2,1)}, u32[]{:S(2)}, u32[]{:S(2)}) collective-permute-start(bf16[4,72,5760]{2,1,0:T(8,128)(2,1)} %get-tuple-element.172), channel_id=1, source_target_pairs={{0,2},{16,17},{1,3},{17,16},{2,0},{18,19},{3,1},{19,18},{4,6},{20,... | collective-permute-start | bytes 9953288 | tf_op jit(solution)/shard_map/ppermute | solution.py:520
  575.9 45.7 %collective-permute-start.72 = (bf16[4,72,3456]{2,1,0:T(8,128)(2,1)S(1)}, bf16[4,72,3456]{2,1,0:T(8,128)(2,1)}, u32[]{:S(2)}, u32[]{:S(2)}) collective-permute-start(bf16[4,72,3456]{2,1,0:T(8,128)(2,1)S(1)} %get-tuple-element.185), channel_id=1, source_target_pairs={{0,2},{16,17},{1,3},{17,16},{2,0},{18,19},{3,1},{19,18},{4,6},{20,... | collective-permute-start | bytes 5971976 | tf_op jit(solution)/shard_map/ppermute | solution.py:520
  601.5 50.5 %collective-permute-start.80 = (bf16[2,72,5760]{2,1,0:T(8,128)(2,1)}, bf16[2,72,5760]{2,1,0:T(8,128)(2,1)}, u32[]{:S(2)}, u32[]{:S(2)}) collective-permute-start(bf16[2,72,5760]{2,1,0:T(8,128)(2,1)} %slice.407), channel_id=1, source_target_pairs={{0,1},{16,18},{1,0},{17,19},{2,3},{18,16},{3,2},{19,17},{4,5},{20,... | collective-permute-start | bytes 4976648 | tf_op jit(solution)/shard_map/ppermute | solution.py:520
  655.5 34.2 %collective-permute-start.94 = (bf16[72,5760]{1,0:T(8,128)(2,1)}, bf16[72,5760]{1,0:T(8,128)(2,1)}, u32[]{:S(2)}, u32[]{:S(2)}) collective-permute-start(bf16[72,5760]{1,0:T(8,128)(2,1)} %slice_bitcast_fusion.1), channel_id=1, source_target_pairs={{0,4},{4,0},{8,12},{12,8},{1,5},{5,1},{9,13},{13,9},{2,6},{6,2},{1... | collective-permute-start | bytes 2488328 | tf_op jit(solution)/shard_map/ppermute | solution.py:520
  (200 other events, 2211.3 us)

commit v6 on v5

--- a/solution.py
+++ b/solution.py
@@ -1038,6 +1038,8 @@
     ada_at = (3 * D + FF + D) // blocks
     grad_b_flat = jnp.concatenate([bias_own[:ada_at], grad_bada, bias_own[ada_at:]])
     grads_down.add(grad_mod_part)
+    grads_first.add()
+    grad_wada = after(grad_wada, grads_first.token)
     images_all = slots * blocks
     tokens_img = local_tok * lax.axis_size("blk")
     rate_w = LR_COEF / math.sqrt(images_all * tokens_img)

time: 746 us -> 744 us (level)
  transfers between devices with their start and end apart: 97 -> 97, of which waited for: 33 -> 32; matrix products, arithmetic and copies ran while one was open for 35% -> 35% of each run, Pallas kernels for 20% -> 20%
where the time goes in v6:
time: 744 us; the launch traced here: 734 us
  waiting for transfers between devices  162 us (22%)
  Pallas kernels  156 us (21%)
  starting transfers between devices  123 us (17%)
  matrix products  118 us (16%)
  other arithmetic  93.7 us (13%)
  local copies, waits for them, and re-layouts  78.2 us (11%)
    pallas_call x7, Pallas kernels, half_grads(): pl.pallas_call(kernel, grid_spec=pltpu.PrefetchScalarGridSpec(num_scalar_...  62.4 us
    dot_general x8, matrix products, matmul_t(): jnp.einsum('...j,ij->...i', left_arr, right_arr, preferred_element_type=j...  57.8 us
    dot_general x8, matrix products, matmul(): jnp.einsum('...i,ij->...j', left_arr, right_arr, preferred_element_type=j...  57.2 us
    ppermute x20, waiting for transfers between devices, send(): self.came = lax.ppermute(self.give, axes, route)  55.2 us
    pallas_call x7, Pallas kernels, update_rows(): pl.pallas_call(kernel, in_specs=[pl.BlockSpec(memory_space=pl.ANY)] * num...  32.2 us
    ppermute x5, waiting for transfers between devices, first_stage(): others[k] = lax.ppermute(held[k], 'inner', Z_PAIR)  28.7 us
    ppermute x5, waiting for transfers between devices, third_stage(): came = after(lax.ppermute(twos[k], EVERY, NEAR_FIRST), *late)  27.1 us
    ppermute x5, waiting for transfers between devices, gather_groups(): far_four = lax.ppermute(fours[k], EVERY, NEAR_SECOND)  26.7 us
  transfers between devices with their start and end apart: 97, of which 32 were waited for; matrix products, arithmetic and copies ran while one was open for 35% of the time, Pallas kernels for 20%

profile of v6, /device:TPU:0, one launch (start us, length us, event | category | flops | bytes accessed | tf_op | source)
XLA Modules:
  0.0 734.0 jit_solution(4647452952929437452)
XLA Ops:
  78.9 9.4 %collective-permute-done.18 = bf16[72,3200]{1,0:T(8,128)(2,1)S(1)} collective-permute-done((bf16[72,3200]{1,0:T(8,128)(2,1)S(1)}, bf16[72,3200]{1,0:T(8,128)(2,1)S(1)}, u32[]{:S(2)}, u32[]{:S(2)}) %collective-permute-start.18) | collective-permute-done | bytes 460832 | tf_op jit(solution)/shard_map/ppermute | solution.py:372
  88.5 10.8 %collective-permute-done.16.refs_1_ = bf16[4,72,3456]{2,1,0:T(8,128)(2,1)S(1)} collective-permute-done((bf16[4,72,3456]{2,1,0:T(8,128)(2,1)S(1)}, bf16[4,72,3456]{2,1,0:T(8,128)(2,1)S(1)}, u32[]{:S(2)}, u32[]{:S(2)}) %collective-permute-start.16) | collective-permute-done | bytes 1990688 | tf_op jit(solution)/shard_map/ppermute | solution.py:389
  127.2 14.2 %collective-permute-done.24 = bf16[72,4608]{1,0:T(8,128)(2,1)S(1)} collective-permute-done((bf16[72,4608]{1,0:T(8,128)(2,1)S(1)}, bf16[72,4608]{1,0:T(8,128)(2,1)S(1)}, u32[]{:S(2)}, u32[]{:S(2)}) %collective-permute-start.24) | collective-permute-done | bytes 663584 | tf_op jit(solution)/shard_map/ppermute | solution.py:372
  170.6 14.9 %attention.1 = bf16[4,128,1152]{2,1,0:T(8,128)(2,1)} custom-call(bf16[4,128,1152]{2,1,0:T(8,128)(2,1)S(1)} %slice.378.q_ref, bf16[4,128,2304]{2,1,0:T(8,128)(2,1)S(1)} %slice.379.near_ref, bf16[4,128,2304]{2,1,0:T(8,128)(2,1)S(1)} %copy-done.7), custom_call_target="tpu_custom_call" | custom-call | bytes 46200000 | tf_op jit(solution)/shard_map/attention/pallas_call | solution.py:664
  232.9 8.6 %collective-permute-start.37 = (bf16[128,2816]{1,0:T(8,128)(2,1)S(1)}, bf16[128,2816]{1,0:T(8,128)(2,1)S(1)}, u32[]{:S(2)}, u32[]{:S(2)}) collective-permute-start(bf16[128,2816]{1,0:T(8,128)(2,1)S(1)} %broadcast_select_fusion.2), channel_id=1, source_target_pairs={{0,4},{4,0},{8,12},{12,8},{1,5},{5,1},{9,13},{13,9},{2,6},{6,2},{1... | collective-permute-start | bytes 2162696 | tf_op jit(solution)/shard_map/ppermute | solution.py:372
  246.5 14.0 %fusion.5 = (f32[4,128,4608]{2,1,0:T(8,128)}, bf16[4,128,4608]{2,1,0:T(8,128)(2,1)}) fusion(f32[4608]{0:T(1024)S(1)} %copy-done.94, bf16[4,128,1152]{2,1,0:T(8,128)(2,1)S(1)} %add_convert_fusion.11, bf16[1152,4608,1]{1,0,2:T(8,128)(2,1)S(1)} %bitcast.261), kind=kOutput, calls=%fused_computation.10 | convolution fusion | flops 5483003904 | bytes 25970688 | tf_op jit(solution)/shard_map/...i,ij->...j/dot_general | solution.py:634
  270.0 17.7 %collective-permute-done.40 = bf16[2,128,2816]{2,1,0:T(8,128)(2,1)S(1)} collective-permute-done((bf16[2,128,2816]{2,1,0:T(8,128)(2,1)S(1)}, bf16[2,128,2816]{2,1,0:T(8,128)(2,1)S(1)}, u32[]{:S(2)}, u32[]{:S(2)}) %collective-permute-start.40) | collective-permute-done | bytes 1441824 | tf_op jit(solution)/shard_map/ppermute | solution.py:378
  299.1 11.3 %add_convert_fusion.10 = (bf16[4,128,1152]{2,1,0:T(8,128)(2,1)}, f32[4,128,1152]{2,1,0:T(8,128)}) fusion(f32[4,128,1152]{2,1,0:T(8,128)S(1)} %copy-done.26, f32[4,1152]{1,0:T(4,128)S(1)} %copy-done.99, f32[1152]{0:T(1024)S(1)} %copy-done.106, bf16[4,128,4608]{2,1,0:T(8,128)(2,1)} %get-tuple-element.143, bf16[4608,1152,1]{1,0,2:T(8,128)(2,1)S(1)} %bitcast.265), kind=kOutput, calls=%fused_computation.74 | convolution fusion | flops 5438177280 | bytes 21256704 | tf_op jit(solution)/shard_map/...i,ij->...j/dot_general | solution.py:634
  317.0 7.3 collective-permute-done.41.refs_1_
  329.9 8.5 %place_blocks.9 = (bf16[16,128,2048]{2,1,0:T(8,128)(2,1)}, bf16[16,128,768]{2,1,0:T(8,128)(2,1)S(1)}) custom-call(s32[32]{0:T(128)S(1)} %stack.519.table_ref, bf16[4,128,2816]{2,1,0:T(8,128)(2,1)} %pad_maximum_fusion.1.refs_0_, bf16[4,128,2816]{2,1,0:T(8,128)(2,1)} %collective-permute-done.41.refs_1_, bf16[4,128,2816]{2,1,0:T(8,128)(2,1)} %collective-permute-done.42.refs_2_, ...), custom_call_target="tpu_custom_call" | custom-call | bytes 12815827 | tf_op jit(solution)/shard_map/place_blocks/pallas_call | solution.py:167
  338.5 9.8 %multiply_convert_fusion.2 = (bf16[4,128,2048]{2,1,0:T(8,128)(2,1)}, f32[4,128,2048]{2,1,0:T(8,128)S(1)}) fusion(f32[2048]{0:T(1024)S(1)} %copy-done.109, bf16[4,128,2048]{2,1,0:T(8,128)(2,1)S(1)} %copy-done.15, bf16[2048,2048,1]{1,0,2:T(8,128)(2,1)} %bitcast.355), kind=kOutput, calls=%fused_computation.30 | convolution fusion | flops 4301258752 | bytes 16785408 | tf_op jit(solution)/shard_map/...i,ij->...j/dot_general | solution.py:634
  359.4 11.2 %convert_reduce_fusion.3 = (f32[2048]{0:T(1024)}, bf16[4,128,2048]{2,1,0:T(8,128)(2,1)}) fusion(f32[4,128,2048]{2,1,0:T(8,128)S(1)} %copy-done.115, f32[2048]{0:T(1024)S(1)} %copy-done.108, bf16[4,128,2048]{2,1,0:T(8,128)(2,1)S(1)} %get-tuple-element.307, bf16[2048,2048,1]{1,0,2:T(8,128)(2,1)} %bitcast.356), kind=kOutput, calls=%fused_computation.29 | convolution fusion | flops 4308596736 | bytes 16793600 | tf_op jit(solution)/shard_map/...j,ij->...i/dot_general | solution.py:638
  377.4 8.8 %half_grads.7 = (bf16[4,128,2816]{2,1,0:T(8,128)(2,1)}, bf16[4,128,2816]{2,1,0:T(8,128)(2,1)}) custom-call(s32[9]{0:T(128)S(1)} %stack.538.table_ref, bf16[512,2048]{1,0:T(8,128)(2,1)S(1)} %bitcast.278, bf16[512,2048]{1,0:T(8,128)(2,1)S(1)} %copy-done.18, bf16[512,2048]{1,0:T(8,128)(2,1)} %bitcast.333, bf16[512,2048]{1,0:T(8,128)(2,1)} %copy-done.60), custom_call_target="tpu_custom_call" | custom-call | bytes 32045924 | tf_op jit(solution)/shard_map/half_grads/pallas_call | solution.py:314
  404.0 9.1 %convert_reduce_fusion.5 = (f32[1152]{0:T(1024)}, bf16[4,128,1152]{2,1,0:T(8,128)(2,1)}, f32[4,128,1152]{2,1,0:T(8,128)}) fusion(f32[4,1152]{1,0:T(4,128)S(1)} %copy-done.100, bf16[4,128,2048]{2,1,0:T(8,128)(2,1)} %get-tuple-element.159, bf16[1152,2048,1]{1,0,2:T(8,128)(2,1)} %bitcast.279, f32[4]{0:T(128)S(1)} %convert_element_type.327, ...), kind=kOutput, calls=%fused_computation.63 | convolution fusion | flops 2420046848 | bytes 11557392 | tf_op jit(solution)/shard_map/...j,ij->...i/dot_general | solution.py:638
  415.3 11.2 %convert_reduce_fusion = (f32[4608]{0:T(1024)}, bf16[4,128,4608]{2,1,0:T(8,128)(2,1)}) fusion(f32[4,128,4608]{2,1,0:T(8,128)} %get-tuple-element.160, bf16[4,128,1152]{2,1,0:T(8,128)(2,1)} %get-tuple-element.241, bf16[4608,1152,1]{1,0,2:T(8,128)(2,1)S(1)} %bitcast.268), kind=kOutput, calls=%fused_computation.11 | convolution fusion | flops 5445250560 | bytes 25970688 | tf_op jit(solution)/shard_map/...j,ij->...i/dot_general | solution.py:638
  426.5 15.4 %half_grads.10 = (bf16[4,288,1152]{2,1,0:T(8,128)(2,1)}, bf16[4,288,1152]{2,1,0:T(8,128)(2,1)}) custom-call(s32[9]{0:T(128)S(1)} %stack.538.table_ref, bf16[512,4608]{1,0:T(8,128)(2,1)} %bitcast.319, bf16[512,4608]{1,0:T(8,128)(2,1)} %collective-permute-done.50.mate_left, bf16[512,1152]{1,0:T(8,128)(2,1)} %bitcast.96.own_right, ...), custom_call_target="tpu_custom_call" | custom-call | bytes 37928436 | tf_op jit(solution)/shard_map/half_grads/pallas_call | solution.py:314
  449.6 9.6 %multiply_reduce_fusion.3 = (f32[4,128]{1,0:T(4,128)S(1)}, f32[4,128,1152]{2,1,0:T(8,128)}) fusion(f32[4,128,1152]{2,1,0:T(8,128)} %copy-done.25, f32[4,1152]{1,0:T(4,128)S(1)} %copy-done.68, f32[4,128]{1,0:T(4,128)S(1)} %broadcast_multiply_fusion, bf16[4,128,4608]{2,1,0:T(8,128)(2,1)} %get-tuple-element.164, bf16[1152,4608,1]{1,0,2:T(8,128)(2,1)S(1)} %bitcast.264), kind=kOutput, calls=%fused_computation.72 | convolution fusion | flops 5438176768 | bytes 20076544 | tf_op jit(solution)/shard_map/...j,ij->...i/dot_general | solution.py:638
  473.1 10.8 %collective-permute-done.57 = bf16[2,128,2816]{2,1,0:T(8,128)(2,1)} collective-permute-done((bf16[2,128,2816]{2,1,0:T(8,128)(2,1)}, bf16[2,128,2816]{2,1,0:T(8,128)(2,1)}, u32[]{:S(2)}, u32[]{:S(2)}) %collective-permute-start.57) | collective-permute-done | bytes 1441824 | tf_op jit(solution)/shard_map/ppermute | solution.py:520
  489.9 10.8 %half_grads.11 = (bf16[4,72,5760]{2,1,0:T(8,128)(2,1)S(1)}, bf16[4,72,5760]{2,1,0:T(8,128)(2,1)}) custom-call(s32[9]{0:T(128)S(1)} %stack.538.table_ref, bf16[512,1152]{1,0:T(8,128)(2,1)S(1)} %bitcast.272, bf16[512,1152]{1,0:T(8,128)(2,1)S(1)} %collective-permute-done.55.mate_left, bf16[512,4608]{1,0:T(8,128)(2,1)} %bitcast.321, ...), custom_call_target="tpu_custom_call" | custom-call | bytes 37928436 | tf_op jit(solution)/shard_map/half_grads/pallas_call | solution.py:314
  513.3 20.9 %attention_grads.1 = (bf16[4,128,1152]{2,1,0:T(8,128)(2,1)S(1)}, f32[4,128,2304]{2,1,0:T(8,128)S(1)}, bf16[4,128,2304]{2,1,0:T(8,128)(2,1)S(1)}) custom-call(bf16[4,128,1152]{2,1,0:T(8,128)(2,1)S(1)} %copy-done.3, bf16[4,128,2304]{2,1,0:T(8,128)(2,1)S(1)} %slice.379.near_ref, bf16[4,128,2304]{2,1,0:T(8,128)(2,1)S(1)} %copy-done.8, ...), custom_call_target="tpu_custom_call" | custom-call | bytes 69300000 | tf_op jit(solution)/shard_map/attention_grads/pallas_call | solution.py:705
  567.0 8.9 %half_grads.13 = (bf16[4,72,3456]{2,1,0:T(8,128)(2,1)S(1)}, bf16[4,72,3456]{2,1,0:T(8,128)(2,1)}) custom-call(s32[9]{0:T(128)S(1)} %stack.538.table_ref, bf16[512,1152]{1,0:T(8,128)(2,1)S(1)} %bitcast.274, bf16[512,1152]{1,0:T(8,128)(2,1)S(1)} %collective-permute-done.66.mate_left, bf16[512,3456]{1,0:T(8,128)(2,1)} %bitcast.109.own_right, ...), custom_call_target="tpu_custom_call" | custom-call | bytes 30921328 | tf_op jit(solution)/shard_map/half_grads/pallas_call | solution.py:314
  581.3 9.5 %fusion.22 = (f32[4,128]{1,0:T(4,128)S(1)}, f32[4,128,1152]{2,1,0:T(8,128)S(1)}) fusion(bf16[4,128,1152]{2,1,0:T(8,128)(2,1)S(1)} %copy-done.29, f32[4,1152]{1,0:T(4,128)S(1)} %copy-done.70, f32[4,128]{1,0:T(4,128)S(1)} %copy-done.86, bf16[4,128,3456]{2,1,0:T(8,128)(2,1)} %pad_maximum_fusion, bf16[1152,3456,1]{1,0,2:T(8,128)(2,1)} %bitcast.270), kind=kOutput, calls=%fused_computation.62 | convolution fusion | flops 4079812096 | bytes 15063040 | tf_op jit(solution)/shard_map/...j,ij->...i/dot_general | solution.py:638
  606.0 15.5 %collective-permute-done.72 = bf16[4,72,3456]{2,1,0:T(8,128)(2,1)} collective-permute-done((bf16[4,72,3456]{2,1,0:T(8,128)(2,1)S(1)}, bf16[4,72,3456]{2,1,0:T(8,128)(2,1)}, u32[]{:S(2)}, u32[]{:S(2)}) %collective-permute-start.72) | collective-permute-done | bytes 1990688 | tf_op jit(solution)/shard_map/ppermute | solution.py:520
  688.8 21.9 %collective-permute-done.88 = bf16[72,3456]{1,0:T(8,128)(2,1)S(1)} collective-permute-done((bf16[72,3456]{1,0:T(8,128)(2,1)S(1)}, bf16[72,3456]{1,0:T(8,128)(2,1)S(1)}, u32[]{:S(2)}, u32[]{:S(2)}) %collective-permute-start.88) | collective-permute-done | bytes 497696 | tf_op jit(solution)/shard_map/ppermute | solution.py:520
  (652 shorter events, 440.8 us)
Async XLA Ops:
  78.9 35.4 %collective-permute-start.19 = (bf16[4,72,3456]{2,1,0:T(8,128)(2,1)S(1)}, bf16[4,72,3456]{2,1,0:T(8,128)(2,1)S(1)}, u32[]{:S(2)}, u32[]{:S(2)}) collective-permute-start(bf16[4,72,3456]{2,1,0:T(8,128)(2,1)S(1)} %pad_maximum_fusion.4.refs_0_), channel_id=1, source_target_pairs={{0,16},{16,0},{1,17},{17,1},{2,18},{18,2},{3,19},{19,3},{4,20},{20... | collective-permute-start | bytes 5971976 | tf_op jit(solution)/shard_map/ppermute | solution.py:390
  151.9 34.7 %collective-permute-start.27 = (bf16[4,72,3200]{2,1,0:T(8,128)(2,1)}, bf16[4,72,3200]{2,1,0:T(8,128)(2,1)}, u32[]{:S(2)}, u32[]{:S(2)}) collective-permute-start(bf16[4,72,3200]{2,1,0:T(8,128)(2,1)} %collective-permute-done.22.refs_1_), channel_id=1, source_target_pairs={{0,16},{16,0},{1,17},{17,1},{2,18},{18,2},{3,19},{19,3},{4,20},{20... | collective-permute-start | bytes 5529608 | tf_op jit(solution)/shard_map/ppermute | solution.py:397
  151.9 34.7 %collective-permute-start.26 = (bf16[4,72,3200]{2,1,0:T(8,128)(2,1)}, bf16[4,72,3200]{2,1,0:T(8,128)(2,1)}, u32[]{:S(2)}, u32[]{:S(2)}) collective-permute-start(bf16[4,72,3200]{2,1,0:T(8,128)(2,1)} %pad_maximum_fusion.5.refs_0_), channel_id=1, source_target_pairs={{0,16},{16,0},{1,17},{17,1},{2,18},{18,2},{3,19},{19,3},{4,20},{20... | collective-permute-start | bytes 5529608 | tf_op jit(solution)/shard_map/ppermute | solution.py:390
  166.4 38.1 %collective-permute-start.29 = (bf16[4,72,4608]{2,1,0:T(8,128)(2,1)}, bf16[4,72,4608]{2,1,0:T(8,128)(2,1)}, u32[]{:S(2)}, u32[]{:S(2)}) collective-permute-start(bf16[4,72,4608]{2,1,0:T(8,128)(2,1)} %pad_maximum_fusion.2.refs_0_), channel_id=1, source_target_pairs={{0,2},{16,17},{1,3},{17,16},{2,0},{18,19},{3,1},{19,18},{4,6},{20,... | collective-permute-start | bytes 7962632 | tf_op jit(solution)/shard_map/ppermute | solution.py:389
  204.5 37.0 %collective-permute-start.33 = (bf16[4,72,4608]{2,1,0:T(8,128)(2,1)}, bf16[4,72,4608]{2,1,0:T(8,128)(2,1)}, u32[]{:S(2)}, u32[]{:S(2)}) collective-permute-start(bf16[4,72,4608]{2,1,0:T(8,128)(2,1)} %collective-permute-done.29.refs_1_), channel_id=1, source_target_pairs={{0,16},{16,0},{1,17},{17,1},{2,18},{18,2},{3,19},{19,3},{4,20},{20... | collective-permute-start | bytes 7962632 | tf_op jit(solution)/shard_map/ppermute | solution.py:397
  204.7 36.8 %collective-permute-start.32 = (bf16[4,72,4608]{2,1,0:T(8,128)(2,1)}, bf16[4,72,4608]{2,1,0:T(8,128)(2,1)}, u32[]{:S(2)}, u32[]{:S(2)}) collective-permute-start(bf16[4,72,4608]{2,1,0:T(8,128)(2,1)} %pad_maximum_fusion.2.refs_0_), channel_id=1, source_target_pairs={{0,16},{16,0},{1,17},{17,1},{2,18},{18,2},{3,19},{19,3},{4,20},{20... | collective-permute-start | bytes 7962632 | tf_op jit(solution)/shard_map/ppermute | solution.py:390
  230.3 32.3 %collective-permute-start.35 = (bf16[4,288,1152]{2,1,0:T(8,128)(2,1)}, bf16[4,288,1152]{2,1,0:T(8,128)(2,1)}, u32[]{:S(2)}, u32[]{:S(2)}) collective-permute-start(bf16[4,288,1152]{2,1,0:T(8,128)(2,1)} %pad_maximum_fusion.3.refs_0_), channel_id=1, source_target_pairs={{0,2},{16,17},{1,3},{17,16},{2,0},{18,19},{3,1},{19,18},{4,6},{20,... | collective-permute-start | bytes 7962632 | tf_op jit(solution)/shard_map/ppermute | solution.py:389
  289.5 34.8 %collective-permute-start.41 = (bf16[4,128,2816]{2,1,0:T(8,128)(2,1)}, bf16[4,128,2816]{2,1,0:T(8,128)(2,1)}, u32[]{:S(2)}, u32[]{:S(2)}) collective-permute-start(bf16[4,128,2816]{2,1,0:T(8,128)(2,1)} %pad_maximum_fusion.1.refs_0_), channel_id=1, source_target_pairs={{0,2},{16,17},{1,3},{17,16},{2,0},{18,19},{3,1},{19,18},{4,6},{20,... | collective-permute-start | bytes 8650760 | tf_op jit(solution)/shard_map/ppermute | solution.py:389
  293.7 34.7 %collective-permute-start.42 = (bf16[4,128,2816]{2,1,0:T(8,128)(2,1)}, bf16[4,128,2816]{2,1,0:T(8,128)(2,1)}, u32[]{:S(2)}, u32[]{:S(2)}) collective-permute-start(bf16[4,128,2816]{2,1,0:T(8,128)(2,1)} %pad_maximum_fusion.1.refs_0_), channel_id=1, source_target_pairs={{0,16},{16,0},{1,17},{17,1},{2,18},{18,2},{3,19},{19,3},{4,20},{20... | collective-permute-start | bytes 8650760 | tf_op jit(solution)/shard_map/ppermute | solution.py:390
  327.9 98.7 %collective-permute-start.50 = (bf16[512,4608]{1,0:T(8,128)(2,1)}, bf16[512,4608]{1,0:T(8,128)(2,1)}, u32[]{:S(2)}, u32[]{:S(2)}) collective-permute-start(bf16[512,4608]{1,0:T(8,128)(2,1)} %bitcast.318), channel_id=1, source_target_pairs={{0,16},{16,0},{1,17},{17,1},{2,18},{18,2},{3,19},{19,3},{4,20},{20... | collective-permute-start | bytes 14155784 | tf_op jit(solution)/shard_map/ppermute | solution.py:410
  328.4 42.6 %collective-permute-start.48 = (bf16[512,2048]{1,0:T(8,128)(2,1)}, bf16[512,2048]{1,0:T(8,128)(2,1)S(1)}, u32[]{:S(2)}, u32[]{:S(2)}) collective-permute-start(bf16[512,2048]{1,0:T(8,128)(2,1)} %bitcast.277), channel_id=1, source_target_pairs={{0,16},{16,0},{1,17},{17,1},{2,18},{18,2},{3,19},{19,3},{4,20},{20... | collective-permute-start | bytes 6291464 | tf_op jit(solution)/shard_map/ppermute | solution.py:410
  348.3 37.9 %collective-permute-start.46 = (bf16[512,2048]{1,0:T(8,128)(2,1)}, bf16[512,2048]{1,0:T(8,128)(2,1)}, u32[]{:S(2)}, u32[]{:S(2)}) collective-permute-start(bf16[512,2048]{1,0:T(8,128)(2,1)} %bitcast.90.own_left), channel_id=1, source_target_pairs={{0,16},{16,0},{1,17},{17,1},{2,18},{18,2},{3,19},{19,3},{4,20},{20... | collective-permute-start | bytes 6291464 | tf_op jit(solution)/shard_map/ppermute | solution.py:410
  392.9 49.9 %collective-permute-start.52 = (bf16[4,128,2816]{2,1,0:T(8,128)(2,1)}, bf16[4,128,2816]{2,1,0:T(8,128)(2,1)}, u32[]{:S(2)}, u32[]{:S(2)}) collective-permute-start(bf16[4,128,2816]{2,1,0:T(8,128)(2,1)} %get-tuple-element.155), channel_id=1, source_target_pairs={{0,2},{16,17},{1,3},{17,16},{2,0},{18,19},{3,1},{19,18},{4,6},{20,... | collective-permute-start | bytes 8650760 | tf_op jit(solution)/shard_map/ppermute | solution.py:520
  394.3 108.0 %collective-permute-start.53 = (bf16[512,1152]{1,0:T(8,128)(2,1)}, bf16[512,1152]{1,0:T(8,128)(2,1)}, u32[]{:S(2)}, u32[]{:S(2)}) collective-permute-start(bf16[512,1152]{1,0:T(8,128)(2,1)} %bitcast.99.own_left), channel_id=1, source_target_pairs={{0,16},{16,0},{1,17},{17,1},{2,18},{18,2},{3,19},{19,3},{4,20},{20... | collective-permute-start | bytes 3538952 | tf_op jit(solution)/shard_map/ppermute | solution.py:410
  403.1 67.2 %collective-permute-start.58 = (bf16[4,72,2048]{2,1,0:T(8,128)(2,1)}, bf16[4,72,2048]{2,1,0:T(8,128)(2,1)}, u32[]{:S(2)}, u32[]{:S(2)}) collective-permute-start(bf16[4,72,2048]{2,1,0:T(8,128)(2,1)} %copy-done.24), channel_id=1, source_target_pairs={{0,2},{16,17},{1,3},{17,16},{2,0},{18,19},{3,1},{19,18},{4,6},{20,... | collective-permute-start | bytes 3538952 | tf_op jit(solution)/shard_map/ppermute | solution.py:520
  426.5 59.2 %collective-permute-start.56 = (bf16[512,4608]{1,0:T(8,128)(2,1)}, bf16[512,4608]{1,0:T(8,128)(2,1)}, u32[]{:S(2)}, u32[]{:S(2)}) collective-permute-start(bf16[512,4608]{1,0:T(8,128)(2,1)} %bitcast.320), channel_id=1, source_target_pairs={{0,16},{16,0},{1,17},{17,1},{2,18},{18,2},{3,19},{19,3},{4,20},{20... | collective-permute-start | bytes 14155784 | tf_op jit(solution)/shard_map/ppermute | solution.py:410
  441.9 65.7 %collective-permute-start.59 = (bf16[4,288,1152]{2,1,0:T(8,128)(2,1)}, bf16[4,288,1152]{2,1,0:T(8,128)(2,1)}, u32[]{:S(2)}, u32[]{:S(2)}) collective-permute-start(bf16[4,288,1152]{2,1,0:T(8,128)(2,1)} %get-tuple-element.161), channel_id=1, source_target_pairs={{0,2},{16,17},{1,3},{17,16},{2,0},{18,19},{3,1},{19,18},{4,6},{20,... | collective-permute-start | bytes 7962632 | tf_op jit(solution)/shard_map/ppermute | solution.py:520
  449.1 34.8 %collective-permute-start.57 = (bf16[2,128,2816]{2,1,0:T(8,128)(2,1)}, bf16[2,128,2816]{2,1,0:T(8,128)(2,1)}, u32[]{:S(2)}, u32[]{:S(2)}) collective-permute-start(bf16[2,128,2816]{2,1,0:T(8,128)(2,1)} %slice.393), channel_id=1, source_target_pairs={{0,1},{16,18},{1,0},{17,19},{2,3},{18,16},{3,2},{19,17},{4,5},{20,... | collective-permute-start | bytes 4325384 | tf_op jit(solution)/shard_map/ppermute | solution.py:520
  507.7 32.3 %collective-permute-start.64 = (bf16[72,2048]{1,0:T(8,128)(2,1)S(1)}, bf16[72,2048]{1,0:T(8,128)(2,1)S(1)}, u32[]{:S(2)}, u32[]{:S(2)}) collective-permute-start(bf16[72,2048]{1,0:T(8,128)(2,1)S(1)} %slice_bitcast_fusion.9), channel_id=1, source_target_pairs={{0,4},{4,0},{8,12},{12,8},{1,5},{5,1},{9,13},{13,9},{2,6},{6,2},{1... | collective-permute-start | bytes 884744 | tf_op jit(solution)/shard_map/ppermute | solution.py:520
  508.0 32.9 %collective-permute-start.65 = (bf16[128,2816]{1,0:T(8,128)(2,1)S(1)}, bf16[128,2816]{1,0:T(8,128)(2,1)S(1)}, u32[]{:S(2)}, u32[]{:S(2)}) collective-permute-start(bf16[128,2816]{1,0:T(8,128)(2,1)S(1)} %fusion.30), channel_id=1, source_target_pairs={{8,0},{20,28},{9,1},{21,29},{10,2},{22,30},{11,3},{23,31},{12,4},{... | collective-permute-start | bytes 2162696 | tf_op jit(solution)/shard_map/ppermute | solution.py:520
  552.3 43.3 %collective-permute-start.71 = (bf16[4,72,5760]{2,1,0:T(8,128)(2,1)}, bf16[4,72,5760]{2,1,0:T(8,128)(2,1)}, u32[]{:S(2)}, u32[]{:S(2)}) collective-permute-start(bf16[4,72,5760]{2,1,0:T(8,128)(2,1)} %get-tuple-element.172), channel_id=1, source_target_pairs={{0,2},{16,17},{1,3},{17,16},{2,0},{18,19},{3,1},{19,18},{4,6},{20,... | collective-permute-start | bytes 9953288 | tf_op jit(solution)/shard_map/ppermute | solution.py:520
  575.9 45.7 %collective-permute-start.72 = (bf16[4,72,3456]{2,1,0:T(8,128)(2,1)S(1)}, bf16[4,72,3456]{2,1,0:T(8,128)(2,1)}, u32[]{:S(2)}, u32[]{:S(2)}) collective-permute-start(bf16[4,72,3456]{2,1,0:T(8,128)(2,1)S(1)} %get-tuple-element.185), channel_id=1, source_target_pairs={{0,2},{16,17},{1,3},{17,16},{2,0},{18,19},{3,1},{19,18},{4,6},{20,... | collective-permute-start | bytes 5971976 | tf_op jit(solution)/shard_map/ppermute | solution.py:520
  601.5 50.5 %collective-permute-start.80 = (bf16[2,72,5760]{2,1,0:T(8,128)(2,1)}, bf16[2,72,5760]{2,1,0:T(8,128)(2,1)}, u32[]{:S(2)}, u32[]{:S(2)}) collective-permute-start(bf16[2,72,5760]{2,1,0:T(8,128)(2,1)} %slice.407), channel_id=1, source_target_pairs={{0,1},{16,18},{1,0},{17,19},{2,3},{18,16},{3,2},{19,17},{4,5},{20,... | collective-permute-start | bytes 4976648 | tf_op jit(solution)/shard_map/ppermute | solution.py:520
  687.5 32.1 %collective-permute-start.91 = (bf16[72,5760]{1,0:T(8,128)(2,1)S(1)}, bf16[72,5760]{1,0:T(8,128)(2,1)S(1)}, u32[]{:S(2)}, u32[]{:S(2)}) collective-permute-start(bf16[72,5760]{1,0:T(8,128)(2,1)S(1)} %fusion.23), channel_id=1, source_target_pairs={{8,0},{20,28},{9,1},{21,29},{10,2},{22,30},{11,3},{23,31},{12,4},{... | collective-permute-start | bytes 2488328 | tf_op jit(solution)/shard_map/ppermute | solution.py:520
  (200 other events, 2267.7 us)
